TPU v7x, 32 devices: a whole 2x2x4 slice. The times are simulated.
32 devices in a mesh: dp: 16 (over z, y, x), mp: 2 (over core).
Axes of the slice: x: 2, y: 2, z: 4, core: 2. Of those that a mesh axis runs over, the one named last changes fastest.
Arguments:
- image_codes: int32 [2, 16, 128], P(None, 'dp'), may hold values from 0 to 8191
- masked: int32 [2, 16, 128], P(None, 'dp'), may hold values from 0 to 1
- null_caption: int32 [2, 16], P(None, 'dp'), may hold values 0 or 1
- captions: bfloat16 [2, 16, 32, 4096], P(None, 'dp'), may hold values from -6 to 6
- step_count: int32 [1], replicated, may hold values from 2 to 20
- code_table: float32 [8192, 2048], P(('mp', 'dp')), may hold values from -0.625 to 0.625
- table_first: float32 [8192, 2048], P(('mp', 'dp')), may hold values from -1.66893e-06 to 1.66893e-06
- table_second: float32 [8192, 2048], P(('mp', 'dp')), may hold values from 5.402178e-16 to 8.643485e-15
- vectors: float32 [137, 2048], replicated, may hold values from -1 to 2
- vectors_first: float32 [137, 2048], replicated, may hold values from -6.67572e-06 to 6.67572e-06
- vectors_second: float32 [137, 2048], replicated, may hold values from 8.643485e-15 to 1.3829576e-13
- projections: float32 [4, 2048, 2048], P(None, 'dp', 'mp'), may hold values from -0.125 to 0.125
- projections_first: float32 [4, 2048, 2048], P(None, 'dp', 'mp'), may hold values from -1.66893e-06 to 1.66893e-06
- projections_second: float32 [4, 2048, 2048], P(None, 'dp', 'mp'), may hold values from 5.402178e-16 to 8.643485e-15
- text_maps: float32 [2, 4096, 2048], P(None, 'dp', 'mp'), may hold values from -0.09375 to 0.09375
- text_maps_first: float32 [2, 4096, 2048], P(None, 'dp', 'mp'), may hold values from -1.66893e-06 to 1.66893e-06
- text_maps_second: float32 [2, 4096, 2048], P(None, 'dp', 'mp'), may hold values from 5.402178e-16 to 8.643485e-15
- out_maps: float32 [2, 2048, 2048], P(None, ('mp', 'dp')), may hold values from -0.375 to 0.375
- out_maps_first: float32 [2, 2048, 2048], P(None, ('mp', 'dp')), may hold values from -1.66893e-06 to 1.66893e-06
- out_maps_second: float32 [2, 2048, 2048], P(None, ('mp', 'dp')), may hold values from 5.402178e-16 to 8.643485e-15
- expand: float32 [2048, 8192], P('dp', 'mp'), may hold values from -0.125 to 0.125
- expand_first: float32 [2048, 8192], P('dp', 'mp'), may hold values from -1.66893e-06 to 1.66893e-06
- expand_second: float32 [2048, 8192], P('dp', 'mp'), may hold values from 5.402178e-16 to 8.643485e-15
- contract: float32 [8192, 2048], P(('mp', 'dp')), may hold values from -0.0625 to 0.0625
- contract_first: float32 [8192, 2048], P(('mp', 'dp')), may hold values from -1.66893e-06 to 1.66893e-06
- contract_second: float32 [8192, 2048], P(('mp', 'dp')), may hold values from 5.402178e-16 to 8.643485e-15
Outputs:
- loss_value: float32 [], replicated
- grad_norm: float32 [], replicated
- new_code_table: float32 [8192, 2048], P(('mp', 'dp'))
- new_table_first: float32 [8192, 2048], P(('mp', 'dp'))
- new_table_second: float32 [8192, 2048], P(('mp', 'dp'))
- new_vectors: float32 [137, 2048], replicated
- new_vectors_first: float32 [137, 2048], replicated
- new_vectors_second: float32 [137, 2048], replicated
- new_projections: float32 [4, 2048, 2048], P(None, 'dp', 'mp')
- new_projections_first: float32 [4, 2048, 2048], P(None, 'dp', 'mp')
- new_projections_second: float32 [4, 2048, 2048], P(None, 'dp', 'mp')
- new_text_maps: float32 [2, 4096, 2048], P(None, 'dp', 'mp')
- new_text_maps_first: float32 [2, 4096, 2048], P(None, 'dp', 'mp')
- new_text_maps_second: float32 [2, 4096, 2048], P(None, 'dp', 'mp')
- new_out_maps: float32 [2, 2048, 2048], P(None, ('mp', 'dp'))
- new_out_maps_first: float32 [2, 2048, 2048], P(None, ('mp', 'dp'))
- new_out_maps_second: float32 [2, 2048, 2048], P(None, ('mp', 'dp'))
- new_expand: float32 [2048, 8192], P('dp', 'mp')
- new_expand_first: float32 [2048, 8192], P('dp', 'mp')
- new_expand_second: float32 [2048, 8192], P('dp', 'mp')
- new_contract: float32 [8192, 2048], P(('mp', 'dp'))
- new_contract_first: float32 [8192, 2048], P(('mp', 'dp'))
- new_contract_second: float32 [8192, 2048], P(('mp', 'dp'))
All inputs are finite; a program needn't handle non-finite values. No bound on the sum of `null_caption` on one device may be relied on, other than what follows from the above.
Results may differ from a plain program's by a relative error of at most 0.0055.
The roundings to bfloat16 on the way count: a program that leaves them out, or rounds other values in their place, can miss the bound.
Values may be sent and summed in bfloat16 or wider, within the bound.
A program may use at most 576 MiB of HBM per device.

v0:
```python
from functools import partial

import jax
import jax.numpy as jnp
from jax import lax
from jax.experimental import pallas as pl
from jax.experimental.pallas import tpu as pltpu
from jax.sharding import Mesh, PartitionSpec as P

HD = 128
EPS_NORM = 1e-05
CLIP = 0.01
BETA_ONE = 0.9
BETA_TWO = 0.999
ADAM_EPS = 1e-08
DECAY = 0.01
RATE_MATRIX = 0.02
RATE_VECTOR = 0.2
SCALE = HD ** (-0.5)
F32 = jnp.float32
BF16 = jnp.bfloat16
WIRE = jnp.bfloat16

AX, BX, EX, DX, CX = "a", "b", "e", "d", "c"
DP = (AX, BX, EX, DX)
QX = (BX, EX)
MX = (AX, DX)
SWAP = [(0, 1), (1, 0)]
MESH = pl.DeviceIdType.MESH


def dot(x, y, dims):
    return lax.dot_general(x, y, (dims, ((), ())), preferred_element_type=F32)


def nn(x, y):
    return dot(x, y, ((1,), (0,)))


def nt(x, y):
    return dot(x, y, ((1,), (1,)))


def tn(x, y):
    return dot(x, y, ((0,), (0,)))


def place(b, e, c):
    return (b * 2 + e) * 2 + c


def greet(peers):
    barrier = pltpu.get_barrier_semaphore()
    for peer in peers:
        pl.semaphore_signal(barrier, inc=1, device_id=peer, device_id_type=MESH)
    pl.semaphore_wait(barrier, len(peers))


def gather_kernel(x_ref, o_ref, local, send, recv):
    b, e, c = lax.axis_index(BX), lax.axis_index(EX), lax.axis_index(CX)
    to_b, to_e, to_c = {BX: 1 - b}, {EX: 1 - e}, {CX: 1 - c}
    greet((to_b, to_e, to_c))
    me, beside, across, far = (
        place(b, e, c),
        place(b, 1 - e, c),
        place(1 - b, e, c),
        place(1 - b, 1 - e, c),
    )

    def copy(number, source, target, peer):
        made = pltpu.make_async_remote_copy(
            src_ref=source,
            dst_ref=target,
            send_sem=send.at[number],
            recv_sem=recv.at[number],
            device_id=peer,
            device_id_type=MESH,
        )
        made.start()
        return made

    own = pltpu.make_async_copy(x_ref, o_ref.at[me], local)
    e_first = copy(0, x_ref.at[0], o_ref.at[me, 0], to_e)
    b_first = copy(1, x_ref.at[1], o_ref.at[me, 1], to_b)
    e_second = copy(2, x_ref.at[1], o_ref.at[me, 1], to_e)
    b_second = copy(3, x_ref.at[0], o_ref.at[me, 0], to_b)
    started = [copy(4, x_ref, o_ref.at[me], to_c)]
    own.start()
    e_first.wait_recv()
    block = o_ref.at[beside, 0]
    b_third = copy(5, block, block, to_b)
    started.append(copy(6, block, block, to_c))
    b_first.wait_recv()
    block = o_ref.at[across, 1]
    e_third = copy(7, block, block, to_e)
    started.append(copy(8, block, block, to_c))
    e_second.wait_recv()
    block = o_ref.at[beside, 1]
    started.append(copy(9, block, block, to_c))
    b_second.wait_recv()
    block = o_ref.at[across, 0]
    started.append(copy(10, block, block, to_c))
    b_third.wait_recv()
    block = o_ref.at[far, 0]
    started.append(copy(11, block, block, to_c))
    e_third.wait_recv()
    block = o_ref.at[far, 1]
    started.append(copy(12, block, block, to_c))
    own.wait()
    for made in (e_first, b_first, e_second, b_second, b_third, e_third):
        made.wait_send()
    for made in started:
        made.wait()


def gather_eight(x, number, cost):
    return pl.pallas_call(
        gather_kernel,
        out_shape=jax.ShapeDtypeStruct((8,) + x.shape, x.dtype),
        in_specs=[pl.BlockSpec(memory_space=pl.ANY)],
        out_specs=pl.BlockSpec(memory_space=pl.ANY),
        scratch_shapes=[
            pltpu.SemaphoreType.DMA,
            pltpu.SemaphoreType.DMA((13,)),
            pltpu.SemaphoreType.DMA((13,)),
        ],
        compiler_params=pltpu.CompilerParams(collective_id=number, has_side_effects=True),
        cost_estimate=pl.CostEstimate(flops=0, bytes_accessed=cost, transcendentals=0),
    )(x)


def scatter_kernel(p_ref, o_ref, paired, held, from_b, from_e, last, send, recv):
    b, e, c = lax.axis_index(BX), lax.axis_index(EX), lax.axis_index(CX)
    to_b, to_e, to_c = {BX: 1 - b}, {EX: 1 - e}, {CX: 1 - c}
    greet((to_b, to_e, to_c))
    order = ((1 - b, 1 - e), (1 - b, e), (b, 1 - e), (b, e))

    def copy(number, source, target, peer):
        made = pltpu.make_async_remote_copy(
            src_ref=source,
            dst_ref=target,
            send_sem=send.at[number],
            recv_sem=recv.at[number],
            device_id=peer,
            device_id_type=MESH,
        )
        made.start()
        return made

    pairs = [
        copy(k, p_ref.at[place(bb, ee, 1 - c)], paired.at[k], to_c)
        for k, (bb, ee) in enumerate(order)
    ]
    pairs[0].wait_recv()
    held[0] = p_ref[place(1 - b, 1 - e, c)] + paired[0]
    b_first = copy(4, held.at[0, 0], from_b.at[0], to_b)
    e_first = copy(5, held.at[0, 1], from_e.at[0], to_e)
    pairs[1].wait_recv()
    held[1] = p_ref[place(1 - b, e, c)] + paired[1]
    b_second = copy(6, held.at[1, 0], from_b.at[1], to_b)
    pairs[2].wait_recv()
    held[2] = p_ref[place(b, 1 - e, c)] + paired[2]
    e_second = copy(7, held.at[2, 1], from_e.at[1], to_e)
    pairs[3].wait_recv()
    o_ref[...] = p_ref[place(b, e, c)] + paired[3]
    b_first.wait_recv()
    held[2, 0] = held[2, 0] + from_b[0]
    e_third = copy(8, held.at[2, 0], last.at[0], to_e)
    e_first.wait_recv()
    held[1, 1] = held[1, 1] + from_e[0]
    b_third = copy(9, held.at[1, 1], last.at[1], to_b)
    b_second.wait_recv()
    o_ref[0] = o_ref[0] + from_b[1]
    e_second.wait_recv()
    o_ref[1] = o_ref[1] + from_e[1]
    e_third.wait_recv()
    o_ref[0] = o_ref[0] + last[0]
    b_third.wait_recv()
    o_ref[1] = o_ref[1] + last[1]
    for made in pairs + [b_first, e_first, b_second, e_second, b_third, e_third]:
        made.wait_send()


def scatter_eight(parts, number, cost):
    shape = parts.shape[1:]
    half = shape[1:]
    kind = parts.dtype
    return pl.pallas_call(
        scatter_kernel,
        out_shape=jax.ShapeDtypeStruct(shape, kind),
        in_specs=[pl.BlockSpec(memory_space=pltpu.VMEM)],
        out_specs=pl.BlockSpec(memory_space=pltpu.VMEM),
        scratch_shapes=[
            pltpu.VMEM((4,) + shape, kind),
            pltpu.VMEM((3,) + shape, kind),
            pltpu.VMEM((2,) + half, kind),
            pltpu.VMEM((2,) + half, kind),
            pltpu.VMEM((2,) + half, kind),
            pltpu.SemaphoreType.DMA((10,)),
            pltpu.SemaphoreType.DMA((10,)),
        ],
        compiler_params=pltpu.CompilerParams(
            collective_id=number, has_side_effects=True, vmem_limit_bytes=40 << 20
        ),
        cost_estimate=pl.CostEstimate(flops=0, bytes_accessed=cost, transcendentals=0),
    )(parts)


def spread(rows, number):
    count, width = rows.shape
    full = gather_eight(rows.reshape(2, count // 2, width), number, 80_000_000)
    return full.reshape(8 * count, width)


def collect(parts, number):
    count, width = parts.shape
    part = scatter_eight(parts.reshape(8, 2, count // 16, width), number, 150_000_000)
    return part.reshape(count // 8, width)


def share_gather(block):
    a, d, extent = lax.axis_index(AX), lax.axis_index(DX), lax.axis_size(DX)
    other = lax.ppermute(block, AX, SWAP)
    full = jnp.zeros((2, extent) + block.shape, block.dtype)
    zeros = (0,) * block.ndim

    def put(full, piece, row, column):
        return lax.dynamic_update_slice(full, piece[None, None], (row, column) + zeros)

    full = put(full, block, a, d)
    full = put(full, other, 1 - a, d)
    for step in range(1, extent):
        ring = [(k, (k + step) % extent) for k in range(extent)]
        column = lax.rem(d + extent - step, extent)
        full = put(full, lax.ppermute(block, DX, ring), a, column)
        full = put(full, lax.ppermute(other, DX, ring), 1 - a, column)
    return full


def share_scatter(grad):
    a, d, extent = lax.axis_index(AX), lax.axis_index(DX), lax.axis_size(DX)

    def column(k):
        return lax.dynamic_index_in_dim(grad, k, 1, False)

    total = column(d)
    for step in range(1, extent):
        ring = [(k, (k + step) % extent) for k in range(extent)]
        piece = column(lax.rem(d + step, extent)).astype(WIRE)
        total = total + lax.ppermute(piece, DX, ring).astype(F32)
    piece = lax.dynamic_index_in_dim(total, 1 - a, 0, False).astype(WIRE)
    return lax.dynamic_index_in_dim(total, a, 0, False) + lax.ppermute(piece, AX, SWAP).astype(F32)


def exchange(pieces):
    q = lax.axis_index(QX)
    zeros = (0,) * (pieces.ndim - 1)
    full = jnp.zeros_like(pieces)

    def take(k):
        return lax.dynamic_index_in_dim(pieces, k, 0, False)

    full = lax.dynamic_update_slice(full, take(q)[None], (q,) + zeros)
    for step in (1, 2, 3):
        there = jnp.bitwise_xor(q, step)
        moved = lax.ppermute(take(there), QX, [(k, k ^ step) for k in range(4)])
        full = lax.dynamic_update_slice(full, moved[None], (there,) + zeros)
    return full


def layer_norm(inputs, gain, bias):
    average = jnp.mean(inputs, -1, keepdims=True)
    centred = inputs - average
    factor = lax.rsqrt(jnp.mean(centred * centred, -1, keepdims=True) + EPS_NORM)
    normed = centred * factor
    return (normed * gain + bias).astype(BF16), (normed, factor)


def norm_back(upstream, saved, gain):
    normed, factor = saved
    inner = upstream * gain
    back = factor * (
        inner
        - jnp.mean(inner, -1, keepdims=True)
        - normed * jnp.mean(inner * normed, -1, keepdims=True)
    )
    return back, jnp.sum(upstream * normed, 0), jnp.sum(upstream, 0)


def heads(x, images):
    return x.reshape(images, -1, x.shape[-1] // HD, HD)


def flat(x):
    return x.reshape(x.shape[0] * x.shape[1], -1).astype(BF16)


def ein(text, x, y):
    return jnp.einsum(text, x, y, preferred_element_type=F32)


SCORE = "bqhe,bkhe->bhqk"
MIX = "bhqk,bkhe->bqhe"
TURN = "bhqk,bqhe->bkhe"


def attend(queries, keys, values):
    scores = ein(SCORE, queries, keys) * SCALE
    top = jnp.max(scores, -1, keepdims=True)
    logsum = top + jnp.log(jnp.sum(jnp.exp(scores - top), -1, keepdims=True))
    probs = jnp.exp(scores - logsum)
    return flat(ein(MIX, probs.astype(BF16), values)), probs


def attend_back(upstream, queries, keys, values, probs, images):
    grad_out = heads(upstream, images)
    grad_probs = ein(SCORE, grad_out, values)
    inner = jnp.sum(probs * grad_probs, -1, keepdims=True)
    grad_scores = (probs * (grad_probs - inner)).astype(BF16)
    return (
        flat(ein(MIX, grad_scores, keys) * SCALE),
        flat(ein(TURN, grad_scores, queries) * SCALE),
        flat(ein(TURN, probs.astype(BF16), grad_out)),
    )


def adamw(state, grad, rate, decay, fix_one, fix_two):
    master, first, second = state
    first_new = BETA_ONE * first + (1.0 - BETA_ONE) * grad
    second_new = BETA_TWO * second + (1.0 - BETA_TWO) * grad * grad
    update = first_new / fix_one / (jnp.sqrt(second_new / fix_two) + ADAM_EPS)
    return master - rate * (update + decay * master), first_new, second_new


def body(image_codes, masked, null_caption, captions, step_count, *states):
    table_state, vector_state, proj_state, text_state, out_state, expand_state, contract_state = (
        states[k : k + 3] for k in range(0, 21, 3)
    )
    a, b, e, c = (lax.axis_index(k) for k in (AX, BX, EX, CX))
    extent = lax.axis_size(DX)
    vectors = vector_state[0]
    length = vectors.shape[0] - 9
    norm_rows = vectors[length + 1 :]
    width = vectors.shape[1]

    block = table_state[0].shape[0]
    table = share_gather(table_state[0].astype(BF16)).reshape(-1, width)
    codes_here = table.shape[0]

    kinds, in_rows, half = proj_state[0].shape
    deep = kinds
    pieces = proj_state[0].astype(BF16).reshape(kinds, in_rows, 2, 4, HD)
    pieces = exchange(pieces.transpose(3, 0, 1, 2, 4).reshape(4, kinds, in_rows, 2 * HD))
    proj = share_gather(pieces).transpose(3, 0, 2, 1, 4, 5).reshape(kinds, width, 2 * HD)
    w_qkv = proj[:3].transpose(1, 0, 2).reshape(width, 6 * HD)
    w_cross = proj[3]

    out_maps = share_gather(out_state[0].astype(BF16))
    out_maps = out_maps.transpose(2, 0, 1, 3, 4).reshape(2, 2 * HD, width)

    text_rows = text_state[0].shape[1]
    pieces = text_state[0].astype(BF16).reshape(2, text_rows, 2, 4, HD)
    pieces = exchange(pieces.transpose(3, 1, 0, 2, 4).reshape(4, text_rows, 4 * HD))
    w_text = share_gather(pieces).transpose(0, 2, 1, 3, 4).reshape(-1, 4 * HD)

    hidden_width = extent * block
    pieces = expand_state[0].astype(BF16).reshape(in_rows, 2, 4, hidden_width)
    pieces = exchange(pieces.transpose(2, 0, 1, 3).reshape(4, in_rows, 2 * hidden_width))
    expand = share_gather(pieces).transpose(0, 2, 1, 3, 4).reshape(width, 2 * hidden_width)

    contract = share_gather(contract_state[0].astype(BF16)).reshape(-1, width)

    mask_total = lax.psum(jnp.sum(masked).astype(F32), DP)
    group_codes = lax.all_gather(image_codes, QX).reshape(-1)
    group_mask = lax.all_gather(masked, QX).reshape(-1)
    group_captions = lax.all_gather(captions, QX).reshape(-1, captions.shape[-1])
    images = group_codes.shape[0] // length
    chosen = lax.dynamic_index_in_dim(masked, c, 0, False).reshape(-1)[:, None] == 1
    keep = 1.0 - lax.dynamic_index_in_dim(null_caption, c, 0, False).astype(F32)
    keep_rows = jnp.repeat(keep, length)[:, None]
    own_images = keep.shape[0]

    in_half = lax.rem(group_codes, 2 * 4 * hidden_width)
    outer = in_half // block
    inside = (
        (group_codes // (2 * 4 * hidden_width) == c)
        & (lax.rem(outer // extent, 2) == e)
        & (lax.rem(outer // (2 * extent), 2) == b)
    )
    outer = (outer // (4 * extent)) * extent + lax.rem(outer, extent)
    local_code = jnp.where(inside, outer * block + lax.rem(in_half, block), -1)
    at_code = jnp.arange(codes_here)[None, :] == local_code[:, None]

    looked = collect(nn(at_code.astype(BF16), table).astype(BF16), 1).astype(F32)
    x_zero = jnp.where(chosen, vectors[length], looked)
    x_zero = x_zero + jnp.tile(vectors[:length], (own_images, 1))
    a_one, norm_one = layer_norm(x_zero, norm_rows[0], norm_rows[1])
    a_one = spread(a_one, 2)
    triple = nn(a_one, w_qkv).astype(BF16)
    queries, keys, values = (
        heads(triple[:, k : k + 2 * HD], images) for k in (0, 2 * HD, 4 * HD)
    )
    attn_one, probs_one = attend(queries, keys, values)
    x_one = x_zero + collect(nn(attn_one, out_maps[0]), 3)

    pair = nn(group_captions, w_text).astype(BF16)
    text_keys, text_values = heads(pair[:, : 2 * HD], images), heads(pair[:, 2 * HD :], images)
    a_two, norm_two = layer_norm(x_one, norm_rows[2], norm_rows[3])
    a_two = spread(a_two, 2)
    cross = heads(nn(a_two, w_cross).astype(BF16), images)
    attn_two, probs_two = attend(cross, text_keys, text_values)
    x_two = x_one + keep_rows * collect(nn(attn_two, out_maps[1]), 3)

    a_three, norm_three = layer_norm(x_two, norm_rows[4], norm_rows[5])
    a_three = spread(a_three, 2)
    preact = nn(a_three, expand)
    hidden = jax.nn.gelu(preact, approximate=True).astype(BF16)
    x_three = x_two + collect(nn(hidden, contract), 3)

    a_four, norm_four = layer_norm(x_three, norm_rows[6], norm_rows[7])
    a_four = spread(a_four, 2)
    logits = nt(a_four, table)
    target = jnp.sum(jnp.where(at_code, logits, 0.0), 1)
    top = jnp.max(logits, 1)
    total = jnp.sum(jnp.exp(logits - top[:, None]), 1)
    count = target.shape[0]
    stats = jnp.stack([top, total, target, target])
    stats = gather_eight(stats.reshape(2, 8, count // 4), 4, 20_000_000).reshape(8, 4, count)
    peak = jnp.max(stats[:, 0], 0)
    total = jnp.sum(stats[:, 1] * jnp.exp(stats[:, 0] - peak), 0)
    head_logsum = peak + jnp.log(total)
    weight = group_mask.astype(F32)
    loss_sum = jnp.sum(weight * (head_logsum - jnp.sum(stats[:, 2], 0)))

    head_probs = jnp.exp(logits - head_logsum[:, None])
    logit_grad = (head_probs - at_code.astype(F32)) * (weight / mask_total)[:, None]
    logit_grad = logit_grad.astype(BF16)
    upstream = collect(nn(logit_grad, table), 3)
    table_grad = tn(logit_grad, a_four)
    grad_three, gain_six, gain_seven = norm_back(upstream, norm_four, norm_rows[6])
    branch_three = spread(grad_three.astype(BF16), 2)
    hidden_grad = nt(branch_three, contract)
    gelu_pull = jax.vjp(partial(jax.nn.gelu, approximate=True), preact)[1]
    preact_grad = gelu_pull(hidden_grad)[0].astype(BF16)
    back = collect(nt(preact_grad, expand), 3)
    contract_grad = tn(hidden, branch_three)
    contract_shard = share_scatter(contract_grad.reshape(2, extent, block, width))
    expand_grad = tn(a_three, preact_grad).reshape(2, 4, extent, in_rows, 2 * hidden_width)
    expand_shard = exchange(share_scatter(expand_grad.transpose(0, 2, 1, 3, 4)))
    expand_shard = expand_shard.reshape(4, in_rows, 2, hidden_width).transpose(1, 2, 0, 3)
    expand_shard = expand_shard.reshape(expand_state[0].shape)

    back, gain_four, gain_five = norm_back(back, norm_three, norm_rows[4])
    grad_two = grad_three + back
    branch_two = spread(grad_two.astype(BF16) * keep_rows.astype(BF16), 2)
    attn_grad = nt(branch_two, out_maps[1]).astype(BF16)
    cross_grad, key_grad, value_grad = attend_back(
        attn_grad, cross, text_keys, text_values, probs_two, images
    )
    back = collect(nt(cross_grad, w_cross), 3)
    text_grad = tn(group_captions, jnp.concatenate([key_grad, value_grad], 1))
    text_grad = text_grad.reshape(2, 4, extent, text_rows, 4 * HD).transpose(0, 2, 1, 3, 4)
    text_shard = exchange(share_scatter(text_grad)).reshape(4, text_rows, 2, 2, HD)
    text_shard = text_shard.transpose(2, 1, 3, 0, 4).reshape(text_state[0].shape)

    back, gain_two, gain_three = norm_back(back, norm_two, norm_rows[2])
    grad_one = grad_two + back
    branch_one = spread(grad_one.astype(BF16), 2)
    attn_grad = nt(branch_one, out_maps[0]).astype(BF16)
    triple_grad = jnp.concatenate(
        attend_back(attn_grad, queries, keys, values, probs_one, images), 1
    )
    back = collect(nt(triple_grad, w_qkv), 3)
    out_grad = jnp.stack([tn(attn_one, branch_one), tn(attn_two, branch_two)])
    out_grad = out_grad.reshape(2, 2, extent, HD // extent, width).transpose(1, 2, 0, 3, 4)
    out_shard = share_scatter(out_grad)
    proj_grad = jnp.concatenate([tn(a_one, triple_grad), tn(a_two, cross_grad)], 1)
    proj_grad = proj_grad.reshape(2, 4, extent, in_rows, kinds, 2 * HD)
    proj_shard = exchange(share_scatter(proj_grad.transpose(0, 2, 1, 3, 4, 5)))
    proj_shard = proj_shard.reshape(4, in_rows, kinds, 2, HD).transpose(2, 1, 3, 0, 4)
    proj_shard = proj_shard.reshape(proj_state[0].shape)

    back, gain_zero, gain_one = norm_back(back, norm_one, norm_rows[0])
    grad_zero = grad_one + back
    unmasked = jnp.where(chosen, 0.0, grad_zero)
    high = unmasked.astype(BF16)
    low = (unmasked - high.astype(F32)).astype(BF16)
    looked_grad = spread(jnp.concatenate([high, low], 1), 5)
    looked_grad = tn(at_code.astype(BF16), looked_grad)
    table_grad = table_grad + looked_grad[:, :width] + looked_grad[:, width:]
    table_shard = share_scatter(table_grad.reshape(2, extent, block, width))

    position_grad = jnp.sum(grad_zero.reshape(own_images, length, -1), 0)
    mask_grad = jnp.sum(jnp.where(chosen, grad_zero, 0.0), 0)
    vector_grad = jnp.concatenate(
        [
            position_grad,
            jnp.stack(
                [
                    mask_grad,
                    gain_zero,
                    gain_one,
                    gain_two,
                    gain_three,
                    gain_four,
                    gain_five,
                    gain_six,
                    gain_seven,
                ]
            ),
        ],
        0,
    )
    vector_grad = lax.psum(vector_grad, DP + (CX,))
    loss_value = lax.psum(loss_sum, MX) / mask_total

    shards = (table_shard, proj_shard, text_shard, out_shard, expand_shard, contract_shard)
    squares = sum((jnp.sum(piece * piece) for piece in shards))
    grad_norm = jnp.sqrt(lax.psum(squares, DP + (CX,)) + jnp.sum(vector_grad * vector_grad))
    clip_scale = CLIP / jnp.maximum(grad_norm, CLIP)
    count_step = step_count[0].astype(F32)
    fix_one = 1.0 - BETA_ONE**count_step
    fix_two = 1.0 - BETA_TWO**count_step
    results = [loss_value, grad_norm]
    matrices = (table_state, proj_state, text_state, out_state, expand_state, contract_state)
    updated = [
        adamw(state, grad * clip_scale, RATE_MATRIX, DECAY, fix_one, fix_two)
        for state, grad in zip(matrices, shards)
    ]
    vector_new = adamw(
        vector_state, vector_grad * clip_scale, RATE_VECTOR, 0.0, fix_one, fix_two
    )
    updated.insert(1, vector_new)
    for entry in updated:
        results.extend(entry)
    return tuple(results)


def solution(mesh):
    grid = mesh.devices
    extent = grid.shape[0] // 8
    fine = Mesh(grid.reshape(2, 2, 2, extent, grid.shape[1]), (AX, BX, EX, DX, CX))
    rows = P((CX,) + DP, None)
    both = P(None, DP, CX)
    kinds = (rows, P(), both, both, P(None, (CX,) + DP, None), P(DP, CX), rows)
    states = tuple(kind for kind in kinds for _ in range(3))
    batch = P(None, DP, None)
    return jax.shard_map(
        body,
        mesh=fine,
        in_specs=(batch, batch, P(None, DP), P(None, DP, None, None), P()) + states,
        out_specs=(P(), P()) + states,
        check_vma=False,
    )
```

profile of v0, /device:TPU:0, one launch (start us, length us, event | category | flops | bytes accessed | tf_op | source)
XLA Modules:
  0.0 1780.6 jit_solution(6046392072325640372)
XLA Ops:
  24.8 42.0 %all-gather.1 = s32[8,1,128]{2,1,0:T(1,128)} all-gather(s32[2,1,128]{2,1,0:T(1,128)S(1)} %copy-done.163), channel_id=3, replica_groups=mesh['a'=2,'b'=2,'e'=2,'d'=2,'c'=2] {'b','e'}, dimensions={0}, use_global_device_ids=true | all-gather | bytes 5120 | tf_op jit(solution)/shard_map/all_gather | solution.py:374
  94.4 38.5 %psum.29 = f32[]{:T(128)} all-reduce(f32[]{:T(128)S(6)} %convert_element_type.368), channel_id=1, replica_groups=mesh['a'=2,'b'=2,'e'=2,'d'=2,'c'=2] {'a','b','e','d'}, use_global_device_ids=true, to_apply=%region_21.22 | all-reduce | flops 1 | bytes 8 | tf_op jit(solution)/shard_map/psum | solution.py:373
  215.9 9.2 collective-permute-done.11
  236.2 66.1 %collective-permute-done.24 = bf16[256,2048]{1,0:T(8,128)(2,1)} collective-permute-done((bf16[256,2048]{1,0:T(8,128)(2,1)S(1)}, bf16[256,2048]{1,0:T(8,128)(2,1)}, u32[]{:S(2)}, u32[]{:S(2)}) %collective-permute-start.24) | collective-permute-done | bytes 1048608 | tf_op jit(solution)/shard_map/ppermute | solution.py:223
  306.7 29.3 %collective-permute-done.6 = bf16[4,4,128,256]{3,2,0,1:T(8,128)(2,1)} collective-permute-done((bf16[4,4,128,256]{3,2,0,1:T(8,128)(2,1)S(1)}, bf16[4,4,128,256]{3,2,0,1:T(8,128)(2,1)}, u32[]{:S(2)}, u32[]{:S(2)}) %collective-permute-start.6) | collective-permute-done | bytes 1048608 | tf_op jit(solution)/shard_map/ppermute | solution.py:223
  339.5 18.9 %collective-permute-done.15 = bf16[4,256,512]{2,1,0:T(8,128)(2,1)} collective-permute-done((bf16[4,256,512]{2,1,0:T(8,128)(2,1)}, bf16[4,256,512]{2,1,0:T(8,128)(2,1)}, u32[]{:S(2)}, u32[]{:S(2)}) %collective-permute-start.15) | collective-permute-done | bytes 1048608 | tf_op jit(solution)/shard_map/ppermute | solution.py:223
  362.0 15.3 collective-permute-done.21
  389.8 21.7 %shard_map.425 = bf16[2,64,2048]{2,1,0:T(8,128)(2,1)S(1)} custom-call(bf16[8,2,64,2048]{3,2,1,0:T(8,128)(2,1)S(1)} %bitcast.588), custom_call_target="tpu_custom_call" | custom-call | bytes 150000000 | tf_op jit(solution)/shard_map/pallas_call | solution.py:188
  413.3 22.2 %shard_map.426 = bf16[8,2,64,2048]{3,2,1,0:T(8,128)(2,1)} custom-call(bf16[2,64,2048]{2,1,0:T(8,128)(2,1)} %bitcast.653), custom_call_target="tpu_custom_call" | custom-call | bytes 80000000 | tf_op jit(solution)/shard_map/pallas_call | solution.py:117
  466.2 39.7 %shard_map.427 = f32[2,64,2048]{2,1,0:T(8,128)S(1)} custom-call(f32[8,2,64,2048]{3,2,1,0:T(8,128)S(1)} %fusion.156.p_ref), custom_call_target="tpu_custom_call" | custom-call | bytes 150000000 | tf_op jit(solution)/shard_map/pallas_call | solution.py:188
  507.6 21.7 %shard_map.428 = bf16[8,2,64,2048]{3,2,1,0:T(8,128)(2,1)} custom-call(bf16[2,64,2048]{2,1,0:T(8,128)(2,1)} %bitcast.654), custom_call_target="tpu_custom_call" | custom-call | bytes 80000000 | tf_op jit(solution)/shard_map/pallas_call | solution.py:117
  557.2 39.7 %shard_map.429 = f32[2,64,2048]{2,1,0:T(8,128)S(1)} custom-call(f32[8,2,64,2048]{3,2,1,0:T(8,128)S(1)} %fusion.157.p_ref), custom_call_target="tpu_custom_call" | custom-call | bytes 150000000 | tf_op jit(solution)/shard_map/pallas_call | solution.py:188
  599.3 21.7 %shard_map.430 = bf16[8,2,64,2048]{3,2,1,0:T(8,128)(2,1)} custom-call(bf16[2,64,2048]{2,1,0:T(8,128)(2,1)} %bitcast.655), custom_call_target="tpu_custom_call" | custom-call | bytes 80000000 | tf_op jit(solution)/shard_map/pallas_call | solution.py:117
  621.1 11.2 fusion.14
  653.3 39.7 %shard_map.431 = f32[2,64,2048]{2,1,0:T(8,128)S(1)} custom-call(f32[8,2,64,2048]{3,2,1,0:T(8,128)S(1)} %fusion.158.p_ref), custom_call_target="tpu_custom_call" | custom-call | bytes 150000000 | tf_op jit(solution)/shard_map/pallas_call | solution.py:188
  695.3 21.7 %shard_map.432 = bf16[8,2,64,2048]{3,2,1,0:T(8,128)(2,1)} custom-call(bf16[2,64,2048]{2,1,0:T(8,128)(2,1)} %bitcast.656), custom_call_target="tpu_custom_call" | custom-call | bytes 80000000 | tf_op jit(solution)/shard_map/pallas_call | solution.py:117
  727.4 8.3 shard_map.433
  746.3 39.7 %shard_map.434 = f32[2,64,2048]{2,1,0:T(8,128)S(1)} custom-call(f32[8,2,64,2048]{3,2,1,0:T(8,128)S(1)} %fusion.159.p_ref), custom_call_target="tpu_custom_call" | custom-call | bytes 150000000 | tf_op jit(solution)/shard_map/pallas_call | solution.py:188
  792.9 21.8 %shard_map.435 = bf16[8,2,64,2048]{3,2,1,0:T(8,128)(2,1)} custom-call(bf16[2,64,2048]{2,1,0:T(8,128)(2,1)} %bitcast.643), custom_call_target="tpu_custom_call" | custom-call | bytes 80000000 | tf_op jit(solution)/shard_map/pallas_call | solution.py:117
  814.7 12.6 fusion.6
  838.4 39.7 %shard_map.436 = f32[2,64,2048]{2,1,0:T(8,128)S(1)} custom-call(f32[8,2,64,2048]{3,2,1,0:T(8,128)S(1)} %fusion.160.p_ref), custom_call_target="tpu_custom_call" | custom-call | bytes 150000000 | tf_op jit(solution)/shard_map/pallas_call | solution.py:188
  885.5 21.7 %shard_map.437 = bf16[8,2,64,2048]{3,2,1,0:T(8,128)(2,1)} custom-call(bf16[2,64,2048]{2,1,0:T(8,128)(2,1)} %bitcast.641), custom_call_target="tpu_custom_call" | custom-call | bytes 80000000 | tf_op jit(solution)/shard_map/pallas_call | solution.py:117
  920.8 39.7 %shard_map.438 = f32[2,64,2048]{2,1,0:T(8,128)S(1)} custom-call(f32[8,2,64,2048]{3,2,1,0:T(8,128)S(1)} %fusion.161.p_ref), custom_call_target="tpu_custom_call" | custom-call | bytes 150000000 | tf_op jit(solution)/shard_map/pallas_call | solution.py:188
  967.8 21.7 %shard_map.439 = bf16[8,2,64,2048]{3,2,1,0:T(8,128)(2,1)} custom-call(bf16[2,64,2048]{2,1,0:T(8,128)(2,1)} %bitcast.642), custom_call_target="tpu_custom_call" | custom-call | bytes 80000000 | tf_op jit(solution)/shard_map/pallas_call | solution.py:117
  1010.6 39.7 %shard_map.440 = f32[2,64,2048]{2,1,0:T(8,128)S(1)} custom-call(f32[8,2,64,2048]{3,2,1,0:T(8,128)S(1)} %fusion.38.p_ref), custom_call_target="tpu_custom_call" | custom-call | bytes 150000000 | tf_op jit(solution)/shard_map/pallas_call | solution.py:188
  1113.3 11.9 reshape.689
  1125.2 9.8 constant_dynamic-slice_fusion.2
  1135.0 10.6 copy.581
  1161.3 12.0 reshape.688
  1173.3 9.2 constant_dynamic-slice_fusion.5
  1182.5 10.6 copy.580
  1195.4 39.4 %shard_map.441 = bf16[8,2,64,4096]{3,2,1,0:T(8,128)(2,1)} custom-call(bf16[2,64,4096]{2,1,0:T(8,128)(2,1)} %bitcast.608), custom_call_target="tpu_custom_call" | custom-call | bytes 80000000 | tf_op jit(solution)/shard_map/pallas_call | solution.py:117
  1234.8 14.9 fusion.15
  1249.7 10.6 slice_add_fusion
  1260.3 36.0 %psum.28 = f32[]{:T(128)} all-reduce(f32[]{:T(128)} %get-tuple-element.200), channel_id=1, replica_groups=mesh['a'=2,'b'=2,'e'=2,'d'=2,'c'=2] {'a','d'}, use_global_device_ids=true, to_apply=%region_19.20 | all-reduce | flops 1 | bytes 8 | tf_op jit(solution)/shard_map/psum | solution.py:515
  1296.3 9.7 constant_dynamic-slice_fusion.6
  1310.8 9.7 constant_dynamic-slice_fusion.3
  1320.5 10.9 copy.514
  1331.4 11.1 copy.504
  1369.3 22.8 %collective-permute-done.27 = bf16[2,256,2048]{2,1,0:T(8,128)(2,1)S(1)} collective-permute-done((bf16[2,256,2048]{2,1,0:T(8,128)(2,1)S(1)}, bf16[2,256,2048]{2,1,0:T(8,128)(2,1)S(1)}, u32[]{:S(2)}, u32[]{:S(2)}) %collective-permute-start.27) | collective-permute-done | bytes 2097184 | tf_op jit(solution)/shard_map/ppermute | solution.py:250
  1395.8 116.4 %collective-permute-done.42 = bf16[4,128,1024]{2,1,0:T(8,128)(2,1)S(1)} collective-permute-done((bf16[4,128,1024]{2,1,0:T(8,128)(2,1)S(1)}, bf16[4,128,1024]{2,1,0:T(8,128)(2,1)S(1)}, u32[]{:S(2)}, u32[]{:S(2)}) %collective-permute-start.42) | collective-permute-done | bytes 1048608 | tf_op jit(solution)/shard_map/ppermute | solution.py:252
  1515.9 18.9 %collective-permute-done.35 = bf16[4,256,512]{2,1,0:T(8,128)(2,1)} collective-permute-done((bf16[4,256,512]{2,1,0:T(8,128)(2,1)S(1)}, bf16[4,256,512]{2,1,0:T(8,128)(2,1)}, u32[]{:S(2)}, u32[]{:S(2)}) %collective-permute-start.35) | collective-permute-done | bytes 1048608 | tf_op jit(solution)/shard_map/ppermute | solution.py:252
  1537.2 20.2 %collective-permute-done.30 = bf16[4,128,4,256]{3,1,2,0:T(8,128)(2,1)} collective-permute-done((bf16[4,128,4,256]{3,1,2,0:T(8,128)(2,1)}, bf16[4,128,4,256]{3,1,2,0:T(8,128)(2,1)}, u32[]{:S(2)}, u32[]{:S(2)}) %collective-permute-start.30) | collective-permute-done | bytes 1048608 | tf_op jit(solution)/shard_map/ppermute | solution.py:252
  1568.7 10.4 collective-permute-done.28
  1581.7 8.6 collective-permute-done.44
  1591.5 10.7 collective-permute-done.45
  1664.8 38.0 %psum.30 = f32[]{:T(128)} all-reduce(f32[]{:T(128)S(6)} %add.587), channel_id=1, replica_groups=mesh['a'=2,'b'=2,'e'=2,'d'=2,'c'=2] {'a','b','e','d','c'}, use_global_device_ids=true, to_apply=%region_38.39 | all-reduce | flops 1 | bytes 8 | tf_op jit(solution)/shard_map/psum | solution.py:519
  1763.2 8.1 multiply_subtract_fusion
  (735 shorter events, 588.6 us)
Async XLA Ops:
  7.2 535.2 %all-gather.5.cloned.1.call-start = ((), (), s32[]{:S(2)}) async-start(), calls=%async_computation.1 | async-start | bytes 2621440 | tf_op jit(solution)/shard_map/all_gather | solution.py:376
  12.1 219.0 %collective-permute-start = (bf16[256,2048]{1,0:T(8,128)(2,1)}, bf16[256,2048]{1,0:T(8,128)(2,1)}, u32[]{:S(2)}, u32[]{:S(2)}) collective-permute-start(bf16[256,2048]{1,0:T(8,128)(2,1)} %get-tuple-element.156), channel_id=1, source_target_pairs={{0,16},{16,0},{1,17},{17,1},{2,18},{18,2},{3,19},{19,3},{4,20},{20... | collective-permute-start | bytes 3145736 | tf_op jit(solution)/shard_map/ppermute | solution.py:223
  16.1 217.8 %collective-permute-start.1 = (bf16[256,2048]{1,0:T(8,128)(2,1)}, bf16[256,2048]{1,0:T(8,128)(2,1)}, u32[]{:S(2)}, u32[]{:S(2)}) collective-permute-start(bf16[256,2048]{1,0:T(8,128)(2,1)} %get-tuple-element.156), channel_id=1, source_target_pairs={{0,2},{2,0},{1,3},{3,1},{4,6},{6,4},{5,7},{7,5},{8,10},{10,8},{9,1... | collective-permute-start | bytes 3145736 | tf_op jit(solution)/shard_map/ppermute | solution.py:235
  21.2 147.7 %collective-permute-start.3 = (bf16[4,128,256]{2,1,0:T(8,128)(2,1)}, bf16[4,128,256]{2,1,0:T(8,128)(2,1)}, u32[]{:S(2)}, u32[]{:S(2)}) collective-permute-start(bf16[4,128,256]{2,1,0:T(8,128)(2,1)} %get-tuple-element.193), channel_id=1, source_target_pairs={{0,4},{4,0},{8,12},{12,8},{1,5},{5,1},{9,13},{13,9},{2,6},{6,2},{1... | collective-permute-start | bytes 786440 | tf_op jit(solution)/shard_map/ppermute | solution.py:266
  22.8 147.2 %collective-permute-start.4 = (bf16[4,128,256]{2,1,0:T(8,128)(2,1)}, bf16[4,128,256]{2,1,0:T(8,128)(2,1)}, u32[]{:S(2)}, u32[]{:S(2)}) collective-permute-start(bf16[4,128,256]{2,1,0:T(8,128)(2,1)} %get-tuple-element.192), channel_id=1, source_target_pairs={{0,8},{4,12},{8,0},{12,4},{1,9},{5,13},{9,1},{13,5},{2,10},{6,14},... | collective-permute-start | bytes 786440 | tf_op jit(solution)/shard_map/ppermute | solution.py:266
  24.3 148.6 %collective-permute-start.5 = (bf16[4,128,256]{2,1,0:T(8,128)(2,1)}, bf16[4,128,256]{2,1,0:T(8,128)(2,1)}, u32[]{:S(2)}, u32[]{:S(2)}) collective-permute-start(bf16[4,128,256]{2,1,0:T(8,128)(2,1)} %get-tuple-element.191), channel_id=1, source_target_pairs={{0,12},{4,8},{8,4},{12,0},{1,13},{5,9},{9,5},{13,1},{2,14},{6,10},... | collective-permute-start | bytes 786440 | tf_op jit(solution)/shard_map/ppermute | solution.py:266
  24.8 1637.9 %all-reduce.2.cloned.1.call-start = ((), (), s32[]{:S(2)}) async-start(), calls=%async_computation | async-start | bytes 2359296 | tf_op jit(solution)/shard_map/psum | solution.py:514
  168.9 40.4 %collective-permute-start.9 = (bf16[2,64,2048]{2,1,0:T(8,128)(2,1)}, bf16[2,64,2048]{2,1,0:T(8,128)(2,1)S(1)}, u32[]{:S(2)}, u32[]{:S(2)}) collective-permute-start(bf16[2,64,2048]{2,1,0:T(8,128)(2,1)} %get-tuple-element.152), channel_id=1, source_target_pairs={{0,16},{16,0},{1,17},{17,1},{2,18},{18,2},{3,19},{19,3},{4,20},{20... | collective-permute-start | bytes 1572872 | tf_op jit(solution)/shard_map/ppermute | solution.py:223
  170.0 10.7 collective-permute-start.12
  172.9 13.7 collective-permute-start.13
  180.7 11.3 collective-permute-start.14
  186.6 10.1 collective-permute-start.18
  198.7 15.1 collective-permute-start.10
  206.5 95.7 %collective-permute-start.24 = (bf16[256,2048]{1,0:T(8,128)(2,1)S(1)}, bf16[256,2048]{1,0:T(8,128)(2,1)}, u32[]{:S(2)}, u32[]{:S(2)}) collective-permute-start(bf16[256,2048]{1,0:T(8,128)(2,1)S(1)} %copy-done.107), channel_id=1, source_target_pairs={{0,16},{16,0},{1,17},{17,1},{2,18},{18,2},{3,19},{19,3},{4,20},{20... | collective-permute-start | bytes 3145736 | tf_op jit(solution)/shard_map/ppermute | solution.py:223
  209.4 15.7 collective-permute-start.11
  213.8 91.8 %collective-permute-start.25 = (bf16[256,2048]{1,0:T(8,128)(2,1)S(1)}, bf16[256,2048]{1,0:T(8,128)(2,1)S(1)}, u32[]{:S(2)}, u32[]{:S(2)}) collective-permute-start(bf16[256,2048]{1,0:T(8,128)(2,1)S(1)} %copy-done.107), channel_id=1, source_target_pairs={{0,2},{2,0},{1,3},{3,1},{4,6},{6,4},{5,7},{7,5},{8,10},{10,8},{9,1... | collective-permute-start | bytes 3145736 | tf_op jit(solution)/shard_map/ppermute | solution.py:235
  225.0 111.0 %collective-permute-start.6 = (bf16[4,4,128,256]{3,2,0,1:T(8,128)(2,1)S(1)}, bf16[4,4,128,256]{3,2,0,1:T(8,128)(2,1)}, u32[]{:S(2)}, u32[]{:S(2)}) collective-permute-start(bf16[4,4,128,256]{3,2,0,1:T(8,128)(2,1)S(1)} %bitcast_dynamic-update-slice_fusion.30), channel_id=1, source_target_pairs={{0,16},{16,0},{1,17},{17,1},{2,18},{18,2},{3,19},{19,3},{4,20},{20... | collective-permute-start | bytes 3145736 | tf_op jit(solution)/shard_map/ppermute | solution.py:223
  231.1 107.2 %collective-permute-start.7 = (bf16[4,4,128,256]{3,2,0,1:T(8,128)(2,1)S(1)}, bf16[4,4,128,256]{3,2,0,1:T(8,128)(2,1)S(1)}, u32[]{:S(2)}, u32[]{:S(2)}) collective-permute-start(bf16[4,4,128,256]{3,2,0,1:T(8,128)(2,1)S(1)} %bitcast_dynamic-update-slice_fusion.30), channel_id=1, source_target_pairs={{0,2},{2,0},{1,3},{3,1},{4,6},{6,4},{5,7},{7,5},{8,10},{10,8},{9,1... | collective-permute-start | bytes 3145736 | tf_op jit(solution)/shard_map/ppermute | solution.py:235
  233.9 124.5 %collective-permute-start.15 = (bf16[4,256,512]{2,1,0:T(8,128)(2,1)}, bf16[4,256,512]{2,1,0:T(8,128)(2,1)}, u32[]{:S(2)}, u32[]{:S(2)}) collective-permute-start(bf16[4,256,512]{2,1,0:T(8,128)(2,1)} %bitcast_dynamic-update-slice_fusion.27), channel_id=1, source_target_pairs={{0,16},{16,0},{1,17},{17,1},{2,18},{18,2},{3,19},{19,3},{4,20},{20... | collective-permute-start | bytes 3145736 | tf_op jit(solution)/shard_map/ppermute | solution.py:223
  302.3 58.5 %collective-permute-start.16 = (bf16[4,256,512]{2,1,0:T(8,128)(2,1)}, bf16[4,256,512]{2,1,0:T(8,128)(2,1)S(1)}, u32[]{:S(2)}, u32[]{:S(2)}) collective-permute-start(bf16[4,256,512]{2,1,0:T(8,128)(2,1)} %bitcast_dynamic-update-slice_fusion.27), channel_id=1, source_target_pairs={{0,2},{2,0},{1,3},{3,1},{4,6},{6,4},{5,7},{7,5},{8,10},{10,8},{9,1... | collective-permute-start | bytes 3145736 | tf_op jit(solution)/shard_map/ppermute | solution.py:235
  305.6 71.7 %collective-permute-start.21 = (bf16[4,128,1024]{2,1,0:T(8,128)(2,1)}, bf16[4,128,1024]{2,1,0:T(8,128)(2,1)}, u32[]{:S(2)}, u32[]{:S(2)}) collective-permute-start(bf16[4,128,1024]{2,1,0:T(8,128)(2,1)} %bitcast_dynamic-update-slice_fusion.24), channel_id=1, source_target_pairs={{0,16},{16,0},{1,17},{17,1},{2,18},{18,2},{3,19},{19,3},{4,20},{20... | collective-permute-start | bytes 3145736 | tf_op jit(solution)/shard_map/ppermute | solution.py:223
  336.0 42.7 %collective-permute-start.22 = (bf16[4,128,1024]{2,1,0:T(8,128)(2,1)}, bf16[4,128,1024]{2,1,0:T(8,128)(2,1)S(1)}, u32[]{:S(2)}, u32[]{:S(2)}) collective-permute-start(bf16[4,128,1024]{2,1,0:T(8,128)(2,1)} %bitcast_dynamic-update-slice_fusion.24), channel_id=1, source_target_pairs={{0,2},{2,0},{1,3},{3,1},{4,6},{6,4},{5,7},{7,5},{8,10},{10,8},{9,1... | collective-permute-start | bytes 3145736 | tf_op jit(solution)/shard_map/ppermute | solution.py:235
  338.3 46.5 %collective-permute-start.2 = (bf16[256,2048]{1,0:T(8,128)(2,1)}, bf16[256,2048]{1,0:T(8,128)(2,1)S(1)}, u32[]{:S(2)}, u32[]{:S(2)}) collective-permute-start(bf16[256,2048]{1,0:T(8,128)(2,1)} %collective-permute-done), channel_id=1, source_target_pairs={{0,2},{2,0},{1,3},{3,1},{4,6},{6,4},{5,7},{7,5},{8,10},{10,8},{9,1... | collective-permute-start | bytes 3145736 | tf_op jit(solution)/shard_map/ppermute | solution.py:236
  358.5 77.1 %collective-permute-start.26 = (bf16[256,2048]{1,0:T(8,128)(2,1)}, bf16[256,2048]{1,0:T(8,128)(2,1)S(1)}, u32[]{:S(2)}, u32[]{:S(2)}) collective-permute-start(bf16[256,2048]{1,0:T(8,128)(2,1)} %collective-permute-done.24), channel_id=1, source_target_pairs={{0,2},{2,0},{1,3},{3,1},{4,6},{6,4},{5,7},{7,5},{8,10},{10,8},{9,1... | collective-permute-start | bytes 3145736 | tf_op jit(solution)/shard_map/ppermute | solution.py:236
  360.8 75.8 %collective-permute-start.8 = (bf16[4,4,128,256]{3,2,0,1:T(8,128)(2,1)}, bf16[4,4,128,256]{3,2,0,1:T(8,128)(2,1)}, u32[]{:S(2)}, u32[]{:S(2)}) collective-permute-start(bf16[4,4,128,256]{3,2,0,1:T(8,128)(2,1)} %collective-permute-done.6), channel_id=1, source_target_pairs={{0,2},{2,0},{1,3},{3,1},{4,6},{6,4},{5,7},{7,5},{8,10},{10,8},{9,1... | collective-permute-start | bytes 3145736 | tf_op jit(solution)/shard_map/ppermute | solution.py:236
  377.4 160.4 %collective-permute-start.17 = (bf16[4,256,512]{2,1,0:T(8,128)(2,1)}, bf16[4,256,512]{2,1,0:T(8,128)(2,1)}, u32[]{:S(2)}, u32[]{:S(2)}) collective-permute-start(bf16[4,256,512]{2,1,0:T(8,128)(2,1)} %collective-permute-done.15), channel_id=1, source_target_pairs={{0,2},{2,0},{1,3},{3,1},{4,6},{6,4},{5,7},{7,5},{8,10},{10,8},{9,1... | collective-permute-start | bytes 3145736 | tf_op jit(solution)/shard_map/ppermute | solution.py:236
  378.7 161.4 %collective-permute-start.23 = (bf16[4,128,1024]{2,1,0:T(8,128)(2,1)}, bf16[4,128,1024]{2,1,0:T(8,128)(2,1)}, u32[]{:S(2)}, u32[]{:S(2)}) collective-permute-start(bf16[4,128,1024]{2,1,0:T(8,128)(2,1)} %collective-permute-done.21), channel_id=1, source_target_pairs={{0,2},{2,0},{1,3},{3,1},{4,6},{6,4},{5,7},{7,5},{8,10},{10,8},{9,1... | collective-permute-start | bytes 3145736 | tf_op jit(solution)/shard_map/ppermute | solution.py:236
  1082.8 265.0 %collective-permute-start.46 = (bf16[2,256,2048]{2,1,0:T(8,128)(2,1)}, bf16[2,256,2048]{2,1,0:T(8,128)(2,1)}, u32[]{:S(2)}, u32[]{:S(2)}) collective-permute-start(bf16[2,256,2048]{2,1,0:T(8,128)(2,1)} %fusion.24), channel_id=1, source_target_pairs={{0,2},{2,0},{1,3},{3,1},{4,6},{6,4},{5,7},{7,5},{8,10},{10,8},{9,1... | collective-permute-start | bytes 6291464 | tf_op jit(solution)/shard_map/ppermute | solution.py:250
  1098.3 256.0 %collective-permute-start.41 = (bf16[2,4,128,1024]{3,2,1,0:T(8,128)(2,1)}, bf16[2,4,128,1024]{3,2,1,0:T(8,128)(2,1)}, u32[]{:S(2)}, u32[]{:S(2)}) collective-permute-start(bf16[2,4,128,1024]{3,2,1,0:T(8,128)(2,1)} %fusion.23), channel_id=1, source_target_pairs={{0,2},{2,0},{1,3},{3,1},{4,6},{6,4},{5,7},{7,5},{8,10},{10,8},{9,1... | collective-permute-start | bytes 6291464 | tf_op jit(solution)/shard_map/ppermute | solution.py:250
  1107.2 198.8 %collective-permute-start.39 = (bf16[2,2,64,2048]{3,2,0,1:T(8,128)(2,1)}, bf16[2,2,64,2048]{3,2,0,1:T(8,128)(2,1)}, u32[]{:S(2)}, u32[]{:S(2)}) collective-permute-start(bf16[2,2,64,2048]{3,2,0,1:T(8,128)(2,1)} %fusion.70), channel_id=1, source_target_pairs={{0,2},{2,0},{1,3},{3,1},{4,6},{6,4},{5,7},{7,5},{8,10},{10,8},{9,1... | collective-permute-start | bytes 3145736 | tf_op jit(solution)/shard_map/ppermute | solution.py:250
  1145.6 213.1 %collective-permute-start.34 = (bf16[2,4,256,512]{3,2,1,0:T(8,128)(2,1)}, bf16[2,4,256,512]{3,2,1,0:T(8,128)(2,1)}, u32[]{:S(2)}, u32[]{:S(2)}) collective-permute-start(bf16[2,4,256,512]{3,2,1,0:T(8,128)(2,1)} %bitcast.639), channel_id=1, source_target_pairs={{0,2},{2,0},{1,3},{3,1},{4,6},{6,4},{5,7},{7,5},{8,10},{10,8},{9,1... | collective-permute-start | bytes 6291464 | tf_op jit(solution)/shard_map/ppermute | solution.py:250
  1193.1 170.0 %collective-permute-start.29 = (bf16[2,4,128,4,256]{4,2,3,1,0:T(8,128)(2,1)}, bf16[2,4,128,4,256]{4,2,3,1,0:T(8,128)(2,1)}, u32[]{:S(2)}, u32[]{:S(2)}) collective-permute-start(bf16[2,4,128,4,256]{4,2,3,1,0:T(8,128)(2,1)} %bitcast.640), channel_id=1, source_target_pairs={{0,2},{2,0},{1,3},{3,1},{4,6},{6,4},{5,7},{7,5},{8,10},{10,8},{9,1... | collective-permute-start | bytes 6291464 | tf_op jit(solution)/shard_map/ppermute | solution.py:250
  1309.2 37.3 %collective-permute-start.40 = (bf16[2,64,2048]{2,1,0:T(8,128)(2,1)S(1)}, bf16[2,64,2048]{2,1,0:T(8,128)(2,1)S(1)}, u32[]{:S(2)}, u32[]{:S(2)}) collective-permute-start(bf16[2,64,2048]{2,1,0:T(8,128)(2,1)S(1)} %fusion.77), channel_id=1, source_target_pairs={{0,16},{16,0},{1,17},{17,1},{2,18},{18,2},{3,19},{19,3},{4,20},{20... | collective-permute-start | bytes 1572872 | tf_op jit(solution)/shard_map/ppermute | solution.py:252
  1346.5 45.6 %collective-permute-start.27 = (bf16[2,256,2048]{2,1,0:T(8,128)(2,1)S(1)}, bf16[2,256,2048]{2,1,0:T(8,128)(2,1)S(1)}, u32[]{:S(2)}, u32[]{:S(2)}) collective-permute-start(bf16[2,256,2048]{2,1,0:T(8,128)(2,1)S(1)} %fusion.25), channel_id=1, source_target_pairs={{0,2},{2,0},{1,3},{3,1},{4,6},{6,4},{5,7},{7,5},{8,10},{10,8},{9,1... | collective-permute-start | bytes 6291464 | tf_op jit(solution)/shard_map/ppermute | solution.py:250
  1352.6 214.9 %collective-permute-start.47 = (bf16[256,2048]{1,0:T(8,128)(2,1)}, bf16[256,2048]{1,0:T(8,128)(2,1)S(1)}, u32[]{:S(2)}, u32[]{:S(2)}) collective-permute-start(bf16[256,2048]{1,0:T(8,128)(2,1)} %fusion.69), channel_id=1, source_target_pairs={{0,16},{16,0},{1,17},{17,1},{2,18},{18,2},{3,19},{19,3},{4,20},{20... | collective-permute-start | bytes 3145736 | tf_op jit(solution)/shard_map/ppermute | solution.py:252
  1357.3 154.9 %collective-permute-start.42 = (bf16[4,128,1024]{2,1,0:T(8,128)(2,1)S(1)}, bf16[4,128,1024]{2,1,0:T(8,128)(2,1)S(1)}, u32[]{:S(2)}, u32[]{:S(2)}) collective-permute-start(bf16[4,128,1024]{2,1,0:T(8,128)(2,1)S(1)} %fusion.68), channel_id=1, source_target_pairs={{0,16},{16,0},{1,17},{17,1},{2,18},{18,2},{3,19},{19,3},{4,20},{20... | collective-permute-start | bytes 3145736 | tf_op jit(solution)/shard_map/ppermute | solution.py:252
  1361.4 173.4 %collective-permute-start.35 = (bf16[4,256,512]{2,1,0:T(8,128)(2,1)S(1)}, bf16[4,256,512]{2,1,0:T(8,128)(2,1)}, u32[]{:S(2)}, u32[]{:S(2)}) collective-permute-start(bf16[4,256,512]{2,1,0:T(8,128)(2,1)S(1)} %fusion.67), channel_id=1, source_target_pairs={{0,16},{16,0},{1,17},{17,1},{2,18},{18,2},{3,19},{19,3},{4,20},{20... | collective-permute-start | bytes 3145736 | tf_op jit(solution)/shard_map/ppermute | solution.py:252
  1367.7 189.6 %collective-permute-start.30 = (bf16[4,128,4,256]{3,1,2,0:T(8,128)(2,1)}, bf16[4,128,4,256]{3,1,2,0:T(8,128)(2,1)}, u32[]{:S(2)}, u32[]{:S(2)}) collective-permute-start(bf16[4,128,4,256]{3,1,2,0:T(8,128)(2,1)} %fusion.66), channel_id=1, source_target_pairs={{0,16},{16,0},{1,17},{17,1},{2,18},{18,2},{3,19},{19,3},{4,20},{20... | collective-permute-start | bytes 3145736 | tf_op jit(solution)/shard_map/ppermute | solution.py:252
  1394.3 184.8 %collective-permute-start.28 = (bf16[256,2048]{1,0:T(8,128)(2,1)}, bf16[256,2048]{1,0:T(8,128)(2,1)}, u32[]{:S(2)}, u32[]{:S(2)}) collective-permute-start(bf16[256,2048]{1,0:T(8,128)(2,1)} %fusion.65), channel_id=1, source_target_pairs={{0,16},{16,0},{1,17},{17,1},{2,18},{18,2},{3,19},{19,3},{4,20},{20... | collective-permute-start | bytes 3145736 | tf_op jit(solution)/shard_map/ppermute | solution.py:252
  1514.9 64.2 %collective-permute-start.43 = (f32[128,1024]{1,0:T(8,128)}, f32[128,1024]{1,0:T(8,128)}, u32[]{:S(2)}, u32[]{:S(2)}) collective-permute-start(f32[128,1024]{1,0:T(8,128)} %get-tuple-element.159), channel_id=1, source_target_pairs={{0,4},{4,0},{8,12},{12,8},{1,5},{5,1},{9,13},{13,9},{2,6},{6,2},{1... | collective-permute-start | bytes 1572872 | tf_op jit(solution)/shard_map/ppermute | solution.py:266
  1534.8 55.5 %collective-permute-start.44 = (f32[128,1024]{1,0:T(8,128)}, f32[128,1024]{1,0:T(8,128)}, u32[]{:S(2)}, u32[]{:S(2)}) collective-permute-start(f32[128,1024]{1,0:T(8,128)} %get-tuple-element.158), channel_id=1, source_target_pairs={{0,8},{4,12},{8,0},{12,4},{1,9},{5,13},{9,1},{13,5},{2,10},{6,14},... | collective-permute-start | bytes 1572872 | tf_op jit(solution)/shard_map/ppermute | solution.py:266
  1557.4 44.8 %collective-permute-start.45 = (f32[128,1024]{1,0:T(8,128)}, f32[128,1024]{1,0:T(8,128)}, u32[]{:S(2)}, u32[]{:S(2)}) collective-permute-start(f32[128,1024]{1,0:T(8,128)} %get-tuple-element.157), channel_id=1, source_target_pairs={{0,12},{4,8},{8,4},{12,0},{1,13},{5,9},{9,5},{13,1},{2,14},{6,10},... | collective-permute-start | bytes 1572872 | tf_op jit(solution)/shard_map/ppermute | solution.py:266
  1567.6 43.0 %collective-permute-start.36 = (f32[256,512]{1,0:T(8,128)}, f32[256,512]{1,0:T(8,128)}, u32[]{:S(2)}, u32[]{:S(2)}) collective-permute-start(f32[256,512]{1,0:T(8,128)} %get-tuple-element.163), channel_id=1, source_target_pairs={{0,4},{4,0},{8,12},{12,8},{1,5},{5,1},{9,13},{13,9},{2,6},{6,2},{1... | collective-permute-start | bytes 1572872 | tf_op jit(solution)/shard_map/ppermute | solution.py:266
  1579.1 35.9 %collective-permute-start.37 = (f32[256,512]{1,0:T(8,128)}, f32[256,512]{1,0:T(8,128)}, u32[]{:S(2)}, u32[]{:S(2)}) collective-permute-start(f32[256,512]{1,0:T(8,128)} %get-tuple-element.162), channel_id=1, source_target_pairs={{0,8},{4,12},{8,0},{12,4},{1,9},{5,13},{9,1},{13,5},{2,10},{6,14},... | collective-permute-start | bytes 1572872 | tf_op jit(solution)/shard_map/ppermute | solution.py:266
  1579.1 45.6 %collective-permute-start.38 = (f32[256,512]{1,0:T(8,128)}, f32[256,512]{1,0:T(8,128)}, u32[]{:S(2)}, u32[]{:S(2)}) collective-permute-start(f32[256,512]{1,0:T(8,128)} %get-tuple-element.161), channel_id=1, source_target_pairs={{0,12},{4,8},{8,4},{12,0},{1,13},{5,9},{9,5},{13,1},{2,14},{6,10},... | collective-permute-start | bytes 1572872 | tf_op jit(solution)/shard_map/ppermute | solution.py:266
  1590.3 36.4 %collective-permute-start.31 = (f32[128,4,256]{2,0,1:T(8,128)}, f32[128,4,256]{2,0,1:T(8,128)}, u32[]{:S(2)}, u32[]{:S(2)}) collective-permute-start(f32[128,4,256]{2,0,1:T(8,128)} %get-tuple-element.167), channel_id=1, source_target_pairs={{0,4},{4,0},{8,12},{12,8},{1,5},{5,1},{9,13},{13,9},{2,6},{6,2},{1... | collective-permute-start | bytes 1572872 | tf_op jit(solution)/shard_map/ppermute | solution.py:266
  1602.2 33.1 %collective-permute-start.32 = (f32[128,4,256]{2,0,1:T(8,128)}, f32[128,4,256]{2,0,1:T(8,128)}, u32[]{:S(2)}, u32[]{:S(2)}) collective-permute-start(f32[128,4,256]{2,0,1:T(8,128)} %get-tuple-element.166), channel_id=1, source_target_pairs={{0,8},{4,12},{8,0},{12,4},{1,9},{5,13},{9,1},{13,5},{2,10},{6,14},... | collective-permute-start | bytes 1572872 | tf_op jit(solution)/shard_map/ppermute | solution.py:266
  1610.6 36.5 %collective-permute-start.33 = (f32[128,4,256]{2,0,1:T(8,128)}, f32[128,4,256]{2,0,1:T(8,128)}, u32[]{:S(2)}, u32[]{:S(2)}) collective-permute-start(f32[128,4,256]{2,0,1:T(8,128)} %get-tuple-element.165), channel_id=1, source_target_pairs={{0,12},{4,8},{8,4},{12,0},{1,13},{5,9},{9,5},{13,1},{2,14},{6,10},... | collective-permute-start | bytes 1572872 | tf_op jit(solution)/shard_map/ppermute | solution.py:266
  (171 other events, 2503.5 us)
Sparse Core Ops, SparseCore 0:
  24.9 56.5 all-gather.4
  1067.9 129.8 all-reduce.1
where the time goes:
time: 1790 us; the launch traced here: 1780 us
  Pallas kernels  500 us (28%)
  waiting for transfers between devices  392 us (22%)
  local copies, waits for them, and re-layouts  363 us (20%)
  blocking collectives  162 us (9%)
  matrix products  156 us (9%)
  other arithmetic  127 us (7%)
  starting transfers between devices  53.1 us (3%)
  between operations  27.9 us (2%)
    pallas_call x8, Pallas kernels, scatter_eight(): pl.pallas_call(scatter_kernel, out_shape=jax.ShapeDtypeStruct(shape, kind...  300 us
    pallas_call x9, Pallas kernels, gather_eight(): pl.pallas_call(gather_kernel, out_shape=jax.ShapeDtypeStruct((8,) + x.sha...  200 us
    ppermute x6, waiting for transfers between devices, share_scatter(): lax.ppermute(piece, AX, SWAP).astype(F32)  166 us
    dot_general x25, matrix products, dot(): return lax.dot_general(x, y, (dims, ((), ())), preferred_element_type=F32)  147 us
    ppermute x6, waiting for transfers between devices, share_gather(): other = lax.ppermute(block, AX, SWAP)  130 us
    unnamed x365, local copies, waits for them, and re-layouts  96 us
    another operation x8, local copies, waits for them, and re-layouts  61.4 us
    ppermute x18, waiting for transfers between devices, exchange(): moved = lax.ppermute(take(there), QX, [(k, k ^ step) for k in range(4)])  59.2 us
  transfers between devices with their start and end apart: 50, of which 23 were waited for; matrix products, arithmetic and copies ran while one was open for 22% of the time, Pallas kernels for 8%

commit v1 on v0

--- a/solution.py
+++ b/solution.py
@@ -4,6 +4,7 @@
 import jax.numpy as jnp
 from jax import lax
 from jax.experimental import pallas as pl
+from jax.experimental.layout import Layout, with_layout_constraint
 from jax.experimental.pallas import tpu as pltpu
 from jax.sharding import Mesh, PartitionSpec as P
 
@@ -206,6 +207,70 @@
     )(parts)
 
 
+def total_kernel(extent, x_ref, o_ref, held, sums, send, recv):
+    names = (AX, BX, EX, DX, CX)
+    here = dict((name, lax.axis_index(name)) for name in names)
+    near = [
+        {BX: lax.rem(here[BX] + k // 4, 2), EX: lax.rem(here[EX] + k // 2 % 2, 2), CX: lax.rem(here[CX] + k % 2, 2)}
+        for k in range(1, 8)
+    ]
+    away = [
+        {AX: lax.rem(here[AX] + k // extent, 2), DX: lax.rem(here[DX] + k % extent, extent)}
+        for k in range(1, 2 * extent)
+    ]
+    greet(near + away)
+
+    def copy(number, source, target, peer):
+        made = pltpu.make_async_remote_copy(
+            src_ref=source,
+            dst_ref=target,
+            send_sem=send.at[number],
+            recv_sem=recv.at[number],
+            device_id=peer,
+            device_id_type=MESH,
+        )
+        made.start()
+        return made
+
+    first = [copy(k, x_ref, held.at[k], peer) for k, peer in enumerate(near)]
+    for made in first:
+        made.wait_recv()
+    terms = [x_ref[...]] + [held[k] for k in range(7)]
+    while len(terms) > 1:
+        terms = [terms[k] + terms[k + 1] for k in range(0, len(terms), 2)]
+    sums[...] = terms[0]
+    mine = 7 + here[AX] * extent + here[DX]
+    second = [copy(7 + k, sums, held.at[mine], peer) for k, peer in enumerate(away)]
+    held[mine] = terms[0]
+    for made in second:
+        made.wait_recv()
+    total = held[7]
+    for k in range(1, 2 * extent):
+        total = total + held[7 + k]
+    o_ref[...] = total
+    for made in first + second:
+        made.wait_send()
+
+
+def total_all(tile):
+    extent = lax.axis_size(DX)
+    peers = 6 + 2 * extent
+    return pl.pallas_call(
+        partial(total_kernel, extent),
+        out_shape=jax.ShapeDtypeStruct(tile.shape, tile.dtype),
+        in_specs=[pl.BlockSpec(memory_space=pltpu.VMEM)],
+        out_specs=pl.BlockSpec(memory_space=pltpu.VMEM),
+        scratch_shapes=[
+            pltpu.VMEM((peers + 1,) + tile.shape, tile.dtype),
+            pltpu.VMEM(tile.shape, tile.dtype),
+            pltpu.SemaphoreType.DMA((peers,)),
+            pltpu.SemaphoreType.DMA((peers,)),
+        ],
+        compiler_params=pltpu.CompilerParams(collective_id=9, has_side_effects=True),
+        cost_estimate=pl.CostEstimate(flops=0, bytes_accessed=30_000_000, transcendentals=0),
+    )(tile)
+
+
 def spread(rows, number):
     count, width = rows.shape
     full = gather_eight(rows.reshape(2, count // 2, width), number, 80_000_000)
@@ -218,54 +283,166 @@
     return part.reshape(count // 8, width)
 
 
-def share_gather(block):
+def after(value, *needed):
+    return lax.optimization_barrier((value, needed))[0]
+
+
+def plain(x):
+    return with_layout_constraint(x, Layout(tuple(range(x.ndim))))
+
+
+def send(block, axis, step, extent):
+    ring = [(k, (k + step) % extent) for k in range(extent)]
+    return plain(lax.ppermute(plain(block), axis, ring))
+
+
+def own_sends(block):
+    extent = lax.axis_size(DX)
+    across = send(block, AX, 1, 2)
+    return across, [send(block, DX, step, extent) for step in range(1, extent)]
+
+
+def far_sends(across):
+    extent = lax.axis_size(DX)
+    return [send(across, DX, step, extent) for step in range(1, extent)]
+
+
+def assemble(block, across, beside, far, a_axis, d_axis):
     a, d, extent = lax.axis_index(AX), lax.axis_index(DX), lax.axis_size(DX)
-    other = lax.ppermute(block, AX, SWAP)
-    full = jnp.zeros((2, extent) + block.shape, block.dtype)
-    zeros = (0,) * block.ndim
+    shape = list(block.shape)
+    shape[a_axis], shape[d_axis] = 2, extent
+    full = jnp.zeros(shape, block.dtype)
 
     def put(full, piece, row, column):
-        return lax.dynamic_update_slice(full, piece[None, None], (row, column) + zeros)
-
-    full = put(full, block, a, d)
-    full = put(full, other, 1 - a, d)
-    for step in range(1, extent):
-        ring = [(k, (k + step) % extent) for k in range(extent)]
-        column = lax.rem(d + extent - step, extent)
-        full = put(full, lax.ppermute(block, DX, ring), a, column)
-        full = put(full, lax.ppermute(other, DX, ring), 1 - a, column)
+        start = [0] * block.ndim
+        start[a_axis], start[d_axis] = row, column
+        return lax.dynamic_update_slice(full, piece, start)
+
+    full = put(put(full, block, a, d), across, 1 - a, d)
+    for step, (near_piece, far_piece) in enumerate(zip(beside, far)):
+        column = lax.rem(d + extent - step - 1, extent)
+        full = put(put(full, near_piece, a, column), far_piece, 1 - a, column)
     return full
 
 
-def share_scatter(grad):
-    a, d, extent = lax.axis_index(AX), lax.axis_index(DX), lax.axis_size(DX)
-
-    def column(k):
-        return lax.dynamic_index_in_dim(grad, k, 1, False)
-
-    total = column(d)
-    for step in range(1, extent):
-        ring = [(k, (k + step) % extent) for k in range(extent)]
-        piece = column(lax.rem(d + step, extent)).astype(WIRE)
-        total = total + lax.ppermute(piece, DX, ring).astype(F32)
-    piece = lax.dynamic_index_in_dim(total, 1 - a, 0, False).astype(WIRE)
-    return lax.dynamic_index_in_dim(total, a, 0, False) + lax.ppermute(piece, AX, SWAP).astype(F32)
+def pick(array, index, axis):
+    return lax.dynamic_slice_in_dim(array, index, 1, axis)
+
+
+def grad_kernel(with_base, d_ref, left_ref, right_ref, *refs):
+    base_ref = refs[0] if with_base else None
+    keep_ref, piece_ref = refs[-2:]
+    product = tn(left_ref[...], right_ref[...])
+    if with_base:
+        product = product + base_ref[...]
+
+    @pl.when(pl.program_id(0) == 0)
+    def _():
+        keep_ref[0] = product
+
+    @pl.when(pl.program_id(0) > 0)
+    def _():
+        piece_ref[0, 0] = product.astype(piece_ref.dtype)
+
+
+def weight_grad(left, right, rows, wire, base=None):
+    extent = lax.axis_size(DX)
+    count, columns = right.shape
+    lead = left.shape[1] // (rows * extent)
+    if rows % 128:
+        full = tn(left, right) if base is None else tn(left, right) + base
+        full = full.reshape(lead, extent, rows, columns)
+        split = [
+            lax.dynamic_index_in_dim(full, lax.rem(lax.axis_index(DX) + s, extent), 1, False)
+            for s in range(extent)
+        ]
+        return split[0], jnp.stack(split[1:]).astype(wire)
+
+    def block(s, k, d):
+        return k * extent + lax.rem(d[0] + s, extent)
+
+    in_specs = [
+        pl.BlockSpec((left.shape[0], rows), lambda s, k, d: (0, block(s, k, d))),
+        pl.BlockSpec((count, columns), lambda s, k, d: (0, 0)),
+    ]
+    operands = [left, right]
+    if base is not None:
+        in_specs.append(pl.BlockSpec((rows, columns), lambda s, k, d: (block(s, k, d), 0)))
+        operands.append(base)
+    keep_spec = pl.BlockSpec(
+        (1, rows, columns), lambda s, k, d: (jnp.where(s == 0, k, lead - 1), 0, 0)
+    )
+    piece_spec = pl.BlockSpec(
+        (1, 1, rows, columns),
+        lambda s, k, d: (jnp.maximum(s - 1, 0), jnp.where(s == 0, 0, k), 0, 0),
+    )
+    return pl.pallas_call(
+        partial(grad_kernel, base is not None),
+        out_shape=(
+            jax.ShapeDtypeStruct((lead, rows, columns), F32),
+            jax.ShapeDtypeStruct((extent - 1, lead, rows, columns), wire),
+        ),
+        grid_spec=pltpu.PrefetchScalarGridSpec(
+            num_scalar_prefetch=1,
+            grid=(extent, lead),
+            in_specs=in_specs,
+            out_specs=(keep_spec, piece_spec),
+        ),
+        compiler_params=pltpu.CompilerParams(vmem_limit_bytes=48 << 20),
+        cost_estimate=pl.CostEstimate(
+            flops=2 * count * left.shape[1] * columns,
+            bytes_accessed=left.size * 2 + right.size * 2 + left.shape[1] * columns * 4,
+            transcendentals=0,
+        ),
+    )(lax.axis_index(DX).reshape(1), *operands)
+
+
+def product_kernel(left_ref, right_ref, out_ref):
+    out_ref[...] = tn(left_ref[...], right_ref[...])
+
+
+def product(left, right, rows):
+    count, columns = right.shape
+    return pl.pallas_call(
+        product_kernel,
+        out_shape=jax.ShapeDtypeStruct((left.shape[1], columns), F32),
+        grid=(left.shape[1] // rows,),
+        in_specs=[
+            pl.BlockSpec((count, rows), lambda k: (0, k)),
+            pl.BlockSpec((count, columns), lambda k: (0, 0)),
+        ],
+        out_specs=pl.BlockSpec((rows, columns), lambda k: (k, 0)),
+        compiler_params=pltpu.CompilerParams(vmem_limit_bytes=48 << 20),
+        cost_estimate=pl.CostEstimate(
+            flops=2 * count * left.shape[1] * columns,
+            bytes_accessed=left.size * 2 + right.size * 2 + left.shape[1] * columns * 4,
+            transcendentals=0,
+        ),
+    )(left, right)
+
+
+def d_sends(pieces):
+    extent = lax.axis_size(DX)
+    return [send(pieces[step - 1], DX, step, extent) for step in range(1, extent)]
+
+
+def total_at(index, keep, pieces):
+    total = pick(keep.reshape((2, -1) + keep.shape[1:]), index, 0)
+    for piece in pieces:
+        total = total + pick(piece.reshape((2, -1) + piece.shape[1:]), index, 0).astype(F32)
+    return total[0]
+
+
+def a_send(keep, pieces, wire):
+    return send(total_at(1 - lax.axis_index(AX), keep, pieces).astype(wire), AX, 1, 2)
+
+
+def a_total(keep, pieces, across):
+    return total_at(lax.axis_index(AX), keep, pieces) + across.astype(F32)
 
 
 def exchange(pieces):
-    q = lax.axis_index(QX)
-    zeros = (0,) * (pieces.ndim - 1)
-    full = jnp.zeros_like(pieces)
-
-    def take(k):
-        return lax.dynamic_index_in_dim(pieces, k, 0, False)
-
-    full = lax.dynamic_update_slice(full, take(q)[None], (q,) + zeros)
-    for step in (1, 2, 3):
-        there = jnp.bitwise_xor(q, step)
-        moved = lax.ppermute(take(there), QX, [(k, k ^ step) for k in range(4)])
-        full = lax.dynamic_update_slice(full, moved[None], (there,) + zeros)
-    return full
+    return plain(lax.all_to_all(plain(pieces), QX, 0, 0))
 
 
 def layer_norm(inputs, gain, bias):
@@ -287,41 +464,49 @@
     return back, jnp.sum(upstream * normed, 0), jnp.sum(upstream, 0)
 
 
+def dot_images(x, y, x_side, y_side):
+    dims = (((x_side,), (y_side,)), ((0,), (0,)))
+    return lax.dot_general(x, y, dims, preferred_element_type=F32)
+
+
 def heads(x, images):
-    return x.reshape(images, -1, x.shape[-1] // HD, HD)
-
-
-def flat(x):
-    return x.reshape(x.shape[0] * x.shape[1], -1).astype(BF16)
-
-
-def ein(text, x, y):
-    return jnp.einsum(text, x, y, preferred_element_type=F32)
-
-
-SCORE = "bqhe,bkhe->bhqk"
-MIX = "bhqk,bkhe->bqhe"
-TURN = "bhqk,bqhe->bkhe"
+    x = x.reshape(images, -1, x.shape[-1])
+    return [x[..., k : k + HD] for k in range(0, x.shape[-1], HD)]
+
+
+def flat(parts):
+    joined = jnp.concatenate([part.astype(BF16) for part in parts], -1)
+    return joined.reshape(-1, joined.shape[-1])
 
 
 def attend(queries, keys, values):
-    scores = ein(SCORE, queries, keys) * SCALE
-    top = jnp.max(scores, -1, keepdims=True)
-    logsum = top + jnp.log(jnp.sum(jnp.exp(scores - top), -1, keepdims=True))
-    probs = jnp.exp(scores - logsum)
-    return flat(ein(MIX, probs.astype(BF16), values)), probs
-
-
-def attend_back(upstream, queries, keys, values, probs, images):
-    grad_out = heads(upstream, images)
-    grad_probs = ein(SCORE, grad_out, values)
-    inner = jnp.sum(probs * grad_probs, -1, keepdims=True)
-    grad_scores = (probs * (grad_probs - inner)).astype(BF16)
-    return (
-        flat(ein(MIX, grad_scores, keys) * SCALE),
-        flat(ein(TURN, grad_scores, queries) * SCALE),
-        flat(ein(TURN, probs.astype(BF16), grad_out)),
-    )
+    mixed, saved = [], []
+    for query, key, value in zip(queries, keys, values):
+        scores = dot_images(query, key, 2, 2) * SCALE
+        top = jnp.max(scores, -1, keepdims=True)
+        logsum = top + jnp.log(jnp.sum(jnp.exp(scores - top), -1, keepdims=True))
+        probs = jnp.exp(scores - logsum)
+        mixed.append(dot_images(probs.astype(BF16), value, 2, 1))
+        saved.append(probs)
+    return flat(mixed), saved
+
+
+def attend_back(upstream, queries, keys, values, saved, images):
+    grads = []
+    for grad_out, query, key, value, probs in zip(
+        heads(upstream, images), queries, keys, values, saved
+    ):
+        grad_probs = dot_images(grad_out, value, 2, 2)
+        inner = jnp.sum(probs * grad_probs, -1, keepdims=True)
+        grad_scores = (probs * (grad_probs - inner)).astype(BF16)
+        grads.append(
+            (
+                dot_images(grad_scores, key, 2, 1) * SCALE,
+                dot_images(grad_scores, query, 1, 1) * SCALE,
+                dot_images(probs.astype(BF16), grad_out, 1, 1),
+            )
+        )
+    return tuple(flat(parts) for parts in zip(*grads))
 
 
 def adamw(state, grad, rate, decay, fix_one, fix_two):
@@ -336,54 +521,62 @@
     table_state, vector_state, proj_state, text_state, out_state, expand_state, contract_state = (
         states[k : k + 3] for k in range(0, 21, 3)
     )
-    a, b, e, c = (lax.axis_index(k) for k in (AX, BX, EX, CX))
+    b, e, c = (lax.axis_index(k) for k in (BX, EX, CX))
     extent = lax.axis_size(DX)
     vectors = vector_state[0]
     length = vectors.shape[0] - 9
     norm_rows = vectors[length + 1 :]
     width = vectors.shape[1]
-
     block = table_state[0].shape[0]
-    table = share_gather(table_state[0].astype(BF16)).reshape(-1, width)
+    kinds, in_rows, half = proj_state[0].shape
+    text_rows = text_state[0].shape[1]
+    hidden_width = extent * block
+    pair = 2 * HD
+
+    own_images = image_codes.shape[1]
+    tokens = own_images * length
+    small = jnp.concatenate(
+        [
+            image_codes.reshape(2, -1),
+            masked.reshape(2, -1),
+            jnp.broadcast_to(null_caption.reshape(2, -1, 1), masked.shape).reshape(2, -1),
+        ],
+        1,
+    )
+    small = lax.dynamic_index_in_dim(small, c, 0, False)
+    small = jnp.pad(small, (0, 16 * 128 - small.shape[0] % (16 * 128)))
+    own_mask, own_null = small[tokens : 2 * tokens], small[2 * tokens : 3 * tokens]
+    gathered = gather_eight(small.reshape(2, 8, -1), 6, 20_000_000).reshape(8, -1)
+    group_codes = gathered[:, :tokens].reshape(-1)
+    weight = gathered[:, tokens : 2 * tokens].reshape(-1).astype(F32)
+    chosen = own_mask[:, None] == 1
+    keep_rows = 1.0 - own_null[:, None].astype(F32)
+    images = 8 * own_images
+    group_captions = lax.all_gather(captions, QX).reshape(-1, captions.shape[-1])
+
+    table_block = table_state[0].astype(BF16)[None, None]
+    contract_block = contract_state[0].astype(BF16)[None, None]
+    out_block = out_state[0].astype(BF16)[:, None, None]
+    table_own = own_sends(table_block)
+
+    pieces = proj_state[0].astype(BF16).reshape(kinds, in_rows, 2, 4, HD).transpose(3, 1, 0, 2, 4)
+    proj_block = exchange(pieces.reshape(4, in_rows, kinds * pair))[None, :, None]
+    proj_own = own_sends(proj_block)
+    pieces = text_state[0].astype(BF16).reshape(2, text_rows, 2, 4, HD).transpose(3, 1, 0, 2, 4)
+    text_block = exchange(pieces.reshape(4, text_rows, 2 * pair))[None, :, None]
+    pieces = expand_state[0].astype(BF16).reshape(in_rows, 2, 4, hidden_width)
+    pieces = pieces.transpose(2, 0, 1, 3).reshape(4, in_rows, 2 * hidden_width)
+    expand_block = exchange(pieces)[None, :, None]
+    out_block = after(out_block, table_own[0])
+    out_own = own_sends(out_block)
+    table_far = far_sends(table_own[0])
+    table = assemble(table_block, *table_own, table_far, 0, 1).reshape(-1, width)
     codes_here = table.shape[0]
 
-    kinds, in_rows, half = proj_state[0].shape
-    deep = kinds
-    pieces = proj_state[0].astype(BF16).reshape(kinds, in_rows, 2, 4, HD)
-    pieces = exchange(pieces.transpose(3, 0, 1, 2, 4).reshape(4, kinds, in_rows, 2 * HD))
-    proj = share_gather(pieces).transpose(3, 0, 2, 1, 4, 5).reshape(kinds, width, 2 * HD)
-    w_qkv = proj[:3].transpose(1, 0, 2).reshape(width, 6 * HD)
-    w_cross = proj[3]
-
-    out_maps = share_gather(out_state[0].astype(BF16))
-    out_maps = out_maps.transpose(2, 0, 1, 3, 4).reshape(2, 2 * HD, width)
-
-    text_rows = text_state[0].shape[1]
-    pieces = text_state[0].astype(BF16).reshape(2, text_rows, 2, 4, HD)
-    pieces = exchange(pieces.transpose(3, 1, 0, 2, 4).reshape(4, text_rows, 4 * HD))
-    w_text = share_gather(pieces).transpose(0, 2, 1, 3, 4).reshape(-1, 4 * HD)
-
-    hidden_width = extent * block
-    pieces = expand_state[0].astype(BF16).reshape(in_rows, 2, 4, hidden_width)
-    pieces = exchange(pieces.transpose(2, 0, 1, 3).reshape(4, in_rows, 2 * hidden_width))
-    expand = share_gather(pieces).transpose(0, 2, 1, 3, 4).reshape(width, 2 * hidden_width)
-
-    contract = share_gather(contract_state[0].astype(BF16)).reshape(-1, width)
-
-    mask_total = lax.psum(jnp.sum(masked).astype(F32), DP)
-    group_codes = lax.all_gather(image_codes, QX).reshape(-1)
-    group_mask = lax.all_gather(masked, QX).reshape(-1)
-    group_captions = lax.all_gather(captions, QX).reshape(-1, captions.shape[-1])
-    images = group_codes.shape[0] // length
-    chosen = lax.dynamic_index_in_dim(masked, c, 0, False).reshape(-1)[:, None] == 1
-    keep = 1.0 - lax.dynamic_index_in_dim(null_caption, c, 0, False).astype(F32)
-    keep_rows = jnp.repeat(keep, length)[:, None]
-    own_images = keep.shape[0]
-
-    in_half = lax.rem(group_codes, 2 * 4 * hidden_width)
+    in_half = lax.rem(group_codes, 8 * hidden_width)
     outer = in_half // block
     inside = (
-        (group_codes // (2 * 4 * hidden_width) == c)
+        (group_codes // (8 * hidden_width) == c)
         & (lax.rem(outer // extent, 2) == e)
         & (lax.rem(outer // (2 * extent), 2) == b)
     )
@@ -395,26 +588,48 @@
     x_zero = jnp.where(chosen, vectors[length], looked)
     x_zero = x_zero + jnp.tile(vectors[:length], (own_images, 1))
     a_one, norm_one = layer_norm(x_zero, norm_rows[0], norm_rows[1])
-    a_one = spread(a_one, 2)
-    triple = nn(a_one, w_qkv).astype(BF16)
+    proj_far = far_sends(proj_own[0])
+    text_block = after(text_block, proj_own[0], a_one)
+    text_own = own_sends(text_block)
+    a_one = spread(after(a_one, proj_own[0]), 2)
+    proj = assemble(proj_block, *proj_own, proj_far, 0, 2).reshape(width, kinds * pair)
+    w_qkv, w_cross = proj[:, : 3 * pair], proj[:, 3 * pair :]
+    out_far = far_sends(out_own[0])
+    triple = nn(a_one, after(w_qkv, out_own[0])).astype(BF16)
     queries, keys, values = (
-        heads(triple[:, k : k + 2 * HD], images) for k in (0, 2 * HD, 4 * HD)
+        heads(triple[:, k : k + pair], images) for k in (0, pair, 2 * pair)
     )
     attn_one, probs_one = attend(queries, keys, values)
-    x_one = x_zero + collect(nn(attn_one, out_maps[0]), 3)
-
-    pair = nn(group_captions, w_text).astype(BF16)
-    text_keys, text_values = heads(pair[:, : 2 * HD], images), heads(pair[:, 2 * HD :], images)
+    out_maps = assemble(out_block, *out_own, out_far, 1, 2).reshape(2, pair, width)
+    part = nn(attn_one, out_maps[0])
+    expand_block = after(expand_block, part)
+    expand_own = own_sends(expand_block)
+    x_one = x_zero + collect(part, 3)
+
     a_two, norm_two = layer_norm(x_one, norm_rows[2], norm_rows[3])
-    a_two = spread(a_two, 2)
+    text_far = far_sends(text_own[0])
+    contract_block = after(contract_block, a_two)
+    contract_own = own_sends(contract_block)
+    a_two = spread(after(a_two, text_own[0]), 2)
+    w_text = assemble(text_block, *text_own, text_far, 0, 2).reshape(-1, 2 * pair)
+    text_pair = nn(group_captions, w_text).astype(BF16)
+    text_keys, text_values = heads(text_pair[:, :pair], images), heads(text_pair[:, pair:], images)
     cross = heads(nn(a_two, w_cross).astype(BF16), images)
     attn_two, probs_two = attend(cross, text_keys, text_values)
-    x_two = x_one + keep_rows * collect(nn(attn_two, out_maps[1]), 3)
-
+    part = nn(attn_two, out_maps[1])
+    expand_far = far_sends(expand_own[0])
+    x_two = x_one + keep_rows * collect(after(part, expand_own[0]), 3)
+
+    mask_total = after(jnp.broadcast_to(jnp.sum(weight), (8, 128)), x_one)
+    mask_total = mask_total + send(mask_total, AX, 1, 2)
+    mask_total = (mask_total + sum(far_sends(mask_total)))[0, 0]
     a_three, norm_three = layer_norm(x_two, norm_rows[4], norm_rows[5])
-    a_three = spread(a_three, 2)
+    contract_far = far_sends(contract_own[0])
+    a_three = spread(after(a_three, contract_own[0]), 2)
+    expand = assemble(expand_block, *expand_own, expand_far, 0, 2).reshape(width, -1)
     preact = nn(a_three, expand)
     hidden = jax.nn.gelu(preact, approximate=True).astype(BF16)
+    contract = assemble(contract_block, *contract_own, contract_far, 0, 1).reshape(-1, width)
     x_three = x_two + collect(nn(hidden, contract), 3)
 
     a_four, norm_four = layer_norm(x_three, norm_rows[6], norm_rows[7])
@@ -429,94 +644,138 @@
     peak = jnp.max(stats[:, 0], 0)
     total = jnp.sum(stats[:, 1] * jnp.exp(stats[:, 0] - peak), 0)
     head_logsum = peak + jnp.log(total)
-    weight = group_mask.astype(F32)
     loss_sum = jnp.sum(weight * (head_logsum - jnp.sum(stats[:, 2], 0)))
 
     head_probs = jnp.exp(logits - head_logsum[:, None])
     logit_grad = (head_probs - at_code.astype(F32)) * (weight / mask_total)[:, None]
     logit_grad = logit_grad.astype(BF16)
     upstream = collect(nn(logit_grad, table), 3)
-    table_grad = tn(logit_grad, a_four)
     grad_three, gain_six, gain_seven = norm_back(upstream, norm_four, norm_rows[6])
     branch_three = spread(grad_three.astype(BF16), 2)
+
+    contract_keep, pieces = weight_grad(hidden, branch_three, block, BF16)
+    contract_pieces = d_sends(pieces)
     hidden_grad = nt(branch_three, contract)
     gelu_pull = jax.vjp(partial(jax.nn.gelu, approximate=True), preact)[1]
     preact_grad = gelu_pull(hidden_grad)[0].astype(BF16)
-    back = collect(nt(preact_grad, expand), 3)
-    contract_grad = tn(hidden, branch_three)
-    contract_shard = share_scatter(contract_grad.reshape(2, extent, block, width))
-    expand_grad = tn(a_three, preact_grad).reshape(2, 4, extent, in_rows, 2 * hidden_width)
-    expand_shard = exchange(share_scatter(expand_grad.transpose(0, 2, 1, 3, 4)))
-    expand_shard = expand_shard.reshape(4, in_rows, 2, hidden_width).transpose(1, 2, 0, 3)
-    expand_shard = expand_shard.reshape(expand_state[0].shape)
+    expand_keep, pieces = weight_grad(a_three, preact_grad, in_rows, BF16)
+    part = nt(preact_grad, expand)
+    back = collect(after(part, pieces), 3)
+    expand_pieces = d_sends(pieces)
 
     back, gain_four, gain_five = norm_back(back, norm_three, norm_rows[4])
     grad_two = grad_three + back
-    branch_two = spread(grad_two.astype(BF16) * keep_rows.astype(BF16), 2)
+    branch_two = grad_two.astype(BF16) * keep_rows.astype(BF16)
+    table_head = product(logit_grad, a_four, 256)
+    branch_two = spread(after(branch_two, table_head), 2)
     attn_grad = nt(branch_two, out_maps[1]).astype(BF16)
     cross_grad, key_grad, value_grad = attend_back(
         attn_grad, cross, text_keys, text_values, probs_two, images
     )
-    back = collect(nt(cross_grad, w_cross), 3)
-    text_grad = tn(group_captions, jnp.concatenate([key_grad, value_grad], 1))
-    text_grad = text_grad.reshape(2, 4, extent, text_rows, 4 * HD).transpose(0, 2, 1, 3, 4)
-    text_shard = exchange(share_scatter(text_grad)).reshape(4, text_rows, 2, 2, HD)
-    text_shard = text_shard.transpose(2, 1, 3, 0, 4).reshape(text_state[0].shape)
+    pair_grad = jnp.concatenate([key_grad, value_grad], 1)
+    text_keep, text_wire = weight_grad(group_captions, pair_grad, text_rows, WIRE)
+    part = nt(cross_grad, w_cross)
+    contract_across = a_send(contract_keep, after(contract_pieces, part), BF16)
+    back = collect(after(part, text_wire, *contract_pieces), 3)
+    text_pieces = d_sends(text_wire)
 
     back, gain_two, gain_three = norm_back(back, norm_two, norm_rows[2])
     grad_one = grad_two + back
-    branch_one = spread(grad_one.astype(BF16), 2)
+    expand_across = a_send(expand_keep, after(expand_pieces, grad_one), BF16)
+    branch_one = spread(after(grad_one.astype(BF16), *expand_pieces), 2)
     attn_grad = nt(branch_one, out_maps[0]).astype(BF16)
     triple_grad = jnp.concatenate(
         attend_back(attn_grad, queries, keys, values, probs_one, images), 1
     )
-    back = collect(nt(triple_grad, w_qkv), 3)
-    out_grad = jnp.stack([tn(attn_one, branch_one), tn(attn_two, branch_two)])
-    out_grad = out_grad.reshape(2, 2, extent, HD // extent, width).transpose(1, 2, 0, 3, 4)
-    out_shard = share_scatter(out_grad)
-    proj_grad = jnp.concatenate([tn(a_one, triple_grad), tn(a_two, cross_grad)], 1)
-    proj_grad = proj_grad.reshape(2, 4, extent, in_rows, kinds, 2 * HD)
-    proj_shard = exchange(share_scatter(proj_grad.transpose(0, 2, 1, 3, 4, 5)))
-    proj_shard = proj_shard.reshape(4, in_rows, kinds, 2, HD).transpose(2, 1, 3, 0, 4)
-    proj_shard = proj_shard.reshape(proj_state[0].shape)
+    cross_keep, cross_wire = weight_grad(a_two, cross_grad, in_rows, WIRE)
+    cross_pieces = d_sends(cross_wire)
+    triple_keep, triple_wire = weight_grad(a_one, triple_grad, in_rows, WIRE)
+    part = nt(triple_grad, w_qkv)
+    contract_shard = a_total(contract_keep, contract_pieces, contract_across).reshape(block, width)
+    text_across = a_send(text_keep, after(text_pieces, part), WIRE)
+    back = collect(after(part, triple_wire, contract_shard, *text_pieces), 3)
+    triple_pieces = d_sends(triple_wire)
 
     back, gain_zero, gain_one = norm_back(back, norm_one, norm_rows[0])
     grad_zero = grad_one + back
-    unmasked = jnp.where(chosen, 0.0, grad_zero)
-    high = unmasked.astype(BF16)
-    low = (unmasked - high.astype(F32)).astype(BF16)
-    looked_grad = spread(jnp.concatenate([high, low], 1), 5)
-    looked_grad = tn(at_code.astype(BF16), looked_grad)
-    table_grad = table_grad + looked_grad[:, :width] + looked_grad[:, width:]
-    table_shard = share_scatter(table_grad.reshape(2, extent, block, width))
+    looked_grad = jnp.where(chosen, 0.0, grad_zero).astype(BF16)
+    expand_shard = a_total(expand_keep, expand_pieces, expand_across)
+    expand_shard = exchange(expand_shard)
+    cross_across = a_send(cross_keep, after(cross_pieces, grad_zero), WIRE)
+    looked_grad = spread(after(looked_grad, *cross_pieces), 2)
+    table_keep, table_wire = weight_grad(
+        at_code.astype(BF16), looked_grad, block, BF16, table_head
+    )
+    table_pieces = d_sends(table_wire)
+    triple_across = a_send(triple_keep, after(triple_pieces, table_keep), WIRE)
+    text_shard = exchange(a_total(text_keep, text_pieces, text_across))
+    out_grad = [tn(attn_one, branch_one), tn(attn_two, branch_two)]
+    out_grad = plain(jnp.stack(out_grad).reshape(2, 2, extent, HD // extent, width))
+    d = lax.axis_index(DX)
+    out_grad = out_grad.transpose(2, 1, 0, 3, 4)
+    out_wire = [
+        lax.dynamic_index_in_dim(out_grad, lax.rem(d + step, extent), 0, False)
+        for step in range(extent)
+    ]
+    out_pieces = d_sends([wire.astype(BF16) for wire in out_wire[1:]])
+    out_across = a_send(out_wire[0], out_pieces, BF16)
+    table_across = a_send(table_keep, table_pieces, BF16)
+    triple_shard = a_total(triple_keep, triple_pieces, triple_across)
+    cross_shard = a_total(cross_keep, cross_pieces, cross_across)
+    proj_shard = exchange(jnp.concatenate([triple_shard, cross_shard], 2))
+    out_shard = a_total(out_wire[0], out_pieces, out_across).reshape(out_state[0].shape)
+    table_shard = a_total(table_keep, table_pieces, table_across).reshape(block, width)
+
+    def by_head(shard, count):
+        return jnp.stack(
+            [
+                jnp.concatenate(
+                    [
+                        shard[q, :, (kind * 2 + row) * HD : (kind * 2 + row + 1) * HD]
+                        for row in range(2)
+                        for q in range(4)
+                    ],
+                    1,
+                )
+                for kind in range(count)
+            ]
+        )
+
+    expand_shard = jnp.concatenate(
+        [
+            expand_shard[q, :, row * hidden_width : (row + 1) * hidden_width]
+            for row in range(2)
+            for q in range(4)
+        ],
+        1,
+    )
+    text_shard = by_head(text_shard, 2)
+    proj_shard = by_head(proj_shard, kinds)
 
     position_grad = jnp.sum(grad_zero.reshape(own_images, length, -1), 0)
     mask_grad = jnp.sum(jnp.where(chosen, grad_zero, 0.0), 0)
-    vector_grad = jnp.concatenate(
-        [
-            position_grad,
-            jnp.stack(
-                [
-                    mask_grad,
-                    gain_zero,
-                    gain_one,
-                    gain_two,
-                    gain_three,
-                    gain_four,
-                    gain_five,
-                    gain_six,
-                    gain_seven,
-                ]
-            ),
-        ],
-        0,
-    )
-    vector_grad = lax.psum(vector_grad, DP + (CX,))
-    loss_value = lax.psum(loss_sum, MX) / mask_total
+    gains = [gain_zero, gain_one, gain_two, gain_three, gain_four, gain_five, gain_six, gain_seven]
+    vector_grad = jnp.concatenate([position_grad, jnp.stack([mask_grad] + gains)], 0)
+    rows = vector_grad.shape[0]
+    padded = -(-rows // 16) * 16
+    vector_grad = jnp.pad(vector_grad, ((0, padded - rows), (0, 0)))
+    vector_grad = after(vector_grad, table_keep)
+    vector_part = scatter_eight(vector_grad.reshape(8, 2, 8, -1), 7, 40_000_000)
+    vector_part = vector_part + send(vector_part, AX, 1, 2)
+    if extent == 2:
+        vector_part = vector_part + far_sends(vector_part)[0]
+    else:
+        vector_part = lax.psum(vector_part, DX)
 
     shards = (table_shard, proj_shard, text_shard, out_shard, expand_shard, contract_shard)
     squares = sum((jnp.sum(piece * piece) for piece in shards))
-    grad_norm = jnp.sqrt(lax.psum(squares, DP + (CX,)) + jnp.sum(vector_grad * vector_grad))
+    squares = squares + jnp.sum(vector_part * vector_part) / (2 * extent)
+    lanes = jnp.arange(128)[None, :]
+    numbers = jnp.where(lanes == 0, squares, jnp.where(lanes == 1, loss_sum, 0.0))
+    numbers = total_all(jnp.broadcast_to(numbers, (8, 128)))
+    loss_value = numbers[0, 1] / 8.0 / mask_total
+    grad_norm = jnp.sqrt(numbers[0, 0])
+    vector_grad = gather_eight(vector_part, 8, 40_000_000).reshape(padded, width)[:rows]
     clip_scale = CLIP / jnp.maximum(grad_norm, CLIP)
     count_step = step_count[0].astype(F32)
     fix_one = 1.0 - BETA_ONE**count_step

time: 1790 us -> 1410 us (0.79)
  Pallas kernels: 500 us -> 773 us
  local copies, waits for them, and re-layouts: 363 us -> 130 us
  waiting for transfers between devices: 392 us -> 180 us
  blocking collectives: 162 us -> 0 us
  matrix products: 156 us -> 93.1 us
  starting transfers between devices: 53.1 us -> 76.6 us
    ppermute x48 -> x36, waiting for transfers between devices: 392 us -> 169 us  [send(): return plain(lax.ppermute(plain(block), axis, ring))]
    pallas_call x9 -> x11, Pallas kernels: 200 us -> 325 us  [gather_eight(): pl.pallas_call(gather_kernel, out_shape=jax.ShapeDtypeStruct((8,) + x.sha...]
    psum x3 -> x0, blocking collectives: 113 us -> none  [the longest x1 38.5 us: body(): mask_total = lax.psum(jnp.sum(masked).astype(F32), DP)]
    pallas_call x0 -> x8, Pallas kernels: none -> 89.1 us  [the longest x6 70.2 us: weight_grad(): pl.pallas_call(partial(grad_kernel, base is not None), out_shape=(jax.Sha...]
    dot_general x25 -> x18, matrix products: 147 us -> 82.6 us  [dot(): return lax.dot_general(x, y, (dims, ((), ())), preferred_element_type=F32)]
    another operation x8 -> x4, local copies, waits for them, and re-layouts: 61.4 us -> 2.07 us
    pallas_call x8 -> x9, Pallas kernels: 300 us -> 359 us  [scatter_eight(): pl.pallas_call(scatter_kernel, out_shape=jax.ShapeDtypeStruct(shape, kind...]
    all_gather x2 -> x0, blocking collectives: 49.2 us -> none  [the longest x1 42 us: body(): group_codes = lax.all_gather(image_codes, QX).reshape(-1)]
  transfers between devices with their start and end apart: 50 -> 43, of which waited for: 23 -> 12; matrix products, arithmetic and copies ran while one was open for 22% -> 16% of each run, Pallas kernels for 8% -> 38%
where the time goes in v1:
time: 1410 us; the launch traced here: 1400 us
  Pallas kernels  773 us (55%)
  waiting for transfers between devices  180 us (13%)
  local copies, waits for them, and re-layouts  130 us (9%)
  other arithmetic  121 us (9%)
  matrix products  93.1 us (7%)
  starting transfers between devices  76.6 us (5%)
  between operations  27.2 us (2%)
    pallas_call x9, Pallas kernels, scatter_eight(): pl.pallas_call(scatter_kernel, out_shape=jax.ShapeDtypeStruct(shape, kind...  359 us
    pallas_call x11, Pallas kernels, gather_eight(): pl.pallas_call(gather_kernel, out_shape=jax.ShapeDtypeStruct((8,) + x.sha...  325 us
    ppermute x36, waiting for transfers between devices, send(): return plain(lax.ppermute(plain(block), axis, ring))  169 us
    dot_general x18, matrix products, dot(): return lax.dot_general(x, y, (dims, ((), ())), preferred_element_type=F32)  82.6 us
    pallas_call x6, Pallas kernels, weight_grad(): pl.pallas_call(partial(grad_kernel, base is not None), out_shape=(jax.Sha...  70.2 us
    ppermute x36, starting transfers between devices, send(): return plain(lax.ppermute(plain(block), axis, ring))  49.9 us
    unnamed x324, local copies, waits for them, and re-layouts  48.1 us
    dynamic_update_slice x23, local copies, waits for them, and re-layouts, put(): return lax.dynamic_update_slice(full, piece, start)  34.2 us
  transfers between devices with their start and end apart: 43, of which 12 were waited for; matrix products, arithmetic and copies ran while one was open for 16% of the time, Pallas kernels for 38%

profile of v1, /device:TPU:0, one launch (start us, length us, event | category | flops | bytes accessed | tf_op | source)
XLA Modules:
  0.0 1401.2 jit_solution(17083625916797885136)
XLA Ops:
  24.6 41.1 %shard_map.425 = s32[8,2,8,128]{3,2,1,0:T(8,128)} custom-call(s32[2,8,128]{2,1,0:T(8,128)} %pad_bitcast_fusion.x_ref), custom_call_target="tpu_custom_call" | custom-call | bytes 20000000 | tf_op jit(solution)/shard_map/pallas_call | solution.py:118
  88.2 17.3 %collective-permute-done.6 = bf16[2,1,1,64,2048]{4,3,2,1,0:T(8,128)(2,1)} collective-permute-done((bf16[2,1,1,64,2048]{4,3,2,1,0:T(8,128)(2,1)}, bf16[2,1,1,64,2048]{4,3,2,1,0:T(8,128)(2,1)}, u32[]{:S(2)}, u32[]{:S(2)}) %collective-permute-start.6) | collective-permute-done | bytes 524320 | tf_op jit(solution)/shard_map/ppermute | solution.py:296
  119.0 4.9 fusion.9
  123.9 41.5 %shard_map.426 = bf16[2,64,2048]{2,1,0:T(8,128)(2,1)S(1)} custom-call(bf16[8,2,64,2048]{3,2,1,0:T(8,128)(2,1)S(1)} %bitcast.566), custom_call_target="tpu_custom_call" | custom-call | bytes 150000000 | tf_op jit(solution)/shard_map/pallas_call | solution.py:189
  176.5 54.5 %shard_map.427 = bf16[8,2,64,2048]{3,2,1,0:T(8,128)(2,1)} custom-call(bf16[2,64,2048]{2,1,0:T(8,128)(2,1)} %bitcast.646), custom_call_target="tpu_custom_call" | custom-call | bytes 80000000 | tf_op jit(solution)/shard_map/pallas_call | solution.py:118
  250.7 39.7 %shard_map.428 = f32[2,64,2048]{2,1,0:T(8,128)S(1)} custom-call(f32[8,2,64,2048]{3,2,1,0:T(8,128)S(1)} %bitcast.559), custom_call_target="tpu_custom_call" | custom-call | bytes 150000000 | tf_op jit(solution)/shard_map/pallas_call | solution.py:189
  295.6 59.0 %shard_map.429 = bf16[8,2,64,2048]{3,2,1,0:T(8,128)(2,1)} custom-call(bf16[2,64,2048]{2,1,0:T(8,128)(2,1)} %bitcast.647), custom_call_target="tpu_custom_call" | custom-call | bytes 80000000 | tf_op jit(solution)/shard_map/pallas_call | solution.py:118
  369.9 11.2 collective-permute-done.11
  392.1 41.8 %shard_map.430 = f32[2,64,2048]{2,1,0:T(8,128)S(1)} custom-call(f32[8,2,64,2048]{3,2,1,0:T(8,128)S(1)} %bitcast.558), custom_call_target="tpu_custom_call" | custom-call | bytes 150000000 | tf_op jit(solution)/shard_map/pallas_call | solution.py:189
  436.3 22.8 %shard_map.431 = bf16[8,2,64,2048]{3,2,1,0:T(8,128)(2,1)} custom-call(bf16[2,64,2048]{2,1,0:T(8,128)(2,1)} %bitcast.648), custom_call_target="tpu_custom_call" | custom-call | bytes 80000000 | tf_op jit(solution)/shard_map/pallas_call | solution.py:118
  469.0 8.9 multiply_convert_fusion.1
  477.9 6.9 collective-permute-done.17
  491.4 39.0 %shard_map.432 = f32[2,64,2048]{2,1,0:T(8,128)S(1)} custom-call(f32[8,2,64,2048]{3,2,1,0:T(8,128)S(1)} %fusion.191.p_ref), custom_call_target="tpu_custom_call" | custom-call | bytes 150000000 | tf_op jit(solution)/shard_map/pallas_call | solution.py:189
  532.7 22.0 %shard_map.433 = bf16[8,2,64,2048]{3,2,1,0:T(8,128)(2,1)} custom-call(bf16[2,64,2048]{2,1,0:T(8,128)(2,1)} %bitcast.649), custom_call_target="tpu_custom_call" | custom-call | bytes 80000000 | tf_op jit(solution)/shard_map/pallas_call | solution.py:118
  554.8 7.9 fusion.188
  565.4 8.4 shard_map.434
  597.8 39.0 %shard_map.435 = f32[2,64,2048]{2,1,0:T(8,128)S(1)} custom-call(f32[8,2,64,2048]{3,2,1,0:T(8,128)S(1)} %fusion.192.p_ref), custom_call_target="tpu_custom_call" | custom-call | bytes 150000000 | tf_op jit(solution)/shard_map/pallas_call | solution.py:189
  638.5 9.0 shard_map.439.refs_0_
  652.8 22.0 %shard_map.436 = bf16[8,2,64,2048]{3,2,1,0:T(8,128)(2,1)} custom-call(bf16[2,64,2048]{2,1,0:T(8,128)(2,1)} %bitcast.640), custom_call_target="tpu_custom_call" | custom-call | bytes 80000000 | tf_op jit(solution)/shard_map/pallas_call | solution.py:118
  676.4 10.5 shard_map.442
  686.9 8.5 fusion.6.right_ref
  695.4 14.5 %shard_map.437 = (f32[8,128,1024]{2,1,0:T(8,128)}, bf16[1,8,128,1024]{3,2,1,0:T(8,128)(2,1)}) custom-call(s32[1]{0:T(128)} %bitcast.d_ref, bf16[1024,2048]{1,0:T(8,128)(2,1)} %bitcast.607, bf16[1024,1024]{1,0:T(8,128)(2,1)S(1)} %fusion.6.right_ref), custom_call_target="tpu_custom_call" | custom-call | flops 4294967296 | bytes 14680064 | tf_op jit(solution)/shard_map/pallas_call | solution.py:379
  709.9 4.6 fusion.193
  714.5 39.7 %shard_map.438 = f32[2,64,2048]{2,1,0:T(8,128)S(1)} custom-call(f32[8,2,64,2048]{3,2,1,0:T(8,128)S(1)} %bitcast.563), custom_call_target="tpu_custom_call" | custom-call | bytes 150000000 | tf_op jit(solution)/shard_map/pallas_call | solution.py:189
  761.5 21.8 %shard_map.440 = bf16[8,2,64,2048]{3,2,1,0:T(8,128)(2,1)} custom-call(bf16[2,64,2048]{2,1,0:T(8,128)(2,1)} %bitcast.639), custom_call_target="tpu_custom_call" | custom-call | bytes 80000000 | tf_op jit(solution)/shard_map/pallas_call | solution.py:118
  793.0 8.9 shard_map.441
  802.7 11.5 shard_map.447
  818.0 18.3 %collective-permute-done.20 = bf16[2,256,2048]{2,1,0:T(8,128)(2,1)} collective-permute-done((bf16[2,256,2048]{2,1,0:T(8,128)(2,1)}, bf16[2,256,2048]{2,1,0:T(8,128)(2,1)}, u32[]{:S(2)}, u32[]{:S(2)}) %collective-permute-start.20) | collective-permute-done | bytes 2097184 | tf_op jit(solution)/shard_map/ppermute | solution.py:296
  836.3 39.1 %shard_map.443 = f32[2,64,2048]{2,1,0:T(8,128)S(1)} custom-call(f32[8,2,64,2048]{3,2,1,0:T(8,128)S(1)} %bitcast.557), custom_call_target="tpu_custom_call" | custom-call | bytes 150000000 | tf_op jit(solution)/shard_map/pallas_call | solution.py:189
  881.3 21.7 %shard_map.444 = bf16[8,2,64,2048]{3,2,1,0:T(8,128)(2,1)} custom-call(bf16[2,64,2048]{2,1,0:T(8,128)(2,1)} %bitcast.638), custom_call_target="tpu_custom_call" | custom-call | bytes 80000000 | tf_op jit(solution)/shard_map/pallas_call | solution.py:118
  921.3 9.1 fusion.153
  950.0 76.5 %collective-permute-done.30 = bf16[4,256,512]{2,1,0:T(8,128)(2,1)S(1)} collective-permute-done((bf16[4,256,512]{2,1,0:T(8,128)(2,1)S(1)}, bf16[4,256,512]{2,1,0:T(8,128)(2,1)S(1)}, u32[]{:S(2)}, u32[]{:S(2)}) %collective-permute-start.30) | collective-permute-done | bytes 1048608 | tf_op jit(solution)/shard_map/ppermute | solution.py:296
  1039.3 13.5 shard_map.445
  1053.6 4.7 multiply_reduce_fusion
  1058.4 69.1 %shard_map.446 = f32[2,64,2048]{2,1,0:T(8,128)S(1)} custom-call(f32[8,2,64,2048]{3,2,1,0:T(8,128)S(1)} %bitcast.562), custom_call_target="tpu_custom_call" | custom-call | bytes 150000000 | tf_op jit(solution)/shard_map/pallas_call | solution.py:189
  1132.1 21.9 %shard_map.448 = bf16[8,2,64,2048]{3,2,1,0:T(8,128)(2,1)} custom-call(bf16[2,64,2048]{2,1,0:T(8,128)(2,1)} %bitcast.645), custom_call_target="tpu_custom_call" | custom-call | bytes 80000000 | tf_op jit(solution)/shard_map/pallas_call | solution.py:118
  1154.1 11.3 shard_map.449
  1169.3 9.7 shard_map.450
  1202.3 14.4 %collective-permute-done.35 = f32[2,8,2304]{2,1,0:T(8,128)S(1)} collective-permute-done((f32[2,8,2304]{2,1,0:T(8,128)S(1)}, f32[2,8,2304]{2,1,0:T(8,128)S(1)}, u32[]{:S(2)}, u32[]{:S(2)}) %collective-permute-start.35) | collective-permute-done | bytes 147488 | tf_op jit(solution)/shard_map/ppermute | solution.py:296
  1217.9 30.3 %shard_map.452 = f32[8,2,8,2304]{3,2,1,0:T(8,128)} custom-call(f32[2,8,2304]{2,1,0:T(8,128)} %get-tuple-element.135.x_ref), custom_call_target="tpu_custom_call" | custom-call | bytes 40000000 | tf_op jit(solution)/shard_map/pallas_call | solution.py:118
  1263.1 6.2 collective-permute-start.26
  1278.4 4.7 all-to-all-start.3
  1299.5 16.3 %collective-permute-done.26 = bf16[1,256,2048]{2,1,0:T(8,128)(2,1)} collective-permute-done((bf16[1,256,2048]{2,1,0:T(8,128)(2,1)}, bf16[1,256,2048]{2,1,0:T(8,128)(2,1)}, u32[]{:S(2)}, u32[]{:S(2)}) %collective-permute-start.26) | collective-permute-done | bytes 1048608 | tf_op jit(solution)/shard_map/ppermute | solution.py:296
  1319.8 11.1 all-to-all-done.3
  1346.7 10.0 shard_map.451
  1360.2 6.9 multiply_subtract_fusion.1
  1367.1 5.4 multiply_subtract_fusion.2
  1385.8 5.9 multiply_subtract_fusion
  (617 shorter events, 351.2 us)
Async XLA Ops:
  10.0 70.0 %collective-permute-start = (bf16[1,1,256,2048]{3,2,1,0:T(8,128)(2,1)}, bf16[1,1,256,2048]{3,2,1,0:T(8,128)(2,1)}, u32[]{:S(2)}, u32[]{:S(2)}) collective-permute-start(bf16[1,1,256,2048]{3,2,1,0:T(8,128)(2,1)} %get-tuple-element.160), channel_id=1, source_target_pairs={{0,16},{16,0},{1,17},{17,1},{2,18},{18,2},{3,19},{19,3},{4,20},{20... | collective-permute-start | bytes 3145736 | tf_op jit(solution)/shard_map/ppermute | solution.py:296
  14.1 71.8 %collective-permute-start.1 = (bf16[1,1,256,2048]{3,2,1,0:T(8,128)(2,1)}, bf16[1,1,256,2048]{3,2,1,0:T(8,128)(2,1)}, u32[]{:S(2)}, u32[]{:S(2)}) collective-permute-start(bf16[1,1,256,2048]{3,2,1,0:T(8,128)(2,1)} %get-tuple-element.160), channel_id=1, source_target_pairs={{0,2},{2,0},{1,3},{3,1},{4,6},{6,4},{5,7},{7,5},{8,10},{10,8},{9,1... | collective-permute-start | bytes 3145736 | tf_op jit(solution)/shard_map/ppermute | solution.py:296
  18.9 87.8 %all-to-all-start = ((bf16[4,128,1024]{2,1,0:T(8,128)(2,1)}), bf16[4,128,1024]{2,1,0:T(8,128)(2,1)}, u32[]{:S(2)}, u32[]{:S(2)}) async-start(bf16[4,128,1024]{2,1,0:T(8,128)(2,1)} %reshape.774), calls=%async_computation | async-start | bytes 2097152 | tf_op jit(solution)/shard_map/all_to_all | solution.py:445
  23.2 358.9 %all-gather.3.cloned.1.call-start = ((), (), s32[]{:S(2)}) async-start(), calls=%async_computation.6 | async-start | bytes 2621440 | tf_op jit(solution)/shard_map/all_gather | solution.py:555
  70.9 94.5 %copy-start.135 = (pred[128]{0:T(512)(128)(4,1)}, pred[128]{0:T(512)(128)(4,1)S(1)}, u32[]{:S(2)}) copy-start(pred[128]{0:T(512)(128)(4,1)S(1)} %compare_bitcast_fusion) | copy-start | bytes 388
  80.0 86.0 %copy-start.106 = (f32[1,2048]{1,0:T(1,128)}, f32[1,2048]{1,0:T(1,128)S(1)}, u32[]{:S(2)}) copy-start(f32[1,2048]{1,0:T(1,128)S(1)} %get-tuple-element.219) | copy-start | bytes 24580
  80.1 25.5 %collective-permute-start.6 = (bf16[2,1,1,64,2048]{4,3,2,1,0:T(8,128)(2,1)}, bf16[2,1,1,64,2048]{4,3,2,1,0:T(8,128)(2,1)}, u32[]{:S(2)}, u32[]{:S(2)}) collective-permute-start(bf16[2,1,1,64,2048]{4,3,2,1,0:T(8,128)(2,1)} %convert_bitcast_fusion.2), channel_id=1, source_target_pairs={{0,16},{16,0},{1,17},{17,1},{2,18},{18,2},{3,19},{19,3},{4,20},{20... | collective-permute-start | bytes 1572872 | tf_op jit(solution)/shard_map/ppermute | solution.py:296
  80.1 26.6 %collective-permute-start.7 = (bf16[2,1,1,64,2048]{4,3,2,1,0:T(8,128)(2,1)}, bf16[2,1,1,64,2048]{4,3,2,1,0:T(8,128)(2,1)S(1)}, u32[]{:S(2)}, u32[]{:S(2)}) collective-permute-start(bf16[2,1,1,64,2048]{4,3,2,1,0:T(8,128)(2,1)} %convert_bitcast_fusion.2), channel_id=1, source_target_pairs={{0,2},{2,0},{1,3},{3,1},{4,6},{6,4},{5,7},{7,5},{8,10},{10,8},{9,1... | collective-permute-start | bytes 1572872 | tf_op jit(solution)/shard_map/ppermute | solution.py:296
  80.5 37.2 %collective-permute-start.2 = (bf16[1,1,256,2048]{3,2,1,0:T(8,128)(2,1)}, bf16[1,1,256,2048]{3,2,1,0:T(8,128)(2,1)}, u32[]{:S(2)}, u32[]{:S(2)}) collective-permute-start(bf16[1,1,256,2048]{3,2,1,0:T(8,128)(2,1)} %collective-permute-done), channel_id=1, source_target_pairs={{0,2},{2,0},{1,3},{3,1},{4,6},{6,4},{5,7},{7,5},{8,10},{10,8},{9,1... | collective-permute-start | bytes 3145736 | tf_op jit(solution)/shard_map/ppermute | solution.py:296
  105.5 63.3 %collective-permute-start.8 = (bf16[2,1,1,64,2048]{4,3,2,1,0:T(8,128)(2,1)}, bf16[2,1,1,64,2048]{4,3,2,1,0:T(8,128)(2,1)}, u32[]{:S(2)}, u32[]{:S(2)}) collective-permute-start(bf16[2,1,1,64,2048]{4,3,2,1,0:T(8,128)(2,1)} %collective-permute-done.6), channel_id=1, source_target_pairs={{0,2},{2,0},{1,3},{3,1},{4,6},{6,4},{5,7},{7,5},{8,10},{10,8},{9,1... | collective-permute-start | bytes 1572872 | tf_op jit(solution)/shard_map/ppermute | solution.py:296
  106.8 64.6 %all-to-all-start.1 = ((bf16[4,256,512]{2,1,0:T(8,128)(2,1)}), bf16[4,256,512]{2,1,0:T(8,128)(2,1)}, u32[]{:S(2)}, u32[]{:S(2)}) async-start(bf16[4,256,512]{2,1,0:T(8,128)(2,1)} %reshape.785), calls=%async_computation.1 | async-start | bytes 2097152 | tf_op jit(solution)/shard_map/all_to_all | solution.py:445
  111.0 56.1 %collective-permute-start.3 = (bf16[1,4,1,128,1024]{4,3,2,1,0:T(8,128)(2,1)}, bf16[1,4,1,128,1024]{4,3,2,1,0:T(8,128)(2,1)}, u32[]{:S(2)}, u32[]{:S(2)}) collective-permute-start(bf16[1,4,1,128,1024]{4,3,2,1,0:T(8,128)(2,1)} %bitcast.15), channel_id=1, source_target_pairs={{0,16},{16,0},{1,17},{17,1},{2,18},{18,2},{3,19},{19,3},{4,20},{20... | collective-permute-start | bytes 3145736 | tf_op jit(solution)/shard_map/ppermute | solution.py:296
  111.1 126.3 %collective-permute-start.4 = (bf16[1,4,1,128,1024]{4,3,2,1,0:T(8,128)(2,1)}, bf16[1,4,1,128,1024]{4,3,2,1,0:T(8,128)(2,1)}, u32[]{:S(2)}, u32[]{:S(2)}) collective-permute-start(bf16[1,4,1,128,1024]{4,3,2,1,0:T(8,128)(2,1)} %bitcast.15), channel_id=1, source_target_pairs={{0,2},{2,0},{1,3},{3,1},{4,6},{6,4},{5,7},{7,5},{8,10},{10,8},{9,1... | collective-permute-start | bytes 3145736 | tf_op jit(solution)/shard_map/ppermute | solution.py:296
  165.7 124.7 %copy-start.6 = (f32[128,2048]{1,0:T(8,128)}, f32[128,2048]{1,0:T(8,128)S(1)}, u32[]{:S(2)}) copy-start(f32[128,2048]{1,0:T(8,128)S(1)} %get-tuple-element.158) | copy-start | bytes 3145732
  167.1 71.7 %collective-permute-start.5 = (bf16[1,4,1,128,1024]{4,3,2,1,0:T(8,128)(2,1)}, bf16[1,4,1,128,1024]{4,3,2,1,0:T(8,128)(2,1)S(1)}, u32[]{:S(2)}, u32[]{:S(2)}) collective-permute-start(bf16[1,4,1,128,1024]{4,3,2,1,0:T(8,128)(2,1)} %collective-permute-done.3), channel_id=1, source_target_pairs={{0,2},{2,0},{1,3},{3,1},{4,6},{6,4},{5,7},{7,5},{8,10},{10,8},{9,1... | collective-permute-start | bytes 3145736 | tf_op jit(solution)/shard_map/ppermute | solution.py:296
  171.4 121.5 %all-to-all-start.2 = ((bf16[4,128,1024]{2,1,0:T(8,128)(2,1)}), bf16[4,128,1024]{2,1,0:T(8,128)(2,1)}, u32[]{:S(2)}, u32[]{:S(2)}) async-start(bf16[4,128,1024]{2,1,0:T(8,128)(2,1)} %reshape.795), calls=%async_computation.2 | async-start | bytes 2097152 | tf_op jit(solution)/shard_map/all_to_all | solution.py:445
  175.9 119.7 %collective-permute-start.9 = (bf16[1,4,1,256,512]{4,3,2,1,0:T(8,128)(2,1)}, bf16[1,4,1,256,512]{4,3,2,1,0:T(8,128)(2,1)}, u32[]{:S(2)}, u32[]{:S(2)}) collective-permute-start(bf16[1,4,1,256,512]{4,3,2,1,0:T(8,128)(2,1)} %bitcast.31), channel_id=1, source_target_pairs={{0,16},{16,0},{1,17},{17,1},{2,18},{18,2},{3,19},{19,3},{4,20},{20... | collective-permute-start | bytes 3145736 | tf_op jit(solution)/shard_map/ppermute | solution.py:296
  176.0 184.5 %collective-permute-start.10 = (bf16[1,4,1,256,512]{4,3,2,1,0:T(8,128)(2,1)}, bf16[1,4,1,256,512]{4,3,2,1,0:T(8,128)(2,1)}, u32[]{:S(2)}, u32[]{:S(2)}) collective-permute-start(bf16[1,4,1,256,512]{4,3,2,1,0:T(8,128)(2,1)} %bitcast.31), channel_id=1, source_target_pairs={{0,2},{2,0},{1,3},{3,1},{4,6},{6,4},{5,7},{7,5},{8,10},{10,8},{9,1... | collective-permute-start | bytes 3145736 | tf_op jit(solution)/shard_map/ppermute | solution.py:296
  290.6 143.3 %copy-start.8 = (f32[128,2048]{1,0:T(8,128)}, f32[128,2048]{1,0:T(8,128)S(1)}, u32[]{:S(2)}) copy-start(f32[128,2048]{1,0:T(8,128)S(1)} %get-tuple-element.156) | copy-start | bytes 3145732
  292.0 144.4 %collective-permute-start.13 = (bf16[1,1,256,2048]{3,2,1,0:T(8,128)(2,1)}, bf16[1,1,256,2048]{3,2,1,0:T(8,128)(2,1)}, u32[]{:S(2)}, u32[]{:S(2)}) collective-permute-start(bf16[1,1,256,2048]{3,2,1,0:T(8,128)(2,1)} %convert_bitcast_fusion), channel_id=1, source_target_pairs={{0,16},{16,0},{1,17},{17,1},{2,18},{18,2},{3,19},{19,3},{4,20},{20... | collective-permute-start | bytes 3145736 | tf_op jit(solution)/shard_map/ppermute | solution.py:296
  292.1 174.3 %collective-permute-start.16 = (bf16[1,1,256,2048]{3,2,1,0:T(8,128)(2,1)}, bf16[1,1,256,2048]{3,2,1,0:T(8,128)(2,1)}, u32[]{:S(2)}, u32[]{:S(2)}) collective-permute-start(bf16[1,1,256,2048]{3,2,1,0:T(8,128)(2,1)} %convert_bitcast_fusion), channel_id=1, source_target_pairs={{0,2},{2,0},{1,3},{3,1},{4,6},{6,4},{5,7},{7,5},{8,10},{10,8},{9,1... | collective-permute-start | bytes 3145736 | tf_op jit(solution)/shard_map/ppermute | solution.py:296
  292.9 99.2 %collective-permute-start.12 = (bf16[1,4,1,128,1024]{4,3,2,1,0:T(8,128)(2,1)}, bf16[1,4,1,128,1024]{4,3,2,1,0:T(8,128)(2,1)}, u32[]{:S(2)}, u32[]{:S(2)}) collective-permute-start(bf16[1,4,1,128,1024]{4,3,2,1,0:T(8,128)(2,1)} %bitcast.43), channel_id=1, source_target_pairs={{0,16},{16,0},{1,17},{17,1},{2,18},{18,2},{3,19},{19,3},{4,20},{20... | collective-permute-start | bytes 3145736 | tf_op jit(solution)/shard_map/ppermute | solution.py:296
  354.7 26.4 %collective-permute-start.11 = (bf16[1,4,1,256,512]{4,3,2,1,0:T(8,128)(2,1)}, bf16[1,4,1,256,512]{4,3,2,1,0:T(8,128)(2,1)S(1)}, u32[]{:S(2)}, u32[]{:S(2)}) collective-permute-start(bf16[1,4,1,256,512]{4,3,2,1,0:T(8,128)(2,1)} %collective-permute-done.9), channel_id=1, source_target_pairs={{0,2},{2,0},{1,3},{3,1},{4,6},{6,4},{5,7},{7,5},{8,10},{10,8},{9,1... | collective-permute-start | bytes 3145736 | tf_op jit(solution)/shard_map/ppermute | solution.py:296
  360.4 102.4 %collective-permute-start.14 = (bf16[1,4,1,128,1024]{4,3,2,1,0:T(8,128)(2,1)}, bf16[1,4,1,128,1024]{4,3,2,1,0:T(8,128)(2,1)}, u32[]{:S(2)}, u32[]{:S(2)}) collective-permute-start(bf16[1,4,1,128,1024]{4,3,2,1,0:T(8,128)(2,1)} %bitcast.43), channel_id=1, source_target_pairs={{0,2},{2,0},{1,3},{3,1},{4,6},{6,4},{5,7},{7,5},{8,10},{10,8},{9,1... | collective-permute-start | bytes 3145736 | tf_op jit(solution)/shard_map/ppermute | solution.py:296
  434.2 96.3 %copy-start.10 = (f32[128,2048]{1,0:T(8,128)}, f32[128,2048]{1,0:T(8,128)S(1)}, u32[]{:S(2)}) copy-start(f32[128,2048]{1,0:T(8,128)S(1)} %get-tuple-element.154) | copy-start | bytes 3145732
  434.5 33.4 %collective-permute-start.15 = (bf16[1,4,1,128,1024]{4,3,2,1,0:T(8,128)(2,1)}, bf16[1,4,1,128,1024]{4,3,2,1,0:T(8,128)(2,1)S(1)}, u32[]{:S(2)}, u32[]{:S(2)}) collective-permute-start(bf16[1,4,1,128,1024]{4,3,2,1,0:T(8,128)(2,1)} %collective-permute-done.12), channel_id=1, source_target_pairs={{0,2},{2,0},{1,3},{3,1},{4,6},{6,4},{5,7},{7,5},{8,10},{10,8},{9,1... | collective-permute-start | bytes 3145736 | tf_op jit(solution)/shard_map/ppermute | solution.py:296
  459.1 25.7 %collective-permute-start.17 = (bf16[1,1,256,2048]{3,2,1,0:T(8,128)(2,1)}, bf16[1,1,256,2048]{3,2,1,0:T(8,128)(2,1)S(1)}, u32[]{:S(2)}, u32[]{:S(2)}) collective-permute-start(bf16[1,1,256,2048]{3,2,1,0:T(8,128)(2,1)} %collective-permute-done.13), channel_id=1, source_target_pairs={{0,2},{2,0},{1,3},{3,1},{4,6},{6,4},{5,7},{7,5},{8,10},{10,8},{9,1... | collective-permute-start | bytes 3145736 | tf_op jit(solution)/shard_map/ppermute | solution.py:296
  577.5 4.6 collective-permute-start.18
  582.7 4.4 collective-permute-start.19
  787.5 48.8 %collective-permute-start.20 = (bf16[2,256,2048]{2,1,0:T(8,128)(2,1)}, bf16[2,256,2048]{2,1,0:T(8,128)(2,1)}, u32[]{:S(2)}, u32[]{:S(2)}) collective-permute-start(bf16[2,256,2048]{2,1,0:T(8,128)(2,1)} %bitcast.81), channel_id=1, source_target_pairs={{0,2},{2,0},{1,3},{3,1},{4,6},{6,4},{5,7},{7,5},{8,10},{10,8},{9,1... | collective-permute-start | bytes 6291464 | tf_op jit(solution)/shard_map/ppermute | solution.py:296
  788.8 92.4 %collective-permute-start.21 = (bf16[8,128,1024]{2,1,0:T(8,128)(2,1)}, bf16[8,128,1024]{2,1,0:T(8,128)(2,1)}, u32[]{:S(2)}, u32[]{:S(2)}) collective-permute-start(bf16[8,128,1024]{2,1,0:T(8,128)(2,1)} %bitcast.84), channel_id=1, source_target_pairs={{0,2},{2,0},{1,3},{3,1},{4,6},{6,4},{5,7},{7,5},{8,10},{10,8},{9,1... | collective-permute-start | bytes 6291464 | tf_op jit(solution)/shard_map/ppermute | solution.py:296
  801.9 128.6 %collective-permute-start.23 = (bf16[8,256,512]{2,1,0:T(8,128)(2,1)}, bf16[8,256,512]{2,1,0:T(8,128)(2,1)}, u32[]{:S(2)}, u32[]{:S(2)}) collective-permute-start(bf16[8,256,512]{2,1,0:T(8,128)(2,1)} %bitcast.92), channel_id=1, source_target_pairs={{0,2},{2,0},{1,3},{3,1},{4,6},{6,4},{5,7},{7,5},{8,10},{10,8},{9,1... | collective-permute-start | bytes 6291464 | tf_op jit(solution)/shard_map/ppermute | solution.py:296
  814.2 317.9 %collective-permute-start.24 = (bf16[8,128,256]{2,1,0:T(8,128)(2,1)}, bf16[8,128,256]{2,1,0:T(8,128)(2,1)}, u32[]{:S(2)}, u32[]{:S(2)}) collective-permute-start(bf16[8,128,256]{2,1,0:T(8,128)(2,1)} %bitcast.95), channel_id=1, source_target_pairs={{0,2},{2,0},{1,3},{3,1},{4,6},{6,4},{5,7},{7,5},{8,10},{10,8},{9,1... | collective-permute-start | bytes 1572872 | tf_op jit(solution)/shard_map/ppermute | solution.py:296
  932.2 94.2 %collective-permute-start.30 = (bf16[4,256,512]{2,1,0:T(8,128)(2,1)S(1)}, bf16[4,256,512]{2,1,0:T(8,128)(2,1)S(1)}, u32[]{:S(2)}, u32[]{:S(2)}) collective-permute-start(bf16[4,256,512]{2,1,0:T(8,128)(2,1)S(1)} %fusion.29), channel_id=1, source_target_pairs={{0,16},{16,0},{1,17},{17,1},{2,18},{18,2},{3,19},{19,3},{4,20},{20... | collective-permute-start | bytes 3145736 | tf_op jit(solution)/shard_map/ppermute | solution.py:296
  940.2 113.4 %collective-permute-start.22 = (bf16[1,256,2048]{2,1,0:T(8,128)(2,1)}, bf16[1,256,2048]{2,1,0:T(8,128)(2,1)}, u32[]{:S(2)}, u32[]{:S(2)}) collective-permute-start(bf16[1,256,2048]{2,1,0:T(8,128)(2,1)} %add_convert_fusion.3), channel_id=1, source_target_pairs={{0,16},{16,0},{1,17},{17,1},{2,18},{18,2},{3,19},{19,3},{4,20},{20... | collective-permute-start | bytes 3145736 | tf_op jit(solution)/shard_map/ppermute | solution.py:296
  943.8 238.9 %collective-permute-start.33 = (bf16[4,128,1024]{2,1,0:T(8,128)(2,1)}, bf16[4,128,1024]{2,1,0:T(8,128)(2,1)}, u32[]{:S(2)}, u32[]{:S(2)}) collective-permute-start(bf16[4,128,1024]{2,1,0:T(8,128)(2,1)} %fusion.30), channel_id=1, source_target_pairs={{0,16},{16,0},{1,17},{17,1},{2,18},{18,2},{3,19},{19,3},{4,20},{20... | collective-permute-start | bytes 3145736 | tf_op jit(solution)/shard_map/ppermute | solution.py:296
  1029.4 157.7 %all-to-all-start.4 = ((f32[4,256,512]{2,1,0:T(8,128)}), f32[4,256,512]{2,1,0:T(8,128)}, u32[]{:S(2)}, u32[]{:S(2)}) async-start(f32[4,256,512]{2,1,0:T(8,128)} %bitcast_add_fusion.1), calls=%async_computation.4 | async-start | bytes 4194304 | tf_op jit(solution)/shard_map/all_to_all | solution.py:445
  1036.7 154.9 %collective-permute-start.31 = (bf16[2,2,64,2048]{3,2,1,0:T(8,128)(2,1)}, bf16[2,2,64,2048]{3,2,1,0:T(8,128)(2,1)}, u32[]{:S(2)}, u32[]{:S(2)}) collective-permute-start(bf16[2,2,64,2048]{3,2,1,0:T(8,128)(2,1)} %fusion.31), channel_id=1, source_target_pairs={{0,2},{2,0},{1,3},{3,1},{4,6},{6,4},{5,7},{7,5},{8,10},{10,8},{9,1... | collective-permute-start | bytes 3145736 | tf_op jit(solution)/shard_map/ppermute | solution.py:296
  1052.8 143.9 %collective-permute-start.27 = (bf16[8,128,768]{2,1,0:T(8,128)(2,1)}, bf16[8,128,768]{2,1,0:T(8,128)(2,1)}, u32[]{:S(2)}, u32[]{:S(2)}) collective-permute-start(bf16[8,128,768]{2,1,0:T(8,128)(2,1)} %bitcast.100), channel_id=1, source_target_pairs={{0,2},{2,0},{1,3},{3,1},{4,6},{6,4},{5,7},{7,5},{8,10},{10,8},{9,1... | collective-permute-start | bytes 4718600 | tf_op jit(solution)/shard_map/ppermute | solution.py:296
  1165.4 93.9 %collective-permute-start.25 = (bf16[2,256,2048]{2,1,0:T(8,128)(2,1)}, bf16[2,256,2048]{2,1,0:T(8,128)(2,1)}, u32[]{:S(2)}, u32[]{:S(2)}) collective-permute-start(bf16[2,256,2048]{2,1,0:T(8,128)(2,1)} %bitcast.98), channel_id=1, source_target_pairs={{0,2},{2,0},{1,3},{3,1},{4,6},{6,4},{5,7},{7,5},{8,10},{10,8},{9,1... | collective-permute-start | bytes 6291464 | tf_op jit(solution)/shard_map/ppermute | solution.py:296
  1179.0 21.0 %collective-permute-start.34 = (f32[2,8,2304]{2,1,0:T(8,128)S(1)}, f32[2,8,2304]{2,1,0:T(8,128)S(1)}, u32[]{:S(2)}, u32[]{:S(2)}) collective-permute-start(f32[2,8,2304]{2,1,0:T(8,128)S(1)} %shard_map.450), channel_id=1, source_target_pairs={{0,16},{16,0},{1,17},{17,1},{2,18},{18,2},{3,19},{19,3},{4,20},{20... | collective-permute-start | bytes 442376 | tf_op jit(solution)/shard_map/ppermute | solution.py:296
  1182.7 18.5 %collective-permute-start.29 = (bf16[4,128,256]{2,1,0:T(8,128)(2,1)S(1)}, bf16[4,128,256]{2,1,0:T(8,128)(2,1)S(1)}, u32[]{:S(2)}, u32[]{:S(2)}) collective-permute-start(bf16[4,128,256]{2,1,0:T(8,128)(2,1)S(1)} %fusion.53), channel_id=1, source_target_pairs={{0,16},{16,0},{1,17},{17,1},{2,18},{18,2},{3,19},{19,3},{4,20},{20... | collective-permute-start | bytes 786440 | tf_op jit(solution)/shard_map/ppermute | solution.py:296
  1187.1 91.3 %all-to-all-start.5 = ((f32[4,128,1024]{2,1,0:T(8,128)}), f32[4,128,1024]{2,1,0:T(8,128)}, u32[]{:S(2)}, u32[]{:S(2)}) async-start(f32[4,128,1024]{2,1,0:T(8,128)} %bitcast_add_fusion), calls=%async_computation.5 | async-start | bytes 4194304 | tf_op jit(solution)/shard_map/all_to_all | solution.py:445
  1194.1 57.3 %collective-permute-start.32 = (bf16[1,2,64,2048]{3,2,1,0:T(8,128)(2,1)}, bf16[1,2,64,2048]{3,2,1,0:T(8,128)(2,1)}, u32[]{:S(2)}, u32[]{:S(2)}) collective-permute-start(bf16[1,2,64,2048]{3,2,1,0:T(8,128)(2,1)} %fusion.35), channel_id=1, source_target_pairs={{0,16},{16,0},{1,17},{17,1},{2,18},{18,2},{3,19},{19,3},{4,20},{20... | collective-permute-start | bytes 1572872 | tf_op jit(solution)/shard_map/ppermute | solution.py:296
  1198.9 57.3 %collective-permute-start.28 = (bf16[4,128,768]{2,1,0:T(8,128)(2,1)}, bf16[4,128,768]{2,1,0:T(8,128)(2,1)S(1)}, u32[]{:S(2)}, u32[]{:S(2)}) collective-permute-start(bf16[4,128,768]{2,1,0:T(8,128)(2,1)} %fusion.50), channel_id=1, source_target_pairs={{0,16},{16,0},{1,17},{17,1},{2,18},{18,2},{3,19},{19,3},{4,20},{20... | collective-permute-start | bytes 2359304 | tf_op jit(solution)/shard_map/ppermute | solution.py:296
  1200.0 16.7 %collective-permute-start.35 = (f32[2,8,2304]{2,1,0:T(8,128)S(1)}, f32[2,8,2304]{2,1,0:T(8,128)S(1)}, u32[]{:S(2)}, u32[]{:S(2)}) collective-permute-start(f32[2,8,2304]{2,1,0:T(8,128)S(1)} %add.583), channel_id=1, source_target_pairs={{0,2},{2,0},{1,3},{3,1},{4,6},{6,4},{5,7},{7,5},{8,10},{10,8},{9,1... | collective-permute-start | bytes 442376 | tf_op jit(solution)/shard_map/ppermute | solution.py:296
  1263.1 52.7 %collective-permute-start.26 = (bf16[1,256,2048]{2,1,0:T(8,128)(2,1)}, bf16[1,256,2048]{2,1,0:T(8,128)(2,1)}, u32[]{:S(2)}, u32[]{:S(2)}) collective-permute-start(bf16[1,256,2048]{2,1,0:T(8,128)(2,1)} %add_convert_fusion.2), channel_id=1, source_target_pairs={{0,16},{16,0},{1,17},{17,1},{2,18},{18,2},{3,19},{19,3},{4,20},{20... | collective-permute-start | bytes 3145736 | tf_op jit(solution)/shard_map/ppermute | solution.py:296
  1278.4 52.5 %all-to-all-start.3 = ((f32[4,128,1024]{2,1,0:T(8,128)}), f32[4,128,1024]{2,1,0:T(8,128)}, u32[]{:S(2)}, u32[]{:S(2)}) async-start(f32[4,128,1024]{2,1,0:T(8,128)} %pad_maximum_fusion), calls=%async_computation.3 | async-start | bytes 4194304 | tf_op jit(solution)/shard_map/all_to_all | solution.py:445
  (146 other events, 1594.3 us)
Sparse Core Ops, SparseCore 0:
  25.6 60.4 all-gather.2

commit v2 on v1

v2 whole, which is shorter than its diff:
```python
from functools import partial

import jax
import jax.numpy as jnp
from jax import lax
from jax.experimental import pallas as pl
from jax.experimental.layout import Layout, with_layout_constraint
from jax.experimental.pallas import tpu as pltpu
from jax.sharding import Mesh, PartitionSpec as P

HD = 128
EPS_NORM = 1e-05
CLIP = 0.01
BETA_ONE = 0.9
BETA_TWO = 0.999
ADAM_EPS = 1e-08
DECAY = 0.01
RATE_MATRIX = 0.02
RATE_VECTOR = 0.2
SCALE = HD ** (-0.5)
F32 = jnp.float32
BF16 = jnp.bfloat16
WIRE = jnp.bfloat16

AX, BX, EX, DX, CX = "a", "b", "e", "d", "c"
DP = (AX, BX, EX, DX)
QX = (BX, EX)
MX = (AX, DX)
SWAP = [(0, 1), (1, 0)]
MESH = pl.DeviceIdType.MESH


def dot(x, y, dims):
    return lax.dot_general(x, y, (dims, ((), ())), preferred_element_type=F32)


def nn(x, y):
    return dot(x, y, ((1,), (0,)))


def nt(x, y):
    return dot(x, y, ((1,), (1,)))


def tn(x, y):
    return dot(x, y, ((0,), (0,)))


SHARE, RING, SWAP, EXCHANGE = range(4)
START, FAR, THROUGH = range(3)
GATHER, SCATTER = range(2)


class Here:
    def __init__(self, extent, send, recv, local):
        self.a, self.b, self.e, self.d, self.c = (
            lax.axis_index(name) for name in (AX, BX, EX, DX, CX)
        )
        self.extent = extent
        self.to_a, self.to_b, self.to_e, self.to_c = (
            {AX: 1 - self.a},
            {BX: 1 - self.b},
            {EX: 1 - self.e},
            {CX: 1 - self.c},
        )
        self.to_far = {BX: 1 - self.b, EX: 1 - self.e}
        self.to_d = [{DX: lax.rem(self.d + step, extent)} for step in range(1, extent)]
        self.send, self.recv, self.local = send, recv, local
        self.count = self.local_count = 0
        self.waits = []

    def greet(self, peers):
        barrier = pltpu.get_barrier_semaphore()
        for peer in peers:
            pl.semaphore_signal(barrier, inc=1, device_id=peer, device_id_type=MESH)
        pl.semaphore_wait(barrier, len(peers))

    def copy(self, source, target, peer, hold=False):
        made = pltpu.make_async_remote_copy(
            src_ref=source,
            dst_ref=target,
            send_sem=self.send.at[self.count],
            recv_sem=self.recv.at[self.count],
            device_id=peer,
            device_id_type=MESH,
        )
        self.count += 1
        made.start()
        if not hold:
            self.waits.append(made.wait_send)
        return made

    def late(self, made):
        self.waits.append(made.wait_recv)

    def keep(self, source, target):
        made = pltpu.make_async_copy(source, target, self.local.at[self.local_count])
        self.local_count += 1
        made.start()
        return made

    def finish(self):
        for wait in self.waits:
            wait()


def place(b, e, c):
    return (b * 2 + e) * 2 + c


def spot(array, mode, row, column, first, count):
    if mode == 0:
        return array.at[row, column, pl.ds(first, count)]
    if mode == 1:
        return array.at[row, pl.ds(first, count), column]
    return array.at[pl.ds(first, count), row, column]


def share_start(here, block, array, mode, first, count):
    source = block.at[pl.ds(first, count)]
    target = spot(array, mode, here.a, here.d, first, count)
    here.waits.append(here.keep(source, target).wait)
    across = here.copy(source, target, here.to_a)
    for peer in here.to_d:
        here.late(here.copy(source, target, peer))
    return across


def share_far(here, array, mode, first, count):
    block = spot(array, mode, 1 - here.a, here.d, first, count)
    for peer in here.to_d:
        here.late(here.copy(block, block, peer))


def exchange_start(here, pieces, out, width=0):
    mine = here.b * 2 + here.e
    peers = (
        (None, mine),
        (here.to_e, here.b * 2 + 1 - here.e),
        (here.to_b, (1 - here.b) * 2 + here.e),
        (here.to_far, (1 - here.b) * 2 + 1 - here.e),
    )
    started = []
    for peer, there in peers:
        if width:
            moves = []
            for k in range(pieces.shape[2] // width):
                column = pl.multiple_of((k % 2 * 4 + mine) * width, 128)
                target = out.at[k // 2, :, pl.ds(column, width)]
                moves.append((pieces.at[there, :, pl.ds(k * width, width)], target))
        else:
            moves = [(pieces.at[there], out.at[mine])]
        for source, target in moves:
            if peer is None:
                started.append(here.keep(source, target).wait)
            else:
                started.append(here.copy(source, target, peer).wait_recv)
    return started


def gather_start(here, x_ref, o_ref, cut):
    first, second = pl.ds(0, cut), pl.ds(cut, x_ref.shape[0] - cut)
    me = place(here.b, here.e, here.c)
    e_first = here.copy(x_ref.at[first], o_ref.at[me, first], here.to_e)
    b_first = here.copy(x_ref.at[second], o_ref.at[me, second], here.to_b)
    here.late(here.copy(x_ref, o_ref.at[me], here.to_c))
    e_second = here.copy(x_ref.at[second], o_ref.at[me, second], here.to_e)
    b_second = here.copy(x_ref.at[first], o_ref.at[me, first], here.to_b)
    here.waits.append(here.keep(x_ref, o_ref.at[me]).wait)
    return e_first, b_first, e_second, b_second


def gather_rest(here, o_ref, cut, started):
    first, second = pl.ds(0, cut), pl.ds(cut, o_ref.shape[1] - cut)
    e_first, b_first, e_second, b_second = started
    beside = place(here.b, 1 - here.e, here.c)
    across = place(1 - here.b, here.e, here.c)
    far = place(1 - here.b, 1 - here.e, here.c)

    def on(block, peer):
        return here.copy(block, block, peer)

    e_first.wait_recv()
    b_third = on(o_ref.at[beside, first], here.to_b)
    here.late(on(o_ref.at[beside, first], here.to_c))
    b_first.wait_recv()
    e_third = on(o_ref.at[across, second], here.to_e)
    here.late(on(o_ref.at[across, second], here.to_c))
    e_second.wait_recv()
    here.late(on(o_ref.at[beside, second], here.to_c))
    b_second.wait_recv()
    here.late(on(o_ref.at[across, first], here.to_c))
    b_third.wait_recv()
    here.late(on(o_ref.at[far, first], here.to_c))
    e_third.wait_recv()
    here.late(on(o_ref.at[far, second], here.to_c))


def scatter_start(here, p_ref, paired):
    b, e, c = here.b, here.e, here.c
    order = ((1 - b, 1 - e), (1 - b, e), (b, 1 - e), (b, e))
    return [
        here.copy(p_ref.at[place(bb, ee, 1 - c)], paired.at[k], here.to_c)
        for k, (bb, ee) in enumerate(order)
    ]


def scatter_rest(here, p_ref, o_ref, cut, pairs, paired, held, from_b, from_e, last_b, last_e):
    b, e, c = here.b, here.e, here.c
    first, second = pl.ds(0, cut), pl.ds(cut, o_ref.shape[0] - cut)
    pairs[0].wait_recv()
    held[0] = p_ref[place(1 - b, 1 - e, c)] + paired[0]
    e_first = here.copy(held.at[0, second], from_e.at[0], here.to_e, hold=True)
    b_first = here.copy(held.at[0, first], from_b.at[0], here.to_b, hold=True)
    pairs[2].wait_recv()
    held[2] = p_ref[place(b, 1 - e, c)] + paired[2]
    pairs[1].wait_recv()
    held[1] = p_ref[place(1 - b, e, c)] + paired[1]
    pairs[3].wait_recv()
    o_ref[...] = p_ref[place(b, e, c)] + paired[3]
    b_first.wait_send()
    b_second = here.copy(held.at[1, first], from_b.at[1], here.to_b)
    e_first.wait_send()
    e_second = here.copy(held.at[2, second], from_e.at[1], here.to_e)
    e_first.wait_recv()
    held[1, second] = held[1, second] + from_e[0]
    b_third = here.copy(held.at[1, second], last_b, here.to_b)
    b_first.wait_recv()
    held[2, first] = held[2, first] + from_b[0]
    e_third = here.copy(held.at[2, first], last_e, here.to_e)
    b_second.wait_recv()
    o_ref[first] = o_ref[first] + from_b[1]
    e_second.wait_recv()
    o_ref[second] = o_ref[second] + from_e[1]
    e_third.wait_recv()
    o_ref[first] = o_ref[first] + last_e[...]
    b_third.wait_recv()
    o_ref[second] = o_ref[second] + last_b[...]


def group_kernel(kind, cut, plan, extent, in_count, out_count, *refs):
    ins, outs = list(refs[:in_count]), list(refs[in_count : in_count + out_count])
    scratch = refs[in_count + out_count :]
    here = Here(extent, *scratch[:3])
    x_ref, o_ref = ins.pop(0), outs.pop(0)
    peers = [here.to_b, here.to_e, here.to_c]
    if any(entry[0] == EXCHANGE for entry in plan):
        peers.append(here.to_far)
    if any(
        entry[0] == SWAP or entry[0] == SHARE and any(do[0] != FAR for do in entry[2])
        for entry in plan
    ):
        peers.append(here.to_a)
    if any(entry[0] in (SHARE, RING) for entry in plan):
        peers.extend(here.to_d)
    here.greet(peers)
    if kind == GATHER:
        started = gather_start(here, x_ref, o_ref, cut)
    else:
        started = scatter_start(here, x_ref, scratch[3])
    through = []
    for entry in plan:
        source, out = ins.pop(0), outs.pop(0)
        if entry[3]:
            ins.pop(0)
        if entry[0] == SHARE:
            for action, first, count in entry[2]:
                if action == FAR:
                    share_far(here, out, entry[1], first, count)
                else:
                    across = share_start(here, source, out, entry[1], first, count)
                    if action == THROUGH:
                        through.append((across, out, entry[1], first, count))
                    else:
                        here.late(across)
        elif entry[0] == RING:
            lead = source.shape[1]
            for half in entry[2]:
                row, count = {0: (1 - here.a, lead // 2), 1: (here.a, lead // 2), 2: (0, lead)}[half]
                for step, peer in enumerate(here.to_d):
                    part = pl.ds(row * count, count)
                    here.late(here.copy(source.at[step, part], out.at[step, part], peer))
        elif entry[0] == SWAP:
            for first, count in entry[2]:
                part = pl.ds(first, count)
                here.late(here.copy(source.at[part], out.at[part], here.to_a))
        else:
            here.waits.extend(exchange_start(here, source, out, entry[1]))
    if kind == GATHER:
        gather_rest(here, o_ref, cut, started)
    else:
        scatter_rest(here, x_ref, o_ref, cut, started, *scratch[3:])
    for across, out, mode, first, count in through:
        across.wait_recv()
        share_far(here, out, mode, first, count)
    here.finish()


def share(mode, actions, block, array=None):
    return (SHARE, mode, actions, block, array)


def ring(halves, pieces, array=None):
    return (RING, 0, halves, pieces, array)


def swap(parts, piece, array=None):
    return (SWAP, 0, parts, piece, array)


def exchange(pieces, width=0):
    return (EXCHANGE, width, (), pieces, None)


def group_call(kind, x, number, *moves, cut=2):
    extent = lax.axis_size(DX)
    if kind == GATHER:
        out = jax.ShapeDtypeStruct((8,) + x.shape, x.dtype)
        space, scratch = pl.ANY, []
        cut = x.shape[0] // cut
    else:
        shape = x.shape[1:]
        out = jax.ShapeDtypeStruct(shape, x.dtype)
        space = pltpu.VMEM
        cut = shape[0] // cut
        first, second = (cut,) + shape[1:], (shape[0] - cut,) + shape[1:]
        sizes = ((4,) + shape, (3,) + shape, (2,) + first, (2,) + second, second, first)
        scratch = [pltpu.VMEM(size, x.dtype) for size in sizes]
    operands, outs, aliases, plan, copies, locals_ = [x], [out], {}, [], 13, 2
    for what, mode, actions, source, array in moves:
        operands.append(source)
        if array is not None:
            aliases[len(operands)] = len(outs)
            operands.append(array)
            outs.append(jax.ShapeDtypeStruct(array.shape, array.dtype))
        elif what == SHARE:
            lead, block = source.shape[:1], source.shape[1:]
            full = ((2, extent) + lead, (2,) + lead + (extent,), lead + (2, extent))[mode]
            outs.append(jax.ShapeDtypeStruct(full + block, source.dtype))
        elif what == EXCHANGE and mode:
            parts = source.shape[2] // mode
            shape = (parts // 2, source.shape[1], 8 * mode)
            outs.append(jax.ShapeDtypeStruct(shape, source.dtype))
            copies += 3 * parts
            locals_ += parts
        else:
            outs.append(jax.ShapeDtypeStruct(source.shape, source.dtype))
        plan.append((what, mode, actions, array is not None))
        copies += 3 + 2 * extent * len(actions)
        locals_ += 1 + len(actions)
    anywhere = pl.BlockSpec(memory_space=pl.ANY)
    results = pl.pallas_call(
        partial(group_kernel, kind, cut, plan, extent, len(operands), len(outs)),
        out_shape=tuple(outs),
        in_specs=[pl.BlockSpec(memory_space=space)] + [anywhere] * (len(operands) - 1),
        out_specs=tuple([pl.BlockSpec(memory_space=space)] + [anywhere] * (len(outs) - 1)),
        scratch_shapes=[
            pltpu.SemaphoreType.DMA((copies,)),
            pltpu.SemaphoreType.DMA((copies,)),
            pltpu.SemaphoreType.DMA((locals_,)),
        ]
        + scratch,
        input_output_aliases=aliases,
        compiler_params=pltpu.CompilerParams(
            collective_id=number, has_side_effects=True, vmem_limit_bytes=40 << 20
        ),
        cost_estimate=pl.CostEstimate(
            flops=0, bytes_accessed=80_000_000, transcendentals=0
        ),
    )(*operands)
    return results[0] if not moves else results


def first_kernel(extent, *refs):
    small, text, table_ref, out_ref, proj_ref, text_ref, expand_ref, contract_ref = refs[:8]
    small_out, text_out, proj_block, table, outs = refs[8:13]
    text_pieces, expand_pieces, contract_block, out_block = refs[13:17]
    table_block, proj_pieces = refs[17:19]
    here = Here(extent, *refs[19:])
    peers = [here.to_b, here.to_e, here.to_c, here.to_far, here.to_a] + here.to_d
    here.greet(peers)
    units, rows = table_block.shape[:2]

    def table_unit(k):
        table_block[k] = table_ref[pl.ds(k * rows, rows)].astype(BF16)
        return share_start(here, table_block, table, 0, k, 1)

    def by_head(source, target):
        kinds = source.shape[0]
        for q in range(4):
            for kind in range(kinds):
                for row in range(2):
                    target[q, :, pl.ds((kind * 2 + row) * HD, HD)] = source[
                        kind, :, pl.ds((row * 4 + q) * HD, HD)
                    ].astype(BF16)

    across = [table_unit(0), table_unit(1), table_unit(2)]
    small_started = gather_start(here, small, small_out, small.shape[0] // 2)
    by_head(proj_ref, proj_pieces)
    here.waits.extend(exchange_start(here, proj_pieces, proj_block))
    gather_rest(here, small_out, small.shape[0] // 2, small_started)
    text_started = gather_start(here, text, text_out, text.shape[0] // 2)
    for k in range(units):
        across[k].wait_recv()
        share_far(here, table, 0, k, 1)
        if k + 3 < units:
            across.append(table_unit(k + 3))
        elif k + 3 == units:
            out_block[...] = out_ref[...].astype(BF16)
            across.append(share_start(here, out_block, outs, 2, 0, 1))
        if k == 0:
            by_head(text_ref, text_pieces)
        elif k == 1:
            gather_rest(here, text_out, text.shape[0] // 2, text_started)
            width = expand_ref.shape[1] // 8
            for q in range(4):
                for row in range(2):
                    expand_pieces[q, :, pl.ds(row * width, width)] = expand_ref[
                        :, pl.ds((row * 4 + q) * width, width)
                    ].astype(BF16)
        elif k == 2:
            for unit in range(units):
                contract_block[unit] = contract_ref[pl.ds(unit * rows, rows)].astype(BF16)
    across[units].wait_recv()
    share_far(here, outs, 2, 0, 1)
    here.finish()


def first_call(small, text, table, outs, proj, text_maps, expand, contract):
    extent = lax.axis_size(DX)
    rows, width = table.shape
    kinds, in_rows, half = proj.shape

    def like(shape, kind=BF16):
        return jax.ShapeDtypeStruct(shape, kind)

    table_shape = (4, rows // 4, width)
    proj_shape = (4, in_rows, kinds * 2 * HD)
    out_shape = [
        like((8,) + small.shape, small.dtype),
        like((8,) + text.shape),
        like(proj_shape),
        like((2, extent) + table_shape),
        like((2, 2, extent) + outs.shape[1:]),
        like((4, text_maps.shape[1], 4 * HD)),
        like((4, in_rows, expand.shape[1] // 4)),
        like(table_shape),
        like(outs.shape),
    ]
    copies = 36 + 12 * extent
    anywhere, vmem = pl.BlockSpec(memory_space=pl.ANY), pl.BlockSpec(memory_space=pltpu.VMEM)
    return pl.pallas_call(
        partial(first_kernel, extent),
        out_shape=tuple(out_shape),
        in_specs=[anywhere] * 2 + [vmem] * 6,
        out_specs=tuple([anywhere] * 5 + [vmem] * 4),
        scratch_shapes=[
            pltpu.VMEM(table_shape, BF16),
            pltpu.VMEM(proj_shape, BF16),
            pltpu.SemaphoreType.DMA((copies,)),
            pltpu.SemaphoreType.DMA((copies,)),
            pltpu.SemaphoreType.DMA((12,)),
        ],
        compiler_params=pltpu.CompilerParams(
            collective_id=1, has_side_effects=True, vmem_limit_bytes=48 << 20
        ),
    )(small, text, table, outs, proj, text_maps, expand, contract)


def last_kernel(extent, tile_ref, x_ref, total_ref, o_ref, send, recv, local, held, sums):
    here = Here(extent, send, recv, local)
    near = [
        {
            BX: lax.rem(here.b + k // 4, 2),
            EX: lax.rem(here.e + k // 2 % 2, 2),
            CX: lax.rem(here.c + k % 2, 2),
        }
        for k in range(1, 8)
    ]
    away = [
        {AX: lax.rem(here.a + k // extent, 2), DX: lax.rem(here.d + k % extent, extent)}
        for k in range(1, 2 * extent)
    ]
    here.greet(near + away)
    first = [here.copy(tile_ref, held.at[k], peer) for k, peer in enumerate(near)]
    cut = x_ref.shape[0] // 3
    started = gather_start(here, x_ref, o_ref, cut)
    for made in first:
        made.wait_recv()
    terms = [tile_ref[...]] + [held[k] for k in range(7)]
    while len(terms) > 1:
        terms = [terms[k] + terms[k + 1] for k in range(0, len(terms), 2)]
    sums[...] = terms[0]
    mine = 7 + here.a * extent + here.d
    second = [here.copy(sums, held.at[mine], peer) for peer in away]
    held[mine] = terms[0]
    gather_rest(here, o_ref, cut, started)
    for made in second:
        made.wait_recv()
    total = held[7]
    for k in range(1, 2 * extent):
        total = total + held[7 + k]
    total_ref[...] = total
    here.finish()


def last_call(tile, x):
    extent = lax.axis_size(DX)
    peers = 6 + 2 * extent
    vmem, anywhere = pl.BlockSpec(memory_space=pltpu.VMEM), pl.BlockSpec(memory_space=pl.ANY)
    return pl.pallas_call(
        partial(last_kernel, extent),
        out_shape=(
            jax.ShapeDtypeStruct(tile.shape, tile.dtype),
            jax.ShapeDtypeStruct((8,) + x.shape, x.dtype),
        ),
        in_specs=[vmem, anywhere],
        out_specs=(vmem, anywhere),
        scratch_shapes=[
            pltpu.SemaphoreType.DMA((peers + 13,)),
            pltpu.SemaphoreType.DMA((peers + 13,)),
            pltpu.SemaphoreType.DMA((1,)),
            pltpu.VMEM((peers + 1,) + tile.shape, tile.dtype),
            pltpu.VMEM(tile.shape, tile.dtype),
        ],
        compiler_params=pltpu.CompilerParams(collective_id=19, has_side_effects=True),
    )(tile, x)


def spread(rows, number, *moves, cut=2):
    count, width = rows.shape
    full = group_call(GATHER, rows, number, *moves, cut=cut)
    if moves:
        return (full[0].reshape(8 * count, width),) + tuple(full[1:])
    return full.reshape(8 * count, width)


def collect(parts, number, *moves, cut=2):
    count, width = parts.shape
    parts = parts.reshape(8, count // 8, width)
    return group_call(SCATTER, parts, number, *moves, cut=cut)


def after(value, *needed):
    return lax.optimization_barrier((value, needed))[0]


def plain(x):
    return with_layout_constraint(x, Layout(tuple(range(x.ndim))))


def send(block, axis, step, extent):
    ring = [(k, (k + step) % extent) for k in range(extent)]
    return plain(lax.ppermute(plain(block), axis, ring))


def pick(array, index, axis):
    return lax.dynamic_slice_in_dim(array, index, 1, axis)


def grad_kernel(with_base, extent, rows, d_ref, left_ref, right_ref, *refs):
    keep_ref, piece_ref = refs[-2:]
    product = tn(left_ref[...], right_ref[...])
    if with_base:
        product = product + refs[0][...]
    for k in range(keep_ref.shape[0]):
        for column in range(extent):
            start = (k * extent + column) * rows
            part = product[start : start + rows]
            step = lax.rem(column - d_ref[0] + extent, extent)

            @pl.when(step == 0)
            def _():
                keep_ref[k] = part

            @pl.when(step > 0)
            def _():
                piece_ref[step - 1, k] = part.astype(piece_ref.dtype)


def weight_grad(left, right, rows, wire, base=None):
    extent = lax.axis_size(DX)
    count, columns = right.shape
    lead = left.shape[1] // (rows * extent)
    if rows % 128:
        full = tn(left, right) if base is None else tn(left, right) + base
        full = full.reshape(lead, extent, rows, columns)
        split = [
            lax.dynamic_index_in_dim(full, lax.rem(lax.axis_index(DX) + s, extent), 1, False)
            for s in range(extent)
        ]
        return split[0], jnp.stack(split[1:]).astype(wire)

    chunk = max(1, lead // 4) if rows * extent * (lead // 4) >= 512 else max(1, 512 // (rows * extent))
    deep = chunk * extent * rows
    wide = columns if columns <= 1024 else columns // 2
    in_specs = [
        pl.BlockSpec((count, deep), lambda k, j, d: (0, k)),
        pl.BlockSpec((count, wide), lambda k, j, d: (0, j)),
    ]
    operands = [left, right]
    if base is not None:
        in_specs.append(pl.BlockSpec((deep, wide), lambda k, j, d: (k, j)))
        operands.append(base)
    return pl.pallas_call(
        partial(grad_kernel, base is not None, extent, rows),
        out_shape=(
            jax.ShapeDtypeStruct((lead, rows, columns), F32),
            jax.ShapeDtypeStruct((extent - 1, lead, rows, columns), wire),
        ),
        grid_spec=pltpu.PrefetchScalarGridSpec(
            num_scalar_prefetch=1,
            grid=(lead // chunk, columns // wide),
            in_specs=in_specs,
            out_specs=(
                pl.BlockSpec((chunk, rows, wide), lambda k, j, d: (k, 0, j)),
                pl.BlockSpec((extent - 1, chunk, rows, wide), lambda k, j, d: (0, k, 0, j)),
            ),
        ),
        compiler_params=pltpu.CompilerParams(vmem_limit_bytes=48 << 20),
        cost_estimate=pl.CostEstimate(
            flops=2 * count * left.shape[1] * columns,
            bytes_accessed=left.size * 2 + right.size * 2 + left.shape[1] * columns * 4,
            transcendentals=0,
        ),
    )(lax.axis_index(DX).reshape(1), *operands)


def product_kernel(left_ref, right_ref, out_ref):
    out_ref[...] = tn(left_ref[...], right_ref[...])


def product(left, right):
    count, columns = right.shape
    deep, wide = left.shape[1] // 2, columns // 2
    return pl.pallas_call(
        product_kernel,
        out_shape=jax.ShapeDtypeStruct((left.shape[1], columns), F32),
        grid=(2, 2),
        in_specs=[
            pl.BlockSpec((count, deep), lambda k, j: (0, k)),
            pl.BlockSpec((count, wide), lambda k, j: (0, j)),
        ],
        out_specs=pl.BlockSpec((deep, wide), lambda k, j: (k, j)),
        compiler_params=pltpu.CompilerParams(vmem_limit_bytes=48 << 20),
        cost_estimate=pl.CostEstimate(
            flops=2 * count * left.shape[1] * columns,
            bytes_accessed=left.size * 2 + right.size * 2 + left.shape[1] * columns * 4,
            transcendentals=0,
        ),
    )(left, right)


def total_at(index, keep, pieces):
    total = pick(keep.reshape((2, -1) + keep.shape[1:]), index, 0)
    for step in range(pieces.shape[0]):
        piece = pieces[step].reshape((2, -1) + pieces.shape[2:])
        total = total + pick(piece, index, 0).astype(F32)
    return total[0]


def other_half(keep, pieces, wire):
    return total_at(1 - lax.axis_index(AX), keep, pieces).astype(wire)


def own_half(keep, pieces, across):
    return total_at(lax.axis_index(AX), keep, pieces) + across.astype(F32)


def layer_norm(inputs, gain, bias):
    average = jnp.mean(inputs, -1, keepdims=True)
    centred = inputs - average
    factor = lax.rsqrt(jnp.mean(centred * centred, -1, keepdims=True) + EPS_NORM)
    normed = centred * factor
    return (normed * gain + bias).astype(BF16), (normed, factor)


def norm_back(upstream, saved, gain):
    normed, factor = saved
    inner = upstream * gain
    back = factor * (
        inner
        - jnp.mean(inner, -1, keepdims=True)
        - normed * jnp.mean(inner * normed, -1, keepdims=True)
    )
    return back, jnp.sum(upstream * normed, 0), jnp.sum(upstream, 0)


def dot_images(x, y, x_side, y_side):
    dims = (((x_side,), (y_side,)), ((0,), (0,)))
    return lax.dot_general(x, y, dims, preferred_element_type=F32)


def heads(x, images):
    x = x.reshape(images, -1, x.shape[-1])
    return [x[..., k : k + HD] for k in range(0, x.shape[-1], HD)]


def flat(parts):
    joined = jnp.concatenate([part.astype(BF16) for part in parts], -1)
    return joined.reshape(-1, joined.shape[-1])


def attend(queries, keys, values):
    mixed, saved = [], []
    for query, key, value in zip(queries, keys, values):
        scores = dot_images(query, key, 2, 2) * SCALE
        top = jnp.max(scores, -1, keepdims=True)
        logsum = top + jnp.log(jnp.sum(jnp.exp(scores - top), -1, keepdims=True))
        probs = jnp.exp(scores - logsum)
        mixed.append(dot_images(probs.astype(BF16), value, 2, 1))
        saved.append(probs)
    return flat(mixed), saved


def attend_back(upstream, queries, keys, values, saved, images):
    grads = []
    for grad_out, query, key, value, probs in zip(
        heads(upstream, images), queries, keys, values, saved
    ):
        grad_probs = dot_images(grad_out, value, 2, 2)
        inner = jnp.sum(probs * grad_probs, -1, keepdims=True)
        grad_scores = (probs * (grad_probs - inner)).astype(BF16)
        grads.append(
            (
                dot_images(grad_scores, key, 2, 1) * SCALE,
                dot_images(grad_scores, query, 1, 1) * SCALE,
                dot_images(probs.astype(BF16), grad_out, 1, 1),
            )
        )
    return tuple(flat(parts) for parts in zip(*grads))


def adamw(state, grad, rate, decay, fix_one, fix_two):
    master, first, second = state
    first_new = BETA_ONE * first + (1.0 - BETA_ONE) * grad
    second_new = BETA_TWO * second + (1.0 - BETA_TWO) * grad * grad
    update = first_new / fix_one / (jnp.sqrt(second_new / fix_two) + ADAM_EPS)
    return master - rate * (update + decay * master), first_new, second_new


def body(image_codes, masked, null_caption, captions, step_count, *states):
    table_state, vector_state, proj_state, text_state, out_state, expand_state, contract_state = (
        states[k : k + 3] for k in range(0, 21, 3)
    )
    b, e, c = (lax.axis_index(k) for k in (BX, EX, CX))
    extent = lax.axis_size(DX)
    vectors = vector_state[0]
    length = vectors.shape[0] - 9
    norm_rows = vectors[length + 1 :]
    width = vectors.shape[1]
    block = table_state[0].shape[0]
    kinds, in_rows, half = proj_state[0].shape
    text_rows = text_state[0].shape[1]
    hidden_width = extent * block
    pair = 2 * HD

    own_images = image_codes.shape[1]
    tokens = own_images * length
    small = jnp.concatenate(
        [
            image_codes.reshape(2, -1),
            masked.reshape(2, -1),
            jnp.broadcast_to(null_caption.reshape(2, -1, 1), masked.shape).reshape(2, -1),
        ],
        1,
    )
    small = lax.dynamic_index_in_dim(small, c, 0, False)
    small = jnp.pad(small, (0, -small.shape[0] % (16 * 128)))
    own_mask, own_null = small[tokens : 2 * tokens], small[2 * tokens : 3 * tokens]
    text = lax.dynamic_index_in_dim(captions, c, 0, False)
    text = text.reshape(-1, text.shape[-1])
    gathered, group_captions, proj_block, table, outs, *rest = first_call(
        small.reshape(16, -1),
        text,
        table_state[0],
        out_state[0],
        proj_state[0],
        text_state[0],
        expand_state[0],
        contract_state[0],
    )
    text_pieces, expand_pieces, contract_block, out_block = rest
    gathered = gathered.reshape(8, -1)
    group_captions = group_captions.reshape(-1, group_captions.shape[-1])
    group_codes = gathered[:, :tokens].reshape(-1)
    weight = gathered[:, tokens : 2 * tokens].reshape(-1).astype(F32)
    chosen = own_mask[:, None] == 1
    keep_rows = 1.0 - own_null[:, None].astype(F32)
    images = 8 * own_images
    table = table.reshape(-1, width)
    codes_here = table.shape[0]

    in_half = lax.rem(group_codes, 8 * hidden_width)
    outer = in_half // block
    inside = (
        (group_codes // (8 * hidden_width) == c)
        & (lax.rem(outer // extent, 2) == e)
        & (lax.rem(outer // (2 * extent), 2) == b)
    )
    outer = (outer // (4 * extent)) * extent + lax.rem(outer, extent)
    local_code = jnp.where(inside, outer * block + lax.rem(in_half, block), -1)
    at_code = jnp.arange(codes_here)[None, :] == local_code[:, None]

    part = nn(at_code.astype(BF16), table).astype(BF16)
    looked, proj, text_block = collect(
        part, 2, share(1, ((START, 0, 3),), proj_block), exchange(text_pieces), cut=4
    )
    x_zero = jnp.where(chosen, vectors[length], looked.astype(F32))
    x_zero = x_zero + jnp.tile(vectors[:length], (own_images, 1))
    a_one, norm_one = layer_norm(x_zero, norm_rows[0], norm_rows[1])
    a_one, proj, w_text, expand_block = spread(
        a_one,
        3,
        share(1, ((THROUGH, 3, 1), (FAR, 0, 3)), proj_block, proj),
        share(1, ((START, 0, 1),), text_block),
        exchange(expand_pieces),
        cut=4,
    )
    proj = proj.reshape(width, kinds * pair)
    w_qkv, w_cross = proj[:, : 3 * pair], proj[:, 3 * pair :]
    triple = nn(a_one, w_qkv).astype(BF16)
    queries, keys, values = (
        heads(triple[:, k : k + pair], images) for k in (0, pair, 2 * pair)
    )
    attn_one, probs_one = attend(queries, keys, values)
    part = nn(attn_one, outs[0].reshape(pair, width))
    back, w_text, outs = collect(
        part,
        4,
        share(1, ((START, 1, 3), (FAR, 0, 1)), text_block, w_text),
        share(2, ((START, 1, 1),), out_block, outs),
        cut=4,
    )
    x_one = x_zero + back

    a_two, norm_two = layer_norm(x_one, norm_rows[2], norm_rows[3])
    a_two, w_text, outs, expand = spread(
        a_two,
        5,
        share(1, ((FAR, 1, 3),), text_block, w_text),
        share(2, ((FAR, 1, 1),), out_block, outs),
        share(1, ((START, 0, 2),), expand_block),
        cut=4,
    )
    w_text = w_text.reshape(-1, 2 * pair)
    out_maps = outs.reshape(2, pair, width)
    text_pair = nn(group_captions, w_text).astype(BF16)
    text_keys, text_values = heads(text_pair[:, :pair], images), heads(text_pair[:, pair:], images)
    cross = heads(nn(a_two, w_cross).astype(BF16), images)
    attn_two, probs_two = attend(cross, text_keys, text_values)
    part = nn(attn_two, out_maps[1])
    back, expand, contract = collect(
        part,
        6,
        share(1, ((START, 2, 2), (FAR, 0, 2)), expand_block, expand),
        share(0, ((START, 0, 2),), contract_block),
        cut=4,
    )
    x_two = x_one + keep_rows * back

    a_three, norm_three = layer_norm(x_two, norm_rows[4], norm_rows[5])
    a_three, expand, contract = spread(
        a_three,
        7,
        share(1, ((FAR, 2, 2),), expand_block, expand),
        share(0, ((FAR, 0, 2), (THROUGH, 2, 1), (THROUGH, 3, 1)), contract_block, contract),
        cut=4,
    )
    expand, contract = expand.reshape(width, -1), contract.reshape(-1, width)
    mask_total = after(jnp.broadcast_to(jnp.sum(weight), (8, 128)), x_two)
    mask_total = mask_total + send(mask_total, AX, 1, 2)
    mask_total = mask_total + sum(send(mask_total, DX, step, extent) for step in range(1, extent))
    mask_total = mask_total[0, 0]
    preact = nn(a_three, expand)
    hidden = jax.nn.gelu(preact, approximate=True).astype(BF16)
    x_three = x_two + collect(nn(hidden, contract), 8)

    a_four, norm_four = layer_norm(x_three, norm_rows[6], norm_rows[7])
    a_four = spread(a_four, 9)
    logits = nt(a_four, table)
    target = jnp.sum(jnp.where(at_code, logits, 0.0), 1)
    top = jnp.max(logits, 1)
    total = jnp.sum(jnp.exp(logits - top[:, None]), 1)
    count = target.shape[0]
    stats = jnp.stack([top, total, target, target])
    stats = group_call(GATHER, stats.reshape(16, count // 4), 10).reshape(8, 4, count)
    peak = jnp.max(stats[:, 0], 0)
    total = jnp.sum(stats[:, 1] * jnp.exp(stats[:, 0] - peak), 0)
    head_logsum = peak + jnp.log(total)
    loss_sum = jnp.sum(weight * (head_logsum - jnp.sum(stats[:, 2], 0)))

    head_probs = jnp.exp(logits - head_logsum[:, None])
    logit_grad = (head_probs - at_code.astype(F32)) * (weight / mask_total)[:, None]
    logit_grad = logit_grad.astype(BF16)
    upstream = collect(nn(logit_grad, table), 8)
    grad_three, gain_six, gain_seven = norm_back(upstream, norm_four, norm_rows[6])
    branch_three = spread(grad_three.astype(BF16), 9)

    contract_keep, contract_wire = weight_grad(hidden, branch_three, block, BF16)
    hidden_grad = nt(branch_three, contract)
    gelu_pull = jax.vjp(partial(jax.nn.gelu, approximate=True), preact)[1]
    preact_grad = gelu_pull(hidden_grad)[0].astype(BF16)
    expand_keep, expand_wire = weight_grad(a_three, preact_grad, in_rows, BF16)
    part = nt(preact_grad, expand)
    back, contract_came = collect(part, 11, ring((0,), contract_wire))

    back, gain_four, gain_five = norm_back(back, norm_three, norm_rows[4])
    grad_two = grad_three + back
    branch_two = grad_two.astype(BF16) * keep_rows.astype(BF16)
    table_head = product(logit_grad, a_four)
    contract_half = other_half(contract_keep, contract_came, BF16)
    contract_half = contract_half.reshape(2, block // 2, width)
    branch_two, expand_came, contract_across = spread(
        after(branch_two, table_head),
        12,
        ring((0,), expand_wire),
        swap(((0, 1),), contract_half),
        cut=4,
    )
    attn_grad = nt(branch_two, out_maps[1]).astype(BF16)
    cross_grad, key_grad, value_grad = attend_back(
        attn_grad, cross, text_keys, text_values, probs_two, images
    )
    pair_grad = jnp.concatenate([key_grad, value_grad], 1)
    text_keep, text_wire = weight_grad(group_captions, pair_grad, text_rows, WIRE)
    expand_half = other_half(expand_keep, expand_came, BF16)
    part = nt(cross_grad, w_cross)
    back, contract_across, contract_came, expand_across, text_came = collect(
        part,
        13,
        swap(((1, 1),), contract_half, contract_across),
        ring((1,), contract_wire, contract_came),
        swap(((0, 2),), expand_half),
        ring((0,), text_wire),
        cut=4,
    )

    back, gain_two, gain_three = norm_back(back, norm_two, norm_rows[2])
    grad_one = grad_two + back
    cross_keep, cross_wire = weight_grad(a_two, cross_grad, in_rows, WIRE)
    branch_one, expand_across, expand_came, cross_came = spread(
        after(grad_one.astype(BF16), cross_keep),
        14,
        swap(((2, 2),), expand_half, expand_across),
        ring((1,), expand_wire, expand_came),
        ring((0,), cross_wire),
        cut=4,
    )
    attn_grad = nt(branch_one, out_maps[0]).astype(BF16)
    triple_grad = jnp.concatenate(
        attend_back(attn_grad, queries, keys, values, probs_one, images), 1
    )
    out_one = weight_grad(attn_one, branch_one, HD // extent, BF16)
    out_two = weight_grad(attn_two, branch_two, HD // extent, BF16)
    out_keep = jnp.stack([out_one[0], out_two[0]], 1)
    out_wire = jnp.stack([out_one[1], out_two[1]], 2)
    text_half = other_half(text_keep, text_came, WIRE)
    triple_keep, triple_wire = weight_grad(a_one, triple_grad, in_rows, WIRE)
    part = nt(triple_grad, w_qkv)
    out_wire = plain(out_wire)
    back, text_across, text_came, out_came, triple_came = collect(
        part,
        15,
        swap(((0, 4),), text_half),
        ring((1,), text_wire, text_came),
        ring((0,), out_wire),
        ring((0,), triple_wire),
        cut=4,
    )

    back, gain_zero, gain_one = norm_back(back, norm_one, norm_rows[0])
    grad_zero = grad_one + back
    looked_grad = jnp.where(chosen, 0.0, grad_zero).astype(BF16)
    triple_half = other_half(triple_keep, triple_came, WIRE)
    cross_half = other_half(cross_keep, cross_came, WIRE)
    out_half = other_half(out_keep, out_came, BF16)
    expand_shard = own_half(expand_keep, expand_came, expand_across)
    looked_grad, triple_came, cross_came, triple_across, expand_shard = spread(
        looked_grad,
        16,
        ring((1,), triple_wire, triple_came),
        ring((1,), cross_wire, cross_came),
        swap(((0, 4),), triple_half),
        exchange(plain(expand_shard), hidden_width),
        cut=4,
    )
    table_keep, table_wire = weight_grad(
        at_code.astype(BF16), looked_grad, block, BF16, table_head
    )

    position_grad = jnp.sum(grad_zero.reshape(own_images, length, -1), 0)
    mask_grad = jnp.sum(jnp.where(chosen, grad_zero, 0.0), 0)
    gains = [gain_zero, gain_one, gain_two, gain_three, gain_four, gain_five, gain_six, gain_seven]
    rows = vectors.shape[0]
    padded = -(-rows // 192) * 192
    place_of = jnp.arange(padded - length)[:, None]
    tail = sum(jnp.where(place_of == k, gain, 0.0) for k, gain in enumerate([mask_grad] + gains))
    vector_grad = jnp.concatenate([position_grad, tail], 0)

    text_shard = own_half(text_keep, text_came, text_across)
    vector_part, table_came, out_came, cross_across, out_across, text_shard = group_call(
        SCATTER,
        vector_grad.reshape(8, padded // 8, width),
        17,
        ring((0,), table_wire),
        ring((1,), out_wire, out_came),
        swap(((0, 4),), cross_half),
        swap(((0, out_half.shape[0]),), out_half),
        exchange(plain(text_shard), HD),
        cut=3,
    )
    vector_part = vector_part + send(vector_part, AX, 1, 2)
    if extent == 2:
        vector_part = vector_part + send(vector_part, DX, 1, 2)
    else:
        vector_part = lax.psum(vector_part, DX)
    table_half = other_half(table_keep, table_came, BF16)
    proj_shard = jnp.concatenate(
        [
            own_half(triple_keep, triple_came, triple_across),
            own_half(cross_keep, cross_came, cross_across),
        ],
        2,
    )
    nothing, table_came, table_across, proj_shard = group_call(
        GATHER,
        jnp.broadcast_to(weight[0], (16, 128)),
        18,
        ring((1,), table_wire, table_came),
        swap(((0, 1),), table_half),
        exchange(plain(proj_shard), HD),
    )
    contract_across = contract_across.reshape(1, block, width)
    contract_shard = own_half(contract_keep, contract_came, contract_across).reshape(block, width)
    out_shard = own_half(out_keep, out_came, out_across).reshape(out_state[0].shape)
    table_shard = own_half(table_keep, table_came, table_across).reshape(block, width)

    expand_shard = expand_shard.reshape(expand_state[0].shape)

    shards = (table_shard, proj_shard, text_shard, out_shard, expand_shard, contract_shard)
    squares = sum((jnp.sum(piece * piece) for piece in shards))
    squares = squares + jnp.sum(vector_part * vector_part) / (2 * extent)
    lanes = jnp.arange(128)[None, :]
    numbers = jnp.where(lanes == 0, squares, jnp.where(lanes == 1, loss_sum, 0.0))
    numbers, vector_grad = last_call(jnp.broadcast_to(numbers, (8, 128)), vector_part)
    loss_value = numbers[0, 1] / 8.0 / mask_total
    grad_norm = jnp.sqrt(numbers[0, 0])
    vector_grad = vector_grad.reshape(padded, width)[:rows]
    clip_scale = CLIP / jnp.maximum(grad_norm, CLIP)
    count_step = step_count[0].astype(F32)
    fix_one = 1.0 - BETA_ONE**count_step
    fix_two = 1.0 - BETA_TWO**count_step
    results = [loss_value, grad_norm]
    matrices = (table_state, proj_state, text_state, out_state, expand_state, contract_state)
    updated = [
        adamw(state, grad * clip_scale, RATE_MATRIX, DECAY, fix_one, fix_two)
        for state, grad in zip(matrices, shards)
    ]
    vector_new = adamw(
        vector_state, vector_grad * clip_scale, RATE_VECTOR, 0.0, fix_one, fix_two
    )
    updated.insert(1, vector_new)
    for entry in updated:
        results.extend(entry)
    return tuple(results)


def solution(mesh):
    grid = mesh.devices
    extent = grid.shape[0] // 8
    fine = Mesh(grid.reshape(2, 2, 2, extent, grid.shape[1]), (AX, BX, EX, DX, CX))
    rows = P((CX,) + DP, None)
    both = P(None, DP, CX)
    kinds = (rows, P(), both, both, P(None, (CX,) + DP, None), P(DP, CX), rows)
    states = tuple(kind for kind in kinds for _ in range(3))
    batch = P(None, DP, None)
    return jax.shard_map(
        body,
        mesh=fine,
        in_specs=(batch, batch, P(None, DP), P(None, DP, None, None), P()) + states,
        out_specs=(P(), P()) + states,
        check_vma=False,
    )
```

time: 1410 us -> 1250 us (0.89)
  Pallas kernels: 773 us -> 999 us
  waiting for transfers between devices: 180 us -> 1.46 us
  local copies, waits for them, and re-layouts: 130 us -> 56.4 us
  starting transfers between devices: 76.6 us -> 5.48 us
  other arithmetic: 121 us -> 79 us
    pallas_call x27, Pallas kernels: 764 us -> 990 us  [the longest x19 852 us: group_call(): pl.pallas_call(partial(group_kernel, kind, cut, plan, extent, len(operand...]
    ppermute x36 -> x4, waiting for transfers between devices: 169 us -> 1.46 us  [send(): return plain(lax.ppermute(plain(block), axis, ring))]
    ppermute x36 -> x4, starting transfers between devices: 49.9 us -> 5.48 us  [send(): return plain(lax.ppermute(plain(block), axis, ring))]
    dynamic_update_slice x23 -> x0, local copies, waits for them, and re-layouts: 34.2 us -> none  [put(): return lax.dynamic_update_slice(full, piece, start)]
    all_to_all x6 -> x0, starting transfers between devices: 26.6 us -> none  [exchange(): return plain(lax.all_to_all(plain(pieces), QX, 0, 0))]
    reshape x14 -> x4, local copies, waits for them, and re-layouts: 17.5 us -> 0.11 us  [the longest x1 0.06 us: body(): group_call(GATHER, stats.reshape(16, count // 4), 10).reshape(8, 4, count)]
    convert_element_type x13 -> x10, other arithmetic: 23.3 us -> 7.56 us  [the longest x7 4 us: other_half(): return total_at(1 - lax.axis_index(AX), keep, pieces).astype(wire)]
    unnamed x324 -> x349, local copies, waits for them, and re-layouts: 48.1 us -> 41.1 us
  transfers between devices with their start and end apart: 43 -> 4, of which waited for: 12 -> 1; matrix products, arithmetic and copies ran while one was open for 16% -> 2% of each run, Pallas kernels for 38% -> 4%
where the time goes in v2:
time: 1250 us; the launch traced here: 1240 us
  Pallas kernels  999 us (80%)
  matrix products  86.4 us (7%)
  other arithmetic  79 us (6%)
  local copies, waits for them, and re-layouts  56.4 us (5%)
  between operations  13.2 us (1%)
    pallas_call x19, Pallas kernels, group_call(): pl.pallas_call(partial(group_kernel, kind, cut, plan, extent, len(operand...  852 us
    dot_general x18, matrix products, dot(): return lax.dot_general(x, y, (dims, ((), ())), preferred_element_type=F32)  78.6 us
    pallas_call x1, Pallas kernels, first_call(): pl.pallas_call(partial(first_kernel, extent), out_shape=tuple(out_shape),...  76.9 us
    pallas_call x6, Pallas kernels, weight_grad(): pl.pallas_call(partial(grad_kernel, base is not None, extent, rows), out_...  45.2 us
    unnamed x349, local copies, waits for them, and re-layouts  41.1 us
    sub x7, other arithmetic, adamw(): return (master - rate * (update + decay * master), first_new, second_new)  28.8 us
  transfers between devices with their start and end apart: 4, of which 1 were waited for; matrix products, arithmetic and copies ran while one was open for 2% of the time, Pallas kernels for 4%

profile of v2, /device:TPU:0, one launch (start us, length us, event | category | flops | bytes accessed | tf_op | source)
XLA Modules:
  0.0 1241.1 jit_solution(3149517609975109193)
XLA Ops:
  5.3 76.9 %shard_map.425 = (s32[8,16,128]{2,1,0:T(8,128)S(1)}, bf16[8,32,4096]{2,1,0:T(8,128)(2,1)}, bf16[4,128,1024]{2,1,0:T(8,128)(2,1)S(1)}, bf16[2,2,4,64,2048]{4,3,2,...) custom-call(s32[16,128]{1,0:T(8,128)S(1)} %pad_bitcast_fusion.refs_0, ...), custom_call_target="tpu_custom_call" | custom-call | tf_op jit(solution)/shard_map/pallas_call | solution.py:452
  82.3 7.1 fusion.9
  89.4 48.4 %shard_map.426 = (bf16[128,2048]{1,0:T(8,128)(2,1)S(1)}, bf16[2,4,2,128,1024]{4,3,2,1,0:T(8,128)(2,1)}, bf16[4,256,512]{2,1,0:T(8,128)(2,1)S(1)}) custom-call(bf16[8,128,2048]{2,1,0:T(8,128)(2,1)S(1)} %bitcast.298, bf16[4,128,1024]{2,1,0:T(8,128)(2,1)S(1)} %get-tuple-element.104.refs_1_, bf16[4,256,512]{2,1,0:T(8,128)(2,1)S(1)} %get-tuple-element.105.refs_2_), custom_call_target="tpu_custom_call" | custom-call | bytes 80000000 | tf_op jit(solution)/shard_map/pallas_call | solution.py:352
  138.6 45.9 %shard_map.427 = (bf16[8,128,2048]{2,1,0:T(8,128)(2,1)S(1)}, bf16[2,4,2,128,1024]{4,3,2,1,0:T(8,128)(2,1)}, bf16[2,4,2,256,512]{4,3,2,1,0:T(8,128)(2,1)}, bf16[4,128,1024]{2,1,0:T(8,128)(2,1)S(1)}) custom-call(bf16[128,2048]{1,0:T(8,128)(2,1)S(1)} %add_convert_fusion.6.refs_0_, ...), custom_call_target="tpu_custom_call", output_to_operand_aliasing={{1}: (2, {})} | custom-call | bytes 80000000 | tf_op jit(solution)/shard_map/pallas_call | solution.py:352
  186.6 5.3 fusion.24
  195.5 4.7 fusion.138.refs_0_
  200.1 66.8 %shard_map.428 = (f32[128,2048]{1,0:T(8,128)S(1)}, bf16[2,4,2,256,512]{4,3,2,1,0:T(8,128)(2,1)S(1)}, bf16[2,2,2,64,2048]{4,3,2,1,0:T(8,128)(2,1)S(1)}) custom-call(f32[8,128,2048]{2,1,0:T(8,128)} %fusion.138.refs_0_, bf16[4,256,512]{2,1,0:T(8,128)(2,1)S(1)} %get-tuple-element.108.refs_3_.refs_1_, ...), custom_call_target="tpu_custom_call", output_to_operand_aliasing={{1}: (2, {}), {2}: (4, {})} | custom-call | bytes 80000000 | tf_op jit(solution)/shard_map/pallas_call | solution.py:352
  267.7 41.1 %shard_map.429 = (bf16[8,128,2048]{2,1,0:T(8,128)(2,1)S(1)}, bf16[2,4,2,256,512]{4,3,2,1,0:T(8,128)(2,1)S(1)}, bf16[2,2,2,64,2048]{4,3,2,1,0:T(8,128)(2,1)S(1)}, bf16[2,4,2,128,1024]{4,3,2,1,0:T(8,128)(2,1)}) custom-call(bf16[128,2048]{1,0:T(8,128)(2,1)S(1)} %add_convert_fusion.5.refs_0_, ...), custom_call_target="tpu_custom_call", output_to_operand_aliasing={{1}: (2, {}), {2}: (4, {})} | custom-call | bytes 80000000 | tf_op jit(solution)/shard_map/pallas_call | solution.py:352
  315.9 4.6 fusion.137.refs_0_
  320.6 66.4 %shard_map.430 = (f32[128,2048]{1,0:T(8,128)S(1)}, bf16[2,4,2,128,1024]{4,3,2,1,0:T(8,128)(2,1)S(1)}, bf16[2,2,4,64,2048]{4,3,2,1,0:T(8,128)(2,1)S(1)}) custom-call(f32[8,128,2048]{2,1,0:T(8,128)} %fusion.137.refs_0_, bf16[4,128,1024]{2,1,0:T(8,128)(2,1)S(1)} %get-tuple-element.118.refs_5_.refs_1_, ...), custom_call_target="tpu_custom_call", output_to_operand_aliasing={{1}: (2, {})} | custom-call | bytes 80000000 | tf_op jit(solution)/shard_map/pallas_call | solution.py:352
  389.4 49.2 %shard_map.431 = (bf16[8,128,2048]{2,1,0:T(8,128)(2,1)S(1)}, bf16[2,4,2,128,1024]{4,3,2,1,0:T(8,128)(2,1)S(1)}, bf16[2,2,4,64,2048]{4,3,2,1,0:T(8,128)(2,1)}) custom-call(bf16[128,2048]{1,0:T(8,128)(2,1)S(1)} %add_convert_fusion.4.refs_0_, ...), custom_call_target="tpu_custom_call", output_to_operand_aliasing={{1}: (2, {}), {2}: (4, {})} | custom-call | bytes 80000000 | tf_op jit(solution)/shard_map/pallas_call | solution.py:352
  438.6 7.2 multiply_convert_fusion.1
  445.8 4.5 fusion.168.refs_0_
  451.6 40.2 %shard_map.432 = f32[128,2048]{1,0:T(8,128)S(1)} custom-call(f32[8,128,2048]{2,1,0:T(8,128)S(1)} %fusion.168.refs_0_), custom_call_target="tpu_custom_call" | custom-call | bytes 80000000 | tf_op jit(solution)/shard_map/pallas_call | solution.py:352
  492.5 20.8 %shard_map.433 = bf16[8,128,2048]{2,1,0:T(8,128)(2,1)S(1)} custom-call(bf16[128,2048]{1,0:T(8,128)(2,1)S(1)} %add_convert_fusion.3.refs_0_), custom_call_target="tpu_custom_call" | custom-call | bytes 80000000 | tf_op jit(solution)/shard_map/pallas_call | solution.py:352
  513.3 4.6 fusion.167
  520.0 7.7 shard_map.434
  544.1 3.2 multiply_convert_fusion.left_ref
  547.3 9.6 shard_map.439.refs_0_
  556.9 4.5 fusion.169.refs_0_
  561.4 39.9 %shard_map.435 = f32[128,2048]{1,0:T(8,128)S(1)} custom-call(f32[8,128,2048]{2,1,0:T(8,128)S(1)} %fusion.169.refs_0_), custom_call_target="tpu_custom_call" | custom-call | bytes 80000000 | tf_op jit(solution)/shard_map/pallas_call | solution.py:352
  603.8 21.1 %shard_map.436 = bf16[8,128,2048]{2,1,0:T(8,128)(2,1)S(1)} custom-call(bf16[128,2048]{1,0:T(8,128)(2,1)S(1)} %get-tuple-element.238.refs_0_), custom_call_target="tpu_custom_call" | custom-call | bytes 80000000 | tf_op jit(solution)/shard_map/pallas_call | solution.py:352
  626.9 9.6 shard_map.437
  636.5 9.3 fusion.6.right_ref
  645.8 8.6 shard_map.440
  654.5 4.6 fusion.170.refs_0_
  659.1 40.2 %shard_map.438 = (f32[128,2048]{1,0:T(8,128)S(1)}, bf16[1,2,256,2048]{3,2,1,0:T(8,128)(2,1)S(1)}) custom-call(f32[8,128,2048]{2,1,0:T(8,128)S(1)} %fusion.170.refs_0_, bf16[1,2,256,2048]{3,2,1,0:T(8,128)(2,1)S(1)} %get-tuple-element.132.refs_1_.refs_3_), custom_call_target="tpu_custom_call" | custom-call | bytes 80000000 | tf_op jit(solution)/shard_map/pallas_call | solution.py:352
  704.1 33.7 %shard_map.441 = (bf16[8,128,2048]{2,1,0:T(8,128)(2,1)S(1)}, bf16[1,8,128,1024]{3,2,1,0:T(8,128)(2,1)S(1)}, bf16[2,128,2048]{2,1,0:T(8,128)(2,1)S(1)}) custom-call(bf16[128,2048]{1,0:T(8,128)(2,1)S(1)} %get-tuple-element.134.refs_0_, bf16[1,8,128,1024]{3,2,1,0:T(8,128)(2,1)S(1)} %get-tuple-element.135.refs_1_.refs_3_, bf16[2,128,2048]{2,1,0:T(8,128)(2,1)S(1)} %bitcast.283), custom_call_target="tpu_custom_call" | custom-call | bytes 80000000 | tf_op jit(solution)/shard_map/pallas_call | solution.py:352
  745.0 5.9 fusion.50.refs_0_
  753.9 4.4 shard_map.444
  759.4 4.5 shard_map.442
  767.5 68.3 %shard_map.443 = (f32[128,2048]{1,0:T(8,128)S(1)}, bf16[2,128,2048]{2,1,0:T(8,128)(2,1)S(1)}, bf16[1,2,256,2048]{3,2,1,0:T(8,128)(2,1)S(1)}, bf16[4,128,1024]{2,...) custom-call(f32[8,128,2048]{2,1,0:T(8,128)} %fusion.50.refs_0_, ...), custom_call_target="tpu_custom_call", output_to_operand_aliasing={{1}: (2, {}), {2}: (4, {})} | custom-call | bytes 80000000 | tf_op jit(solution)/shard_map/pallas_call | solution.py:352
  839.3 33.9 %shard_map.445 = (bf16[8,128,2048]{2,1,0:T(8,128)(2,1)S(1)}, bf16[4,128,1024]{2,1,0:T(8,128)(2,1)S(1)}, bf16[1,8,128,1024]{3,2,1,0:T(8,128)(2,1)S(1)}, bf16[1,8,128,256]{3,2,1,0:T(8,128)(2,1)S(1)}) custom-call(bf16[128,2048]{1,0:T(8,128)(2,1)S(1)} %get-tuple-element.145.refs_0_, ...), custom_call_target="tpu_custom_call", output_to_operand_aliasing={{1}: (2, {}), {2}: (4, {})} | custom-call | bytes 80000000 | tf_op jit(solution)/shard_map/pallas_call | solution.py:352
  885.2 7.5 fusion.10
  892.7 7.5 shard_map.446
  902.1 68.3 %shard_map.447 = (f32[128,2048]{1,0:T(8,128)S(1)}, bf16[4,256,512]{2,1,0:T(8,128)(2,1)S(1)}, bf16[1,8,256,512]{3,2,1,0:T(8,128)(2,1)S(1)}, bf16[1,2,2,64,2048]{4...) custom-call(f32[8,128,2048]{2,1,0:T(8,128)} %bitcast.320, ...), custom_call_target="tpu_custom_call", output_to_operand_aliasing={{2}: (3, {})} | custom-call | bytes 80000000 | tf_op jit(solution)/shard_map/pallas_call | solution.py:352
  979.8 58.5 %shard_map.448 = (bf16[8,128,2048]{2,1,0:T(8,128)(2,1)}, bf16[1,8,128,768]{3,2,1,0:T(8,128)(2,1)S(1)}, bf16[1,8,128,256]{3,2,1,0:T(8,128)(2,1)S(1)}, bf16[4,128,768]{2,1,0:T(8,128)(2,1)S(1)}, f32[1,128,4096]{2,1,0:T(8,128)S(1)}) custom-call(bf16[128,2048]{1,0:T(8,128)(2,1)S(1)} %select_convert_fusion.refs_0_, ...), custom_call_target="tpu_custom_call", output_to_operand_aliasing={{1}: (2, {}), {2}: (4, {})} | custom-call | bytes 80000000 | tf_op jit(solution)/shard_map/pallas_call | solution.py:352
  1042.1 10.7 shard_map.449
  1052.9 50.8 %shard_map.450 = (f32[24,2048]{1,0:T(8,128)}, bf16[1,2,256,2048]{3,2,1,0:T(8,128)(2,1)S(1)}, bf16[1,2,2,64,2048]{4,3,2,1,0:T(8,128)(2,1)S(1)}, bf16[4,128,256]{2...) custom-call(f32[8,24,2048]{2,1,0:T(8,128)S(1)} %bitcast.289, ...), custom_call_target="tpu_custom_call", output_to_operand_aliasing={{2}: (3, {})} | custom-call | bytes 80000000 | tf_op jit(solution)/shard_map/pallas_call | solution.py:352
  1112.3 51.4 %shard_map.451 = (f32[8,16,128]{2,1,0:T(8,128)}, bf16[1,2,256,2048]{3,2,1,0:T(8,128)(2,1)S(1)}, bf16[1,256,2048]{2,1,0:T(8,128)(2,1)S(1)}, f32[4,128,1024]{2,1,0:T(8,128)S(1)}) custom-call(f32[16,128]{1,0:T(8,128)S(1)} %broadcast_in_dim.196.refs_0_, bf16[1,2,256,2048]{3,2,1,0:T(8,128)(2,1)S(1)} %get-tuple-element.160.refs_1_, ...), custom_call_target="tpu_custom_call", output_to_operand_aliasing={{1}: (2, {})} | custom-call | bytes 80000000 | tf_op jit(solution)/shard_map/pallas_call | solution.py:352
  1170.0 2.7 multiply_reduce_fusion.1
  1175.5 4.1 multiply_reduce_fusion
  1184.9 15.1 %shard_map.452 = (f32[8,128]{1,0:T(8,128)}, f32[8,24,2048]{2,1,0:T(8,128)}) custom-call(f32[8,128]{1,0:T(8,128)} %broadcast_in_dim.219.tile_ref, f32[24,2048]{1,0:T(8,128)} %get-tuple-element.225.x_ref), custom_call_target="tpu_custom_call" | custom-call | tf_op jit(solution)/shard_map/pallas_call | solution.py:511
  1203.5 7.7 multiply_subtract_fusion.3
  1211.2 4.2 multiply_subtract_fusion.2
  1216.9 3.9 multiply_subtract_fusion.1
  1228.7 4.4 multiply_subtract_fusion.4
  1234.4 4.0 multiply_subtract_fusion
  (516 shorter events, 124.8 us)
Async XLA Ops:
  2.2 135.5 %copy-start.152 = (pred[128]{0:T(512)(128)(4,1)}, pred[128]{0:T(512)(128)(4,1)S(1)}, u32[]{:S(2)}) copy-start(pred[128]{0:T(512)(128)(4,1)S(1)} %compare_bitcast_fusion) | copy-start | bytes 388
  4.0 134.3 %copy-start.127 = (f32[1,2048]{1,0:T(1,128)}, f32[1,2048]{1,0:T(1,128)S(1)}, u32[]{:S(2)}) copy-start(f32[1,2048]{1,0:T(1,128)S(1)} %get-tuple-element.262) | copy-start | bytes 24580
  89.3 48.4 %copy-start.86 = (f32[137,2048]{1,0:T(8,128)S(1)}, f32[137,2048]{1,0:T(8,128)}, u32[]{:S(2)}) copy-start(f32[137,2048]{1,0:T(8,128)} %param.34) | copy-start | bytes 3366916
  138.1 128.9 %copy-start.59 = (f32[128,2048]{1,0:T(8,128)}, f32[128,2048]{1,0:T(8,128)S(1)}, u32[]{:S(2)}) copy-start(f32[128,2048]{1,0:T(8,128)S(1)} %get-tuple-element.248) | copy-start | bytes 3145732
  138.1 46.5 %copy-start.144 = (f32[128]{0:T(128)}, f32[128]{0:T(128)S(1)}, u32[]{:S(2)}) copy-start(f32[128]{0:T(128)S(1)} %broadcast_multiply_fusion.11) | copy-start | bytes 1540
  138.3 46.2 %copy-start.154 = (f32[128]{0:T(128)}, f32[128]{0:T(128)S(1)}, u32[]{:S(2)}) copy-start(f32[128]{0:T(128)S(1)} %add_rsqrt_fusion.3) | copy-start | bytes 1540
  267.2 119.8 %copy-start.61 = (f32[128,2048]{1,0:T(8,128)}, f32[128,2048]{1,0:T(8,128)S(1)}, u32[]{:S(2)}) copy-start(f32[128,2048]{1,0:T(8,128)S(1)} %get-tuple-element.246) | copy-start | bytes 3145732
  267.2 41.6 %copy-start.146 = (f32[128]{0:T(128)}, f32[128]{0:T(128)S(1)}, u32[]{:S(2)}) copy-start(f32[128]{0:T(128)S(1)} %broadcast_multiply_fusion.10) | copy-start | bytes 1540
  267.5 41.4 %copy-start.156 = (f32[128]{0:T(128)}, f32[128]{0:T(128)S(1)}, u32[]{:S(2)}) copy-start(f32[128]{0:T(128)S(1)} %add_rsqrt_fusion.2) | copy-start | bytes 1540
  267.7 41.1 %copy-start.55 = (bf16[8,32,4096]{2,1,0:T(8,128)(2,1)S(1)}, bf16[8,32,4096]{2,1,0:T(8,128)(2,1)}, u32[]{:S(2)}) copy-start(bf16[8,32,4096]{2,1,0:T(8,128)(2,1)} %get-tuple-element.120) | copy-start | bytes 6291460
  387.3 104.5 %copy-start.63 = (f32[128,2048]{1,0:T(8,128)}, f32[128,2048]{1,0:T(8,128)S(1)}, u32[]{:S(2)}) copy-start(f32[128,2048]{1,0:T(8,128)S(1)} %get-tuple-element.244) | copy-start | bytes 3145732
  387.3 51.2 %copy-start.148 = (f32[128]{0:T(128)}, f32[128]{0:T(128)S(1)}, u32[]{:S(2)}) copy-start(f32[128]{0:T(128)S(1)} %broadcast_multiply_fusion.9) | copy-start | bytes 1540
  389.1 49.4 %copy-start.158 = (f32[128]{0:T(128)}, f32[128]{0:T(128)S(1)}, u32[]{:S(2)}) copy-start(f32[128]{0:T(128)S(1)} %add_rsqrt_fusion.1) | copy-start | bytes 1540
  492.0 21.3 %copy-start.150 = (f32[128]{0:T(128)}, f32[128]{0:T(128)S(1)}, u32[]{:S(2)}) copy-start(f32[128]{0:T(128)S(1)} %broadcast_multiply_fusion.8) | copy-start | bytes 1540
  492.3 21.0 %copy-start.160 = (f32[128]{0:T(128)}, f32[128]{0:T(128)S(1)}, u32[]{:S(2)}) copy-start(f32[128]{0:T(128)S(1)} %add_rsqrt_fusion) | copy-start | bytes 1540
  492.5 20.8 %copy-start.172 = (bf16[2,2,4,64,2048]{4,3,2,1,0:T(8,128)(2,1)S(1)}, bf16[2,2,4,64,2048]{4,3,2,1,0:T(8,128)(2,1)}, u32[]{:S(2)}) copy-start(bf16[2,2,4,64,2048]{4,3,2,1,0:T(8,128)(2,1)} %get-tuple-element.103) | copy-start | bytes 12582916
  519.6 16.0 %copy-start.102 = (bf16[8,128,128]{1,2,0:T(8,128)(2,1)S(1)}, bf16[8,128,128]{1,2,0:T(8,128)(2,1)}, u32[]{:S(2)}) copy-start(bf16[8,128,128]{1,2,0:T(8,128)(2,1)} %copy-done.101) | copy-start | bytes 786436
  519.6 16.0 %copy-start.104 = (bf16[8,128,128]{1,2,0:T(8,128)(2,1)S(1)}, bf16[8,128,128]{1,2,0:T(8,128)(2,1)}, u32[]{:S(2)}) copy-start(bf16[8,128,128]{1,2,0:T(8,128)(2,1)} %copy-done.103) | copy-start | bytes 786436
  530.0 6.3 collective-permute-start
  536.3 5.8 collective-permute-start.1
  547.3 9.6 copy-start.173
  561.4 40.0 %copy-start.151 = (f32[128]{0:T(128)S(1)}, f32[128]{0:T(128)}, u32[]{:S(2)}) copy-start(f32[128]{0:T(128)} %copy-done.150) | copy-start | bytes 1540
  561.4 40.0 %copy-start.161 = (f32[128]{0:T(128)S(1)}, f32[128]{0:T(128)}, u32[]{:S(2)}) copy-start(f32[128]{0:T(128)} %copy-done.160) | copy-start | bytes 1540
  603.8 23.1 %copy-start.58 = (bf16[1024,1024]{1,0:T(8,128)(2,1)S(1)}, bf16[1024,1024]{1,0:T(8,128)(2,1)}, u32[]{:S(2)}) copy-start(bf16[1024,1024]{1,0:T(8,128)(2,1)} %copy-done.57) | copy-start | bytes 6291460
  626.9 9.6 copy-start.31
  626.9 9.6 copy-start.34
  636.5 22.5 %copy-start.7 = (bf16[1,2,256,2048]{3,2,1,0:T(8,128)(2,1)}, bf16[1,2,256,2048]{3,2,1,0:T(8,128)(2,1)S(1)}, u32[]{:S(2)}) copy-start(bf16[1,2,256,2048]{3,2,1,0:T(8,128)(2,1)S(1)} %get-tuple-element.132.refs_1_.refs_3_) | copy-start | bytes 6291460
  645.8 8.6 copy-start.5
  659.0 40.2 %copy-start.64 = (f32[128,2048]{1,0:T(8,128)S(1)}, f32[128,2048]{1,0:T(8,128)}, u32[]{:S(2)}) copy-start(f32[128,2048]{1,0:T(8,128)} %copy-done.63) | copy-start | bytes 3145732
  659.0 40.2 %copy-start.149 = (f32[128]{0:T(128)S(1)}, f32[128]{0:T(128)}, u32[]{:S(2)}) copy-start(f32[128]{0:T(128)} %copy-done.148) | copy-start | bytes 1540
  659.1 40.2 %copy-start.159 = (f32[128]{0:T(128)S(1)}, f32[128]{0:T(128)}, u32[]{:S(2)}) copy-start(f32[128]{0:T(128)} %copy-done.158) | copy-start | bytes 1540
  704.1 33.8 %copy-start.94 = (bf16[1,2,2,64,2048]{4,3,2,1,0:T(8,128)(2,1)S(1)}, bf16[1,2,2,64,2048]{4,3,2,1,0:T(8,128)(2,1)}, u32[]{:S(2)}) copy-start(bf16[1,2,2,64,2048]{4,3,2,1,0:T(8,128)(2,1)} %copy-done.93) | copy-start | bytes 3145732
  759.3 80.1 %copy-start.45 = (bf16[1,8,128,256]{3,2,1,0:T(8,128)(2,1)}, bf16[1,8,128,256]{3,2,1,0:T(8,128)(2,1)S(1)}, u32[]{:S(2)}) copy-start(bf16[1,8,128,256]{3,2,1,0:T(8,128)(2,1)S(1)} %get-tuple-element.147.refs_5_.refs_3_) | copy-start | bytes 1572868
  767.5 68.4 %copy-start.62 = (f32[128,2048]{1,0:T(8,128)S(1)}, f32[128,2048]{1,0:T(8,128)}, u32[]{:S(2)}) copy-start(f32[128,2048]{1,0:T(8,128)} %copy-done.61) | copy-start | bytes 3145732
  767.5 68.4 %copy-start.147 = (f32[128]{0:T(128)S(1)}, f32[128]{0:T(128)}, u32[]{:S(2)}) copy-start(f32[128]{0:T(128)} %copy-done.146) | copy-start | bytes 1540
  767.5 68.4 %copy-start.157 = (f32[128]{0:T(128)S(1)}, f32[128]{0:T(128)}, u32[]{:S(2)}) copy-start(f32[128]{0:T(128)} %copy-done.156) | copy-start | bytes 1540
  839.3 33.9 %copy-start.119 = (bf16[1,2,2,64,2048]{4,3,2,1,0:T(8,128)(2,1)S(1)}, bf16[1,2,2,64,2048]{4,3,2,1,0:T(8,128)(2,1)}, u32[]{:S(2)}) copy-start(bf16[1,2,2,64,2048]{4,3,2,1,0:T(8,128)(2,1)} %get-tuple-element.251) | copy-start | bytes 3145732
  902.1 68.3 %copy-start.60 = (f32[128,2048]{1,0:T(8,128)S(1)}, f32[128,2048]{1,0:T(8,128)}, u32[]{:S(2)}) copy-start(f32[128,2048]{1,0:T(8,128)} %copy-done.59) | copy-start | bytes 3145732
  902.1 68.3 %copy-start.128 = (f32[1,2048]{1,0:T(1,128)S(1)}, f32[1,2048]{1,0:T(1,128)}, u32[]{:S(2)}) copy-start(f32[1,2048]{1,0:T(1,128)} %copy-done.127) | copy-start | bytes 24580
  902.1 68.3 %copy-start.145 = (f32[128]{0:T(128)S(1)}, f32[128]{0:T(128)}, u32[]{:S(2)}) copy-start(f32[128]{0:T(128)} %copy-done.144) | copy-start | bytes 1540
  902.1 68.3 %copy-start.155 = (f32[128]{0:T(128)S(1)}, f32[128]{0:T(128)}, u32[]{:S(2)}) copy-start(f32[128]{0:T(128)} %copy-done.154) | copy-start | bytes 1540
  1042.1 10.7 copy-start.70
  1042.1 10.7 copy-start.72
  1104.9 68.6 %collective-permute-start.2 = (f32[24,2048]{1,0:T(8,128)}, f32[24,2048]{1,0:T(8,128)}, u32[]{:S(2)}, u32[]{:S(2)}) collective-permute-start(f32[24,2048]{1,0:T(8,128)} %get-tuple-element.178), channel_id=1, source_target_pairs={{0,16},{16,0},{1,17},{17,1},{2,18},{18,2},{3,19},{19,3},{4,20},{20... | collective-permute-start | bytes 589832 | tf_op jit(solution)/shard_map/ppermute | solution.py:554
  1166.3 9.2 copy-start.16
  1166.3 9.2 copy-start.40
  1174.5 7.2 collective-permute-start.3
  1203.4 7.8 copy-start.20
  (130 other events, 386.6 us)

commit v3 on v2

--- a/solution.py
+++ b/solution.py
@@ -1,3 +1,4 @@
+import math
 from functools import partial
 
 import jax
@@ -46,7 +47,7 @@
     return dot(x, y, ((0,), (0,)))
 
 
-SHARE, RING, SWAP, EXCHANGE = range(4)
+SHARE, RING, SWAP, EXCHANGE, GRAD, PRODUCT = range(6)
 START, FAR, THROUGH = range(3)
 GATHER, SCATTER = range(2)
 
@@ -205,37 +206,130 @@
     ]
 
 
+def by_rows(start, count, body):
+    step = 16 if start % 16 == 0 and count % 16 == 0 else 8
+
+    def some(k, carry):
+        body(lambda origin=0: pl.ds(pl.multiple_of(start - origin + k * step, step), step))
+        return carry
+
+    lax.fori_loop(0, count // step, some, 0)
+
+
 def scatter_rest(here, p_ref, o_ref, cut, pairs, paired, held, from_b, from_e, last_b, last_e):
     b, e, c = here.b, here.e, here.c
-    first, second = pl.ds(0, cut), pl.ds(cut, o_ref.shape[0] - cut)
-    pairs[0].wait_recv()
-    held[0] = p_ref[place(1 - b, 1 - e, c)] + paired[0]
-    e_first = here.copy(held.at[0, second], from_e.at[0], here.to_e, hold=True)
+    count = o_ref.shape[0]
+    rest = count - cut
+    parts = 2 if cut < rest and rest % 32 == 0 else 1
+    chunks = [(cut + k * (rest // parts), rest // parts) for k in range(parts)]
+    first, second = pl.ds(0, cut), pl.ds(cut, rest)
+
+    def pair(k, target, spot):
+        pairs[k].wait_recv()
+
+        def body(at):
+            target[at()] = p_ref[spot, at()] + paired[k, at()]
+
+        by_rows(0, count, body)
+
+    def add(start, size, target, source, origin):
+        def body(at):
+            target[at()] = target[at()] + source[at(origin)]
+
+        by_rows(start, size, body)
+
+    def first_over_e(k):
+        start, size = chunks[k]
+        target = from_e.at[0, pl.ds(start - cut, size)]
+        return here.copy(held.at[0, pl.ds(start, size)], target, here.to_e, hold=True)
+
+    pair(0, held.at[0], place(1 - b, 1 - e, c))
+    moving = first_over_e(0)
     b_first = here.copy(held.at[0, first], from_b.at[0], here.to_b, hold=True)
-    pairs[2].wait_recv()
-    held[2] = p_ref[place(b, 1 - e, c)] + paired[2]
-    pairs[1].wait_recv()
-    held[1] = p_ref[place(1 - b, e, c)] + paired[1]
-    pairs[3].wait_recv()
-    o_ref[...] = p_ref[place(b, e, c)] + paired[3]
+    pair(2, held.at[2], place(b, 1 - e, c))
+    pair(1, held.at[1], place(1 - b, e, c))
+    pair(3, o_ref, place(b, e, c))
     b_first.wait_send()
     b_second = here.copy(held.at[1, first], from_b.at[1], here.to_b)
-    e_first.wait_send()
-    e_second = here.copy(held.at[2, second], from_e.at[1], here.to_e)
-    e_first.wait_recv()
-    held[1, second] = held[1, second] + from_e[0]
-    b_third = here.copy(held.at[1, second], last_b, here.to_b)
+    thirds = []
+    for k, (start, size) in enumerate(chunks):
+        moving.wait_send()
+        came = moving
+        if k + 1 < parts:
+            moving = first_over_e(k + 1)
+        else:
+            e_second = here.copy(held.at[2, second], from_e.at[1], here.to_e)
+        came.wait_recv()
+        add(start, size, held.at[1], from_e.at[0], cut)
+        piece = pl.ds(start, size)
+        thirds.append(
+            here.copy(held.at[1, piece], last_b.at[pl.ds(start - cut, size)], here.to_b)
+        )
     b_first.wait_recv()
-    held[2, first] = held[2, first] + from_b[0]
+    add(0, cut, held.at[2], from_b.at[0], 0)
     e_third = here.copy(held.at[2, first], last_e, here.to_e)
     b_second.wait_recv()
-    o_ref[first] = o_ref[first] + from_b[1]
+    add(0, cut, o_ref, from_b.at[1], 0)
     e_second.wait_recv()
-    o_ref[second] = o_ref[second] + from_e[1]
+    add(cut, rest, o_ref, from_e.at[1], cut)
     e_third.wait_recv()
-    o_ref[first] = o_ref[first] + last_e[...]
-    b_third.wait_recv()
-    o_ref[second] = o_ref[second] + last_b[...]
+    add(0, cut, o_ref, last_e, 0)
+    for made, (start, size) in zip(thirds, chunks):
+        made.wait_recv()
+        add(start, size, o_ref, last_b, cut)
+
+
+def ring_start(here, halves, source, out):
+    lead = source.shape[1]
+    for half in halves:
+        row, count = {0: (1 - here.a, lead // 2), 1: (here.a, lead // 2)}[half]
+        for step, peer in enumerate(here.to_d):
+            part = pl.ds(row * count, count)
+            here.late(here.copy(source.at[step, part], out.at[step, part], peer))
+
+
+def columns_of(right):
+    wide = min(right.shape[1], 1024)
+    return wide, right.shape[1] // wide
+
+
+def grad_in_kernel(here, rows, left, right, keep, wire):
+    lead, extent = keep.shape[0], here.extent
+    deep = rows * extent
+    wide, blocks = columns_of(right)
+
+    def some(k, carry):
+        along = pl.ds(pl.multiple_of(k // blocks * deep, 128), deep)
+        across = pl.ds(pl.multiple_of(lax.rem(k, blocks) * wide, 128), wide)
+        value = tn(left[:, along], right[:, across])
+        for column in range(extent):
+            part = value[column * rows : (column + 1) * rows]
+            step = lax.rem(column - here.d + extent, extent)
+
+            @pl.when(step == 0)
+            def _():
+                keep[k // blocks, :, across] = part
+
+            @pl.when(step > 0)
+            def _():
+                wire[step - 1, k // blocks, :, across] = part.astype(wire.dtype)
+
+        return carry
+
+    lax.fori_loop(0, lead * blocks, some, 0)
+
+
+def product_in_kernel(left, right, out):
+    wide, blocks = columns_of(right)
+    deep = 512
+
+    def some(k, carry):
+        along = pl.ds(pl.multiple_of(k // blocks * deep, 128), deep)
+        across = pl.ds(pl.multiple_of(lax.rem(k, blocks) * wide, 128), wide)
+        out[along, across] = tn(left[:, along], right[:, across])
+        return carry
+
+    lax.fori_loop(0, left.shape[1] // deep * blocks, some, 0)
 
 
 def group_kernel(kind, cut, plan, extent, in_count, out_count, *refs):
@@ -251,7 +345,7 @@
         for entry in plan
     ):
         peers.append(here.to_a)
-    if any(entry[0] in (SHARE, RING) for entry in plan):
+    if any(entry[0] in (SHARE, RING, GRAD) for entry in plan):
         peers.extend(here.to_d)
     here.greet(peers)
     if kind == GATHER:
@@ -260,6 +354,8 @@
         started = scatter_start(here, x_ref, scratch[3])
     through = []
     for entry in plan:
+        if entry[0] in (GRAD, PRODUCT):
+            continue
         source, out = ins.pop(0), outs.pop(0)
         if entry[3]:
             ins.pop(0)
@@ -274,18 +370,21 @@
                     else:
                         here.late(across)
         elif entry[0] == RING:
-            lead = source.shape[1]
-            for half in entry[2]:
-                row, count = {0: (1 - here.a, lead // 2), 1: (here.a, lead // 2), 2: (0, lead)}[half]
-                for step, peer in enumerate(here.to_d):
-                    part = pl.ds(row * count, count)
-                    here.late(here.copy(source.at[step, part], out.at[step, part], peer))
+            ring_start(here, entry[2], source, out)
         elif entry[0] == SWAP:
             for first, count in entry[2]:
                 part = pl.ds(first, count)
                 here.late(here.copy(source.at[part], out.at[part], here.to_a))
         else:
             here.waits.extend(exchange_start(here, source, out, entry[1]))
+    for entry in plan:
+        if entry[0] == GRAD:
+            left, right = ins.pop(0), ins.pop(0)
+            keep, wire, out = outs.pop(0), outs.pop(0), outs.pop(0)
+            grad_in_kernel(here, entry[1], left, right, keep, wire)
+            ring_start(here, entry[2], wire, out)
+        elif entry[0] == PRODUCT:
+            product_in_kernel(ins.pop(0), ins.pop(0), outs.pop(0))
     if kind == GATHER:
         gather_rest(here, o_ref, cut, started)
     else:
@@ -310,6 +409,14 @@
 
 def exchange(pieces, width=0):
     return (EXCHANGE, width, (), pieces, None)
+
+
+def grad(left, right, rows, wire):
+    return (GRAD, rows, (0,), (left, right, wire), None)
+
+
+def product(left, right):
+    return (PRODUCT, 0, (), (left, right), None)
 
 
 def group_call(kind, x, number, *moves, cut=2):
@@ -326,8 +433,30 @@
         first, second = (cut,) + shape[1:], (shape[0] - cut,) + shape[1:]
         sizes = ((4,) + shape, (3,) + shape, (2,) + first, (2,) + second, second, first)
         scratch = [pltpu.VMEM(size, x.dtype) for size in sizes]
-    operands, outs, aliases, plan, copies, locals_ = [x], [out], {}, [], 13, 2
-    for what, mode, actions, source, array in moves:
+    operands, outs, aliases, plan, copies, locals_ = [x], [out], {}, [], 16, 2
+    anywhere, vmem = pl.BlockSpec(memory_space=pl.ANY), pl.BlockSpec(memory_space=pltpu.VMEM)
+    in_specs, out_specs = [pl.BlockSpec(memory_space=space)], [pl.BlockSpec(memory_space=space)]
+    worked = {}
+    for place_of, (what, mode, actions, source, array) in enumerate(moves):
+        if what == GRAD and mode % 128:
+            worked[place_of] = weight_grad(source[0], source[1], mode, source[2])
+            what, source = RING, worked[place_of][1]
+        if what in (GRAD, PRODUCT):
+            operands.extend(source[:2])
+            in_specs.extend([vmem, vmem])
+            rows, columns = source[0].shape[1], source[1].shape[1]
+            if what == PRODUCT:
+                outs.append(jax.ShapeDtypeStruct((rows, columns), F32))
+                out_specs.append(vmem)
+            else:
+                lead = rows // (mode * extent)
+                pieces = jax.ShapeDtypeStruct((extent - 1, lead, mode, columns), source[2])
+                outs.append(jax.ShapeDtypeStruct((lead, mode, columns), F32))
+                outs.extend([pieces, pieces])
+                out_specs.extend([vmem, vmem, anywhere])
+            plan.append((what, mode, actions, False))
+            copies += 2 * extent
+            continue
         operands.append(source)
         if array is not None:
             aliases[len(operands)] = len(outs)
@@ -345,15 +474,25 @@
             locals_ += parts
         else:
             outs.append(jax.ShapeDtypeStruct(source.shape, source.dtype))
+        in_specs.extend([anywhere] * (len(operands) - len(in_specs)))
+        out_specs.append(anywhere)
         plan.append((what, mode, actions, array is not None))
         copies += 3 + 2 * extent * len(actions)
         locals_ += 1 + len(actions)
-    anywhere = pl.BlockSpec(memory_space=pl.ANY)
+    held = [ref for ref in scratch] + [
+        ref for ref, spec in zip(operands + outs, in_specs + out_specs) if spec is vmem
+    ]
+    room = 6 << 20 if any(entry[0] in (GRAD, PRODUCT) for entry in plan) else 1 << 20
+    if kind == SCATTER:
+        held.extend([x, out])
+    room += sum(math.prod(ref.shape) * jnp.dtype(ref.dtype).itemsize for ref in held)
+    order = [k for k, entry in enumerate(plan) if entry[0] not in (GRAD, PRODUCT)]
+    assert order == list(range(len(order)))
     results = pl.pallas_call(
         partial(group_kernel, kind, cut, plan, extent, len(operands), len(outs)),
         out_shape=tuple(outs),
-        in_specs=[pl.BlockSpec(memory_space=space)] + [anywhere] * (len(operands) - 1),
-        out_specs=tuple([pl.BlockSpec(memory_space=space)] + [anywhere] * (len(outs) - 1)),
+        in_specs=in_specs,
+        out_specs=tuple(out_specs),
         scratch_shapes=[
             pltpu.SemaphoreType.DMA((copies,)),
             pltpu.SemaphoreType.DMA((copies,)),
@@ -362,13 +501,18 @@
         + scratch,
         input_output_aliases=aliases,
         compiler_params=pltpu.CompilerParams(
-            collective_id=number, has_side_effects=True, vmem_limit_bytes=40 << 20
+            collective_id=number, has_side_effects=True, vmem_limit_bytes=room
         ),
         cost_estimate=pl.CostEstimate(
             flops=0, bytes_accessed=80_000_000, transcendentals=0
         ),
     )(*operands)
-    return results[0] if not moves else results
+    if not moves:
+        return results[0]
+    results = list(results)
+    for place_of, (keep, pieces) in worked.items():
+        results[place_of + 1 : place_of + 1] = [keep, pieces]
+    return tuple(results)
 
 
 def first_kernel(extent, *refs):
@@ -382,17 +526,22 @@
     units, rows = table_block.shape[:2]
 
     def table_unit(k):
-        table_block[k] = table_ref[pl.ds(k * rows, rows)].astype(BF16)
+        def body(at):
+            table_block[k, at(k * rows)] = table_ref[at()].astype(BF16)
+
+        by_rows(k * rows, rows, body)
         return share_start(here, table_block, table, 0, k, 1)
 
     def by_head(source, target):
-        kinds = source.shape[0]
-        for q in range(4):
-            for kind in range(kinds):
-                for row in range(2):
-                    target[q, :, pl.ds((kind * 2 + row) * HD, HD)] = source[
-                        kind, :, pl.ds((row * 4 + q) * HD, HD)
-                    ].astype(BF16)
+        def body(at):
+            for q in range(4):
+                for kind in range(source.shape[0]):
+                    for row in range(2):
+                        target[q, at(), pl.ds((kind * 2 + row) * HD, HD)] = source[
+                            kind, at(), pl.ds((row * 4 + q) * HD, HD)
+                        ].astype(BF16)
+
+        by_rows(0, source.shape[1], body)
 
     across = [table_unit(0), table_unit(1), table_unit(2)]
     small_started = gather_start(here, small, small_out, small.shape[0] // 2)
@@ -413,14 +562,22 @@
         elif k == 1:
             gather_rest(here, text_out, text.shape[0] // 2, text_started)
             width = expand_ref.shape[1] // 8
-            for q in range(4):
-                for row in range(2):
-                    expand_pieces[q, :, pl.ds(row * width, width)] = expand_ref[
-                        :, pl.ds((row * 4 + q) * width, width)
-                    ].astype(BF16)
+
+            def body(at):
+                for q in range(4):
+                    for row in range(2):
+                        expand_pieces[q, at(), pl.ds(row * width, width)] = expand_ref[
+                            at(), pl.ds((row * 4 + q) * width, width)
+                        ].astype(BF16)
+
+            by_rows(0, expand_ref.shape[0], body)
         elif k == 2:
             for unit in range(units):
-                contract_block[unit] = contract_ref[pl.ds(unit * rows, rows)].astype(BF16)
+
+                def body(at):
+                    contract_block[unit, at(unit * rows)] = contract_ref[at()].astype(BF16)
+
+                by_rows(unit * rows, rows, body)
     across[units].wait_recv()
     share_far(here, outs, 2, 0, 1)
     here.finish()
@@ -626,31 +783,6 @@
     )(lax.axis_index(DX).reshape(1), *operands)
 
 
-def product_kernel(left_ref, right_ref, out_ref):
-    out_ref[...] = tn(left_ref[...], right_ref[...])
-
-
-def product(left, right):
-    count, columns = right.shape
-    deep, wide = left.shape[1] // 2, columns // 2
-    return pl.pallas_call(
-        product_kernel,
-        out_shape=jax.ShapeDtypeStruct((left.shape[1], columns), F32),
-        grid=(2, 2),
-        in_specs=[
-            pl.BlockSpec((count, deep), lambda k, j: (0, k)),
-            pl.BlockSpec((count, wide), lambda k, j: (0, j)),
-        ],
-        out_specs=pl.BlockSpec((deep, wide), lambda k, j: (k, j)),
-        compiler_params=pltpu.CompilerParams(vmem_limit_bytes=48 << 20),
-        cost_estimate=pl.CostEstimate(
-            flops=2 * count * left.shape[1] * columns,
-            bytes_accessed=left.size * 2 + right.size * 2 + left.shape[1] * columns * 4,
-            transcendentals=0,
-        ),
-    )(left, right)
-
-
 def total_at(index, keep, pieces):
     total = pick(keep.reshape((2, -1) + keep.shape[1:]), index, 0)
     for step in range(pieces.shape[0]):
@@ -684,6 +816,57 @@
         - normed * jnp.mean(inner * normed, -1, keepdims=True)
     )
     return back, jnp.sum(upstream * normed, 0), jnp.sum(upstream, 0)
+
+
+def each_head(per, query_rows, key_rows):
+    for image in range(per):
+        for head in range(2):
+            columns = pl.ds(head * HD, HD)
+            yield pl.ds(image * query_rows, query_rows), pl.ds(image * key_rows, key_rows), columns
+
+
+def probabilities(query, key):
+    scores = nt(query, key) * SCALE
+    top = jnp.max(scores, -1, keepdims=True)
+    logsum = top + jnp.log(jnp.sum(jnp.exp(scores - top), -1, keepdims=True))
+    return jnp.exp(scores - logsum)
+
+
+def attend_back_kernel(per, g_ref, q_ref, k_ref, v_ref, o_ref):
+    sizes = q_ref.shape[0] // per, k_ref.shape[0] // per
+    for rows, key_rows, columns in each_head(per, *sizes):
+        grad_out = g_ref[rows, columns]
+        query, key, value = q_ref[rows, columns], k_ref[key_rows, columns], v_ref[key_rows, columns]
+        probs = probabilities(query, key)
+        grad_probs = nt(grad_out, value)
+        inner = jnp.sum(probs * grad_probs, -1, keepdims=True)
+        grad_scores = (probs * (grad_probs - inner)).astype(BF16)
+        grads = (
+            nn(grad_scores, key) * SCALE,
+            tn(grad_scores, query) * SCALE,
+            tn(probs.astype(BF16), grad_out),
+        )
+        for kind, grad in enumerate(grads):
+            o_ref[rows, pl.ds(kind * 2 * HD + columns.start, HD)] = grad.astype(BF16)
+
+
+def attend_back_joint(upstream, triple, images):
+    per = 2 if images % 2 == 0 else 1
+    rows = triple.shape[0] // images * per
+
+    def spec(kind, kinds=1):
+        return pl.BlockSpec((rows, kinds * 2 * HD), lambda k: (k, kind))
+
+    return pl.pallas_call(
+        partial(attend_back_kernel, per),
+        out_shape=jax.ShapeDtypeStruct(triple.shape, BF16),
+        grid=(images // per,),
+        in_specs=[spec(0), spec(0), spec(1), spec(2)],
+        out_specs=spec(0, 3),
+        cost_estimate=pl.CostEstimate(
+            flops=20 * triple.shape[0] * HD * HD, bytes_accessed=1 << 22, transcendentals=1 << 18
+        ),
+    )(upstream, triple, triple, triple)
 
 
 def dot_images(x, y, x_side, y_side):
@@ -823,7 +1006,7 @@
     queries, keys, values = (
         heads(triple[:, k : k + pair], images) for k in (0, pair, 2 * pair)
     )
-    attn_one, probs_one = attend(queries, keys, values)
+    attn_one, unused = attend(queries, keys, values)
     part = nn(attn_one, outs[0].reshape(pair, width))
     back, w_text, outs = collect(
         part,
@@ -897,25 +1080,24 @@
     grad_three, gain_six, gain_seven = norm_back(upstream, norm_four, norm_rows[6])
     branch_three = spread(grad_three.astype(BF16), 9)
 
-    contract_keep, contract_wire = weight_grad(hidden, branch_three, block, BF16)
     hidden_grad = nt(branch_three, contract)
     gelu_pull = jax.vjp(partial(jax.nn.gelu, approximate=True), preact)[1]
     preact_grad = gelu_pull(hidden_grad)[0].astype(BF16)
-    expand_keep, expand_wire = weight_grad(a_three, preact_grad, in_rows, BF16)
     part = nt(preact_grad, expand)
-    back, contract_came = collect(part, 11, ring((0,), contract_wire))
+    back, contract_keep, contract_wire, contract_came = collect(
+        part, 11, grad(hidden, branch_three, block, BF16)
+    )
 
     back, gain_four, gain_five = norm_back(back, norm_three, norm_rows[4])
     grad_two = grad_three + back
     branch_two = grad_two.astype(BF16) * keep_rows.astype(BF16)
-    table_head = product(logit_grad, a_four)
     contract_half = other_half(contract_keep, contract_came, BF16)
     contract_half = contract_half.reshape(2, block // 2, width)
-    branch_two, expand_came, contract_across = spread(
-        after(branch_two, table_head),
+    branch_two, contract_across, expand_keep, expand_wire, expand_came = spread(
+        branch_two,
         12,
-        ring((0,), expand_wire),
         swap(((0, 1),), contract_half),
+        grad(a_three, preact_grad, in_rows, BF16),
         cut=4,
     )
     attn_grad = nt(branch_two, out_maps[1]).astype(BF16)
@@ -923,49 +1105,45 @@
         attn_grad, cross, text_keys, text_values, probs_two, images
     )
     pair_grad = jnp.concatenate([key_grad, value_grad], 1)
-    text_keep, text_wire = weight_grad(group_captions, pair_grad, text_rows, WIRE)
     expand_half = other_half(expand_keep, expand_came, BF16)
     part = nt(cross_grad, w_cross)
-    back, contract_across, contract_came, expand_across, text_came = collect(
+    back, contract_across, contract_came, expand_across, text_keep, text_wire, text_came = collect(
         part,
         13,
         swap(((1, 1),), contract_half, contract_across),
         ring((1,), contract_wire, contract_came),
         swap(((0, 2),), expand_half),
-        ring((0,), text_wire),
+        grad(group_captions, pair_grad, text_rows, WIRE),
         cut=4,
     )
 
     back, gain_two, gain_three = norm_back(back, norm_two, norm_rows[2])
     grad_one = grad_two + back
-    cross_keep, cross_wire = weight_grad(a_two, cross_grad, in_rows, WIRE)
-    branch_one, expand_across, expand_came, cross_came = spread(
-        after(grad_one.astype(BF16), cross_keep),
+    branch_one, expand_across, expand_came, cross_keep, cross_wire, cross_came, table_head = spread(
+        grad_one.astype(BF16),
         14,
         swap(((2, 2),), expand_half, expand_across),
         ring((1,), expand_wire, expand_came),
-        ring((0,), cross_wire),
+        grad(a_two, cross_grad, in_rows, WIRE),
+        product(logit_grad, a_four),
         cut=4,
     )
     attn_grad = nt(branch_one, out_maps[0]).astype(BF16)
-    triple_grad = jnp.concatenate(
-        attend_back(attn_grad, queries, keys, values, probs_one, images), 1
-    )
+    triple_grad = attend_back_joint(attn_grad, triple, images)
     out_one = weight_grad(attn_one, branch_one, HD // extent, BF16)
     out_two = weight_grad(attn_two, branch_two, HD // extent, BF16)
     out_keep = jnp.stack([out_one[0], out_two[0]], 1)
     out_wire = jnp.stack([out_one[1], out_two[1]], 2)
     text_half = other_half(text_keep, text_came, WIRE)
-    triple_keep, triple_wire = weight_grad(a_one, triple_grad, in_rows, WIRE)
     part = nt(triple_grad, w_qkv)
     out_wire = plain(out_wire)
-    back, text_across, text_came, out_came, triple_came = collect(
+    back, text_across, text_came, out_came, triple_keep, triple_wire, triple_came = collect(
         part,
         15,
         swap(((0, 4),), text_half),
         ring((1,), text_wire, text_came),
         ring((0,), out_wire),
-        ring((0,), triple_wire),
+        grad(a_one, triple_grad, in_rows, WIRE),
         cut=4,
     )
 

time: 1250 us -> 1220 us (0.976)
  Pallas kernels: 999 us -> 959 us
    pallas_call x6 -> x1, Pallas kernels: 45.2 us -> 11 us  [weight_grad(): pl.pallas_call(partial(grad_kernel, base is not None, extent, rows), out_...]
    unnamed x349 -> x373, local copies, waits for them, and re-layouts: 41.1 us -> 45.4 us
  transfers between devices with their start and end apart: 4 -> 4, of which waited for: 1 -> 1; matrix products, arithmetic and copies ran while one was open for 2% -> 3% of each run, Pallas kernels for 4% -> 4%
where the time goes in v3:
time: 1220 us; the launch traced here: 1210 us
  Pallas kernels  959 us (79%)
  other arithmetic  78.9 us (6%)
  matrix products  78.9 us (6%)
  local copies, waits for them, and re-layouts  67.3 us (6%)
  between operations  12.8 us (1%)
    pallas_call x19, Pallas kernels, group_call(): pl.pallas_call(partial(group_kernel, kind, cut, plan, extent, len(operand...  846 us
    pallas_call x1, Pallas kernels, first_call(): pl.pallas_call(partial(first_kernel, extent), out_shape=tuple(out_shape),...  76.9 us
    dot_general x18, matrix products, dot(): return lax.dot_general(x, y, (dims, ((), ())), preferred_element_type=F32)  73.5 us
    unnamed x373, local copies, waits for them, and re-layouts  45.4 us
    sub x7, other arithmetic, adamw(): return (master - rate * (update + decay * master), first_new, second_new)  28.8 us
  transfers between devices with their start and end apart: 4, of which 1 were waited for; matrix products, arithmetic and copies ran while one was open for 3% of the time, Pallas kernels for 4%

profile of v3, /device:TPU:0, one launch (start us, length us, event | category | flops | bytes accessed | tf_op | source)
XLA Modules:
  0.0 1205.9 jit_solution(4563345798352901838)
XLA Ops:
  5.4 76.9 %shard_map.425 = (s32[8,16,128]{2,1,0:T(8,128)S(1)}, bf16[8,32,4096]{2,1,0:T(8,128)(2,1)}, bf16[4,128,1024]{2,1,0:T(8,128)(2,1)S(1)}, bf16[2,2,4,64,2048]{4,3,2,...) custom-call(s32[16,128]{1,0:T(8,128)S(1)} %pad_bitcast_fusion.refs_0, ...), custom_call_target="tpu_custom_call" | custom-call | tf_op jit(solution)/shard_map/pallas_call | solution.py:609
  82.3 7.1 fusion.9
  89.4 51.5 %shard_map.426 = (bf16[128,2048]{1,0:T(8,128)(2,1)S(1)}, bf16[2,4,2,128,1024]{4,3,2,1,0:T(8,128)(2,1)S(1)}, bf16[4,256,512]{2,1,0:T(8,128)(2,1)S(1)}) custom-call(bf16[8,128,2048]{2,1,0:T(8,128)(2,1)S(1)} %bitcast.302, bf16[4,128,1024]{2,1,0:T(8,128)(2,1)S(1)} %get-tuple-element.103.refs_1_, bf16[4,256,512]{2,1,0:T(8,128)(2,1)S(1)} %get-tuple-element.104.refs_2_), custom_call_target="tpu_custom_call" | custom-call | bytes 80000000 | tf_op jit(solution)/shard_map/pallas_call | solution.py:491
  141.8 43.5 %shard_map.427 = (bf16[8,128,2048]{2,1,0:T(8,128)(2,1)S(1)}, bf16[2,4,2,128,1024]{4,3,2,1,0:T(8,128)(2,1)S(1)}, bf16[2,4,2,256,512]{4,3,2,1,0:T(8,128)(2,1)S(1)}, bf16[4,128,1024]{2,1,0:T(8,128)(2,1)S(1)}) custom-call(bf16[128,2048]{1,0:T(8,128)(2,1)S(1)} %add_convert_fusion.6.refs_0_, ...), custom_call_target="tpu_custom_call", output_to_operand_aliasing={{1}: (2, {})} | custom-call | bytes 80000000 | tf_op jit(solution)/shard_map/pallas_call | solution.py:491
  185.4 3.4 fusion.24.q_ref.k_ref.v_ref
  193.2 62.4 %shard_map.428 = (f32[128,2048]{1,0:T(8,128)S(1)}, bf16[2,4,2,256,512]{4,3,2,1,0:T(8,128)(2,1)S(1)}, bf16[2,2,2,64,2048]{4,3,2,1,0:T(8,128)(2,1)S(1)}) custom-call(f32[8,128,2048]{2,1,0:T(8,128)S(1)} %fusion.118.refs_0_, bf16[4,256,512]{2,1,0:T(8,128)(2,1)S(1)} %get-tuple-element.107.refs_3_.refs_1_, ...), custom_call_target="tpu_custom_call", output_to_operand_aliasing={{1}: (2, {}), {2}: (4, {})} | custom-call | bytes 80000000 | tf_op jit(solution)/shard_map/pallas_call | solution.py:491
  256.4 37.9 %shard_map.429 = (bf16[8,128,2048]{2,1,0:T(8,128)(2,1)S(1)}, bf16[2,4,2,256,512]{4,3,2,1,0:T(8,128)(2,1)S(1)}, bf16[2,2,2,64,2048]{4,3,2,1,0:T(8,128)(2,1)S(1)}, bf16[2,4,2,128,1024]{4,3,2,1,0:T(8,128)(2,1)S(1)}) custom-call(bf16[128,2048]{1,0:T(8,128)(2,1)S(1)} %add_convert_fusion.5.refs_0_, ...), custom_call_target="tpu_custom_call", output_to_operand_aliasing={{1}: (2, {}), {2}: (4, {})} | custom-call | bytes 80000000 | tf_op jit(solution)/shard_map/pallas_call | solution.py:491
  301.5 63.6 %shard_map.430 = (f32[128,2048]{1,0:T(8,128)S(1)}, bf16[2,4,2,128,1024]{4,3,2,1,0:T(8,128)(2,1)S(1)}, bf16[2,2,4,64,2048]{4,3,2,1,0:T(8,128)(2,1)S(1)}) custom-call(f32[8,128,2048]{2,1,0:T(8,128)S(1)} %fusion.117.refs_0_, bf16[4,128,1024]{2,1,0:T(8,128)(2,1)S(1)} %get-tuple-element.117.refs_5_.refs_1_, ...), custom_call_target="tpu_custom_call", output_to_operand_aliasing={{1}: (2, {})} | custom-call | bytes 80000000 | tf_op jit(solution)/shard_map/pallas_call | solution.py:491
  366.0 47.5 %shard_map.431 = (bf16[8,128,2048]{2,1,0:T(8,128)(2,1)S(1)}, bf16[2,4,2,128,1024]{4,3,2,1,0:T(8,128)(2,1)S(1)}, bf16[2,2,4,64,2048]{4,3,2,1,0:T(8,128)(2,1)S(1)}) custom-call(bf16[128,2048]{1,0:T(8,128)(2,1)S(1)} %add_convert_fusion.4.refs_0_, ...), custom_call_target="tpu_custom_call", output_to_operand_aliasing={{1}: (2, {}), {2}: (4, {})} | custom-call | bytes 80000000 | tf_op jit(solution)/shard_map/pallas_call | solution.py:491
  413.5 6.7 multiply_convert_fusion.1
  420.3 4.5 fusion.148.refs_0_
  424.8 38.3 %shard_map.432 = f32[128,2048]{1,0:T(8,128)S(1)} custom-call(f32[8,128,2048]{2,1,0:T(8,128)S(1)} %fusion.148.refs_0_), custom_call_target="tpu_custom_call" | custom-call | bytes 80000000 | tf_op jit(solution)/shard_map/pallas_call | solution.py:491
  463.8 21.9 %shard_map.433 = bf16[8,128,2048]{2,1,0:T(8,128)(2,1)S(1)} custom-call(bf16[128,2048]{1,0:T(8,128)(2,1)S(1)} %add_convert_fusion.3.refs_0_), custom_call_target="tpu_custom_call" | custom-call | bytes 80000000 | tf_op jit(solution)/shard_map/pallas_call | solution.py:491
  485.8 4.8 fusion.147
  492.6 6.9 shard_map.434
  503.5 2.5 collective-permute-start
  508.3 2.4 fusion.8.left_ref
  512.9 2.9 collective-permute-start.1
  527.7 3.2 multiply_convert_fusion.refs_7_
  531.2 4.5 fusion.149.refs_0_
  537.0 40.2 %shard_map.435 = f32[128,2048]{1,0:T(8,128)S(1)} custom-call(f32[8,128,2048]{2,1,0:T(8,128)S(1)} %fusion.149.refs_0_), custom_call_target="tpu_custom_call" | custom-call | bytes 80000000 | tf_op jit(solution)/shard_map/pallas_call | solution.py:491
  578.8 21.2 %shard_map.436 = bf16[8,128,2048]{2,1,0:T(8,128)(2,1)S(1)} custom-call(bf16[128,2048]{1,0:T(8,128)(2,1)S(1)} %get-tuple-element.236.refs_0_), custom_call_target="tpu_custom_call" | custom-call | bytes 80000000 | tf_op jit(solution)/shard_map/pallas_call | solution.py:491
  600.0 7.0 fusion.6.refs_3_
  607.0 6.9 fusion.150.refs_0_
  613.9 46.4 %shard_map.437 = (f32[128,2048]{1,0:T(8,128)S(1)}, f32[2,256,2048]{2,1,0:T(8,128)S(1)}, bf16[1,2,256,2048]{3,2,1,0:T(8,128)(2,1)S(1)}, bf16[1,2,256,2048]{3,2,1,0:T(8,128)(2,1)S(1)}) custom-call(f32[8,128,2048]{2,1,0:T(8,128)} %fusion.150.refs_0_, bf16[1024,1024]{1,0:T(8,128)(2,1)S(1)} %get-tuple-element.279.refs_1_, bf16[1024,2048]{1,0:T(8,128)(2,1)S(1)} %bitcast.278), custom_call_target="tpu_custom_call" | custom-call | bytes 80000000 | tf_op jit(solution)/shard_map/pallas_call | solution.py:491
  667.0 34.0 %shard_map.438 = (bf16[8,128,2048]{2,1,0:T(8,128)(2,1)S(1)}, bf16[2,128,2048]{2,1,0:T(8,128)(2,1)S(1)}, f32[8,128,1024]{2,1,0:T(8,128)S(1)}, bf16[1,8,128,1024]{...) custom-call(bf16[128,2048]{1,0:T(8,128)(2,1)S(1)} %get-tuple-element.234.refs_0_, bf16[2,128,2048]{2,1,0:T(8,128)(2,1)S(1)} %bitcast.280, ...), custom_call_target="tpu_custom_call" | custom-call | bytes 80000000 | tf_op jit(solution)/shard_map/pallas_call | solution.py:491
  708.7 5.9 fusion.46.refs_0_
  716.6 3.7 fusion.152
  725.1 66.5 %shard_map.439 = (f32[128,2048]{1,0:T(8,128)S(1)}, bf16[2,128,2048]{2,1,0:T(8,128)(2,1)S(1)}, bf16[1,2,256,2048]{3,2,1,0:T(8,128)(2,1)S(1)}, bf16[4,128,1024]{2,...) custom-call(f32[8,128,2048]{2,1,0:T(8,128)} %fusion.46.refs_0_, ...), custom_call_target="tpu_custom_call", output_to_operand_aliasing={{1}: (2, {}), {2}: (4, {})} | custom-call | bytes 80000000 | tf_op jit(solution)/shard_map/pallas_call | solution.py:491
  799.9 35.5 %shard_map.440 = (bf16[8,128,2048]{2,1,0:T(8,128)(2,1)S(1)}, bf16[4,128,1024]{2,1,0:T(8,128)(2,1)S(1)}, bf16[1,8,128,1024]{3,2,1,0:T(8,128)(2,1)S(1)}, f32[8,128...) custom-call(bf16[128,2048]{1,0:T(8,128)(2,1)S(1)} %get-tuple-element, ...), custom_call_target="tpu_custom_call", output_to_operand_aliasing={{1}: (2, {}), {2}: (4, {})} | custom-call | bytes 80000000 | tf_op jit(solution)/shard_map/pallas_call | solution.py:491
  840.7 10.0 shard_map.441.refs_6_
  850.7 9.3 fusion.10
  862.6 67.6 %shard_map.442 = (f32[128,2048]{1,0:T(8,128)S(1)}, bf16[4,256,512]{2,1,0:T(8,128)(2,1)S(1)}, bf16[1,8,256,512]{3,2,1,0:T(8,128)(2,1)S(1)}, bf16[1,2,2,64,2048]{4...) custom-call(f32[8,128,2048]{2,1,0:T(8,128)} %bitcast.324, ...), custom_call_target="tpu_custom_call", output_to_operand_aliasing={{2}: (3, {})} | custom-call | bytes 80000000 | tf_op jit(solution)/shard_map/pallas_call | solution.py:491
  942.9 58.7 %shard_map.443 = (bf16[8,128,2048]{2,1,0:T(8,128)(2,1)S(1)}, bf16[1,8,128,768]{3,2,1,0:T(8,128)(2,1)S(1)}, bf16[1,8,128,256]{3,2,1,0:T(8,128)(2,1)S(1)}, bf16[4,...) custom-call(bf16[128,2048]{1,0:T(8,128)(2,1)S(1)} %select_convert_fusion.refs_0_, ...), custom_call_target="tpu_custom_call", output_to_operand_aliasing={{1}: (2, {}), {2}: (4, {})} | custom-call | bytes 80000000 | tf_op jit(solution)/shard_map/pallas_call | solution.py:491
  1006.8 11.0 shard_map.444
  1017.8 51.2 %shard_map.445 = (f32[24,2048]{1,0:T(8,128)}, bf16[1,2,256,2048]{3,2,1,0:T(8,128)(2,1)S(1)}, bf16[1,2,2,64,2048]{4,3,2,1,0:T(8,128)(2,1)S(1)}, bf16[4,128,256]{2...) custom-call(f32[8,24,2048]{2,1,0:T(8,128)S(1)} %bitcast.291, ...), custom_call_target="tpu_custom_call", output_to_operand_aliasing={{2}: (3, {})} | custom-call | bytes 80000000 | tf_op jit(solution)/shard_map/pallas_call | solution.py:491
  1077.7 51.2 %shard_map.446 = (f32[8,16,128]{2,1,0:T(8,128)}, bf16[1,2,256,2048]{3,2,1,0:T(8,128)(2,1)S(1)}, bf16[1,256,2048]{2,1,0:T(8,128)(2,1)S(1)}, f32[4,128,1024]{2,1,0:T(8,128)S(1)}) custom-call(f32[16,128]{1,0:T(8,128)S(1)} %broadcast_in_dim.194.refs_0_, bf16[1,2,256,2048]{3,2,1,0:T(8,128)(2,1)S(1)} %get-tuple-element.157.refs_1_, ...), custom_call_target="tpu_custom_call", output_to_operand_aliasing={{1}: (2, {})} | custom-call | bytes 80000000 | tf_op jit(solution)/shard_map/pallas_call | solution.py:491
  1129.0 2.6 multiply_reduce_fusion.4
  1135.3 2.7 multiply_reduce_fusion.1
  1140.9 4.1 multiply_reduce_fusion
  1150.0 14.8 %shard_map.447 = (f32[8,128]{1,0:T(8,128)}, f32[8,24,2048]{2,1,0:T(8,128)}) custom-call(f32[8,128]{1,0:T(8,128)} %broadcast_in_dim.217.tile_ref, f32[24,2048]{1,0:T(8,128)} %get-tuple-element.223.x_ref), custom_call_target="tpu_custom_call" | custom-call | tf_op jit(solution)/shard_map/pallas_call | solution.py:668
  1168.3 7.7 multiply_subtract_fusion.3
  1176.0 4.2 multiply_subtract_fusion.2
  1181.7 3.9 multiply_subtract_fusion.1
  1186.0 2.5 multiply_subtract_fusion.5
  1189.4 2.2 multiply_subtract_fusion.6
  1193.5 4.4 multiply_subtract_fusion.4
  1199.2 4.0 multiply_subtract_fusion
  (518 shorter events, 121.5 us)
Async XLA Ops:
  2.2 138.8 %copy-start.163 = (pred[128]{0:T(512)(128)(4,1)}, pred[128]{0:T(512)(128)(4,1)S(1)}, u32[]{:S(2)}) copy-start(pred[128]{0:T(512)(128)(4,1)S(1)} %compare_bitcast_fusion) | copy-start | bytes 388
  4.1 137.5 %copy-start.136 = (f32[1,2048]{1,0:T(1,128)}, f32[1,2048]{1,0:T(1,128)S(1)}, u32[]{:S(2)}) copy-start(f32[1,2048]{1,0:T(1,128)S(1)} %get-tuple-element.260) | copy-start | bytes 24580
  4.1 252.1 %copy-start.138 = (f32[1,2048]{1,0:T(1,128)}, f32[1,2048]{1,0:T(1,128)S(1)}, u32[]{:S(2)}) copy-start(f32[1,2048]{1,0:T(1,128)S(1)} %get-tuple-element.258) | copy-start | bytes 24580
  4.1 361.6 %copy-start.140 = (f32[1,2048]{1,0:T(1,128)}, f32[1,2048]{1,0:T(1,128)S(1)}, u32[]{:S(2)}) copy-start(f32[1,2048]{1,0:T(1,128)S(1)} %get-tuple-element.256) | copy-start | bytes 24580
  4.1 459.5 %copy-start.142 = (f32[1,2048]{1,0:T(1,128)}, f32[1,2048]{1,0:T(1,128)S(1)}, u32[]{:S(2)}) copy-start(f32[1,2048]{1,0:T(1,128)S(1)} %get-tuple-element.254) | copy-start | bytes 24580
  82.3 408.3 %copy-start.149 = (s32[1024]{0:T(1024)}, s32[1024]{0:T(1024)S(1)}, u32[]{:S(2)}) copy-start(s32[1024]{0:T(1024)S(1)} %fusion.102) | copy-start | bytes 12292
  89.4 51.6 %copy-start.96 = (f32[137,2048]{1,0:T(8,128)S(1)}, f32[137,2048]{1,0:T(8,128)}, u32[]{:S(2)}) copy-start(f32[137,2048]{1,0:T(8,128)} %param.34) | copy-start | bytes 3366916
  141.3 114.4 %copy-start.78 = (f32[128,2048]{1,0:T(8,128)}, f32[128,2048]{1,0:T(8,128)S(1)}, u32[]{:S(2)}) copy-start(f32[128,2048]{1,0:T(8,128)S(1)} %get-tuple-element.246) | copy-start | bytes 3145732
  141.3 44.0 %copy-start.155 = (f32[128]{0:T(128)}, f32[128]{0:T(128)S(1)}, u32[]{:S(2)}) copy-start(f32[128]{0:T(128)S(1)} %broadcast_multiply_fusion.11) | copy-start | bytes 1540
  141.6 43.8 %copy-start.165 = (f32[128]{0:T(128)}, f32[128]{0:T(128)S(1)}, u32[]{:S(2)}) copy-start(f32[128]{0:T(128)S(1)} %add_rsqrt_fusion.3) | copy-start | bytes 1540
  185.4 110.3 %copy-start.20 = (bf16[2,4,2,128,1024]{4,3,2,1,0:T(8,128)(2,1)}, bf16[2,4,2,128,1024]{4,3,2,1,0:T(8,128)(2,1)S(1)}, u32[]{:S(2)}) copy-start(bf16[2,4,2,128,1024]{4,3,2,1,0:T(8,128)(2,1)S(1)} %get-tuple-element.110) | copy-start | bytes 12582916
  255.8 109.3 %copy-start.80 = (f32[128,2048]{1,0:T(8,128)}, f32[128,2048]{1,0:T(8,128)S(1)}, u32[]{:S(2)}) copy-start(f32[128,2048]{1,0:T(8,128)S(1)} %get-tuple-element.244) | copy-start | bytes 3145732
  255.9 38.4 %copy-start.157 = (f32[128]{0:T(128)}, f32[128]{0:T(128)S(1)}, u32[]{:S(2)}) copy-start(f32[128]{0:T(128)S(1)} %broadcast_multiply_fusion.10) | copy-start | bytes 1540
  256.1 38.2 %copy-start.167 = (f32[128]{0:T(128)}, f32[128]{0:T(128)S(1)}, u32[]{:S(2)}) copy-start(f32[128]{0:T(128)S(1)} %add_rsqrt_fusion.2) | copy-start | bytes 1540
  256.4 37.9 %copy-start.51 = (bf16[8,32,4096]{2,1,0:T(8,128)(2,1)S(1)}, bf16[8,32,4096]{2,1,0:T(8,128)(2,1)}, u32[]{:S(2)}) copy-start(bf16[8,32,4096]{2,1,0:T(8,128)(2,1)} %get-tuple-element.119) | copy-start | bytes 6291460
  365.4 48.0 %copy-start.159 = (f32[128]{0:T(128)}, f32[128]{0:T(128)S(1)}, u32[]{:S(2)}) copy-start(f32[128]{0:T(128)S(1)} %broadcast_multiply_fusion.9) | copy-start | bytes 1540
  365.7 47.8 %copy-start.169 = (f32[128]{0:T(128)}, f32[128]{0:T(128)S(1)}, u32[]{:S(2)}) copy-start(f32[128]{0:T(128)S(1)} %add_rsqrt_fusion.1) | copy-start | bytes 1540
  463.3 22.5 %copy-start.82 = (f32[128,2048]{1,0:T(8,128)}, f32[128,2048]{1,0:T(8,128)S(1)}, u32[]{:S(2)}) copy-start(f32[128,2048]{1,0:T(8,128)S(1)} %get-tuple-element.240) | copy-start | bytes 3145732
  463.3 22.5 %copy-start.161 = (f32[128]{0:T(128)}, f32[128]{0:T(128)S(1)}, u32[]{:S(2)}) copy-start(f32[128]{0:T(128)S(1)} %broadcast_multiply_fusion.8) | copy-start | bytes 1540
  463.6 22.2 %copy-start.171 = (f32[128]{0:T(128)}, f32[128]{0:T(128)S(1)}, u32[]{:S(2)}) copy-start(f32[128]{0:T(128)S(1)} %add_rsqrt_fusion) | copy-start | bytes 1540
  463.8 21.9 %copy-start.183 = (bf16[2,2,4,64,2048]{4,3,2,1,0:T(8,128)(2,1)S(1)}, bf16[2,2,4,64,2048]{4,3,2,1,0:T(8,128)(2,1)}, u32[]{:S(2)}) copy-start(bf16[2,2,4,64,2048]{4,3,2,1,0:T(8,128)(2,1)} %get-tuple-element.102) | copy-start | bytes 12582916
  503.5 9.5 collective-permute-start
  512.9 12.9 %collective-permute-start.1 = (f32[8,128]{1,0:T(8,128)S(1)}, f32[8,128]{1,0:T(8,128)S(1)}, u32[]{:S(2)}, u32[]{:S(2)}) collective-permute-start(f32[8,128]{1,0:T(8,128)S(1)} %add.497), channel_id=1, source_target_pairs={{0,2},{2,0},{1,3},{3,1},{4,6},{6,4},{5,7},{7,5},{8,10},{10,8},{9,1... | collective-permute-start | bytes 12296 | tf_op jit(solution)/shard_map/ppermute | solution.py:711
  537.0 40.3 %copy-start.83 = (f32[128,2048]{1,0:T(8,128)S(1)}, f32[128,2048]{1,0:T(8,128)}, u32[]{:S(2)}) copy-start(f32[128,2048]{1,0:T(8,128)} %copy-done.82) | copy-start | bytes 3145732
  537.0 40.3 %copy-start.143 = (f32[1,2048]{1,0:T(1,128)S(1)}, f32[1,2048]{1,0:T(1,128)}, u32[]{:S(2)}) copy-start(f32[1,2048]{1,0:T(1,128)} %copy-done.142) | copy-start | bytes 24580
  537.0 40.3 %copy-start.162 = (f32[128]{0:T(128)S(1)}, f32[128]{0:T(128)}, u32[]{:S(2)}) copy-start(f32[128]{0:T(128)} %copy-done.161) | copy-start | bytes 1540
  537.0 40.3 %copy-start.172 = (f32[128]{0:T(128)S(1)}, f32[128]{0:T(128)}, u32[]{:S(2)}) copy-start(f32[128]{0:T(128)} %copy-done.171) | copy-start | bytes 1540
  578.3 21.7 %copy-start.185 = (f32[1024,1024]{1,0:T(8,128)S(1)}, f32[1024,1024]{1,0:T(8,128)}, u32[]{:S(2)}) copy-start(f32[1024,1024]{1,0:T(8,128)} %get-tuple-element.280) | copy-start | bytes 12582916
  578.8 21.2 %copy-start.39 = (bf16[2,2,4,64,2048]{4,3,2,1,0:T(8,128)(2,1)S(1)}, bf16[2,2,4,64,2048]{4,3,2,1,0:T(8,128)(2,1)}, u32[]{:S(2)}) copy-start(bf16[2,2,4,64,2048]{4,3,2,1,0:T(8,128)(2,1)} %copy-done.38) | copy-start | bytes 12582916
  613.9 47.7 %copy-start.141 = (f32[1,2048]{1,0:T(1,128)S(1)}, f32[1,2048]{1,0:T(1,128)}, u32[]{:S(2)}) copy-start(f32[1,2048]{1,0:T(1,128)} %copy-done.140) | copy-start | bytes 24580
  613.9 47.7 %copy-start.160 = (f32[128]{0:T(128)S(1)}, f32[128]{0:T(128)}, u32[]{:S(2)}) copy-start(f32[128]{0:T(128)} %copy-done.159) | copy-start | bytes 1540
  613.9 47.7 %copy-start.170 = (f32[128]{0:T(128)S(1)}, f32[128]{0:T(128)}, u32[]{:S(2)}) copy-start(f32[128]{0:T(128)} %copy-done.169) | copy-start | bytes 1540
  667.0 35.3 %copy-start.100 = (bf16[1,2,2,64,2048]{4,3,2,1,0:T(8,128)(2,1)S(1)}, bf16[1,2,2,64,2048]{4,3,2,1,0:T(8,128)(2,1)}, u32[]{:S(2)}) copy-start(bf16[1,2,2,64,2048]{4,3,2,1,0:T(8,128)(2,1)} %copy-done.99) | copy-start | bytes 3145732
  725.0 69.8 %copy-start.81 = (f32[128,2048]{1,0:T(8,128)S(1)}, f32[128,2048]{1,0:T(8,128)}, u32[]{:S(2)}) copy-start(f32[128,2048]{1,0:T(8,128)} %copy-done.80) | copy-start | bytes 3145732
  725.0 69.8 %copy-start.139 = (f32[1,2048]{1,0:T(1,128)S(1)}, f32[1,2048]{1,0:T(1,128)}, u32[]{:S(2)}) copy-start(f32[1,2048]{1,0:T(1,128)} %copy-done.138) | copy-start | bytes 24580
  725.0 69.8 %copy-start.158 = (f32[128]{0:T(128)S(1)}, f32[128]{0:T(128)}, u32[]{:S(2)}) copy-start(f32[128]{0:T(128)} %copy-done.157) | copy-start | bytes 1540
  725.0 69.8 %copy-start.168 = (f32[128]{0:T(128)S(1)}, f32[128]{0:T(128)}, u32[]{:S(2)}) copy-start(f32[128]{0:T(128)} %copy-done.167) | copy-start | bytes 1540
  725.0 70.3 %copy-start.102 = (f32[128,2048]{1,0:T(8,128)S(1)}, f32[128,2048]{1,0:T(8,128)}, u32[]{:S(2)}) copy-start(f32[128,2048]{1,0:T(8,128)} %get-tuple-element.235) | copy-start | bytes 3145732
  725.0 72.9 %copy-start.26 = (bf16[8,128,2048]{2,1,0:T(8,128)(2,1)S(1)}, bf16[8,128,2048]{2,1,0:T(8,128)(2,1)}, u32[]{:S(2)}) copy-start(bf16[8,128,2048]{2,1,0:T(8,128)(2,1)} %copy-done.25) | copy-start | bytes 12582916
  725.0 72.9 %copy-start.54 = (bf16[1,8,128,1024]{3,2,1,0:T(8,128)(2,1)S(1)}, bf16[1,8,128,1024]{3,2,1,0:T(8,128)(2,1)}, u32[]{:S(2)}) copy-start(bf16[1,8,128,1024]{3,2,1,0:T(8,128)(2,1)} %copy-done.53) | copy-start | bytes 6291460
  799.9 35.5 %copy-start.121 = (bf16[256,1024]{1,0:T(8,128)(2,1)S(1)}, bf16[256,1024]{1,0:T(8,128)(2,1)}, u32[]{:S(2)}) copy-start(bf16[256,1024]{1,0:T(8,128)(2,1)} %copy.87) | copy-start | bytes 1572868
  862.6 68.6 %copy-start.79 = (f32[128,2048]{1,0:T(8,128)S(1)}, f32[128,2048]{1,0:T(8,128)}, u32[]{:S(2)}) copy-start(f32[128,2048]{1,0:T(8,128)} %copy-done.78) | copy-start | bytes 3145732
  862.6 68.6 %copy-start.137 = (f32[1,2048]{1,0:T(1,128)S(1)}, f32[1,2048]{1,0:T(1,128)}, u32[]{:S(2)}) copy-start(f32[1,2048]{1,0:T(1,128)} %copy-done.136) | copy-start | bytes 24580
  862.6 68.6 %copy-start.156 = (f32[128]{0:T(128)S(1)}, f32[128]{0:T(128)}, u32[]{:S(2)}) copy-start(f32[128]{0:T(128)} %copy-done.155) | copy-start | bytes 1540
  862.6 68.6 %copy-start.166 = (f32[128]{0:T(128)S(1)}, f32[128]{0:T(128)}, u32[]{:S(2)}) copy-start(f32[128]{0:T(128)} %copy-done.165) | copy-start | bytes 1540
  942.9 63.9 %copy-start.60 = (bf16[1024,1024]{1,0:T(8,128)(2,1)S(1)}, bf16[1024,1024]{1,0:T(8,128)(2,1)}, u32[]{:S(2)}) copy-start(bf16[1024,1024]{1,0:T(8,128)(2,1)} %fusion.8.left_ref) | copy-start | bytes 6291460
  1070.2 68.5 %collective-permute-start.2 = (f32[24,2048]{1,0:T(8,128)}, f32[24,2048]{1,0:T(8,128)S(1)}, u32[]{:S(2)}, u32[]{:S(2)}) collective-permute-start(f32[24,2048]{1,0:T(8,128)} %get-tuple-element.176), channel_id=1, source_target_pairs={{0,16},{16,0},{1,17},{17,1},{2,18},{18,2},{3,19},{19,3},{4,20},{20... | collective-permute-start | bytes 589832 | tf_op jit(solution)/shard_map/ppermute | solution.py:711
  1139.7 7.2 collective-permute-start.3
  (142 other events, 499.4 us)

commit v4 on v3

--- a/solution.py
+++ b/solution.py
@@ -411,8 +411,8 @@
     return (EXCHANGE, width, (), pieces, None)
 
 
-def grad(left, right, rows, wire):
-    return (GRAD, rows, (0,), (left, right, wire), None)
+def grad(left, right, rows, wire, halves=(0,)):
+    return (GRAD, rows, halves, (left, right, wire), None)
 
 
 def product(left, right):
@@ -1085,7 +1085,7 @@
     preact_grad = gelu_pull(hidden_grad)[0].astype(BF16)
     part = nt(preact_grad, expand)
     back, contract_keep, contract_wire, contract_came = collect(
-        part, 11, grad(hidden, branch_three, block, BF16)
+        part, 11, grad(hidden, branch_three, block, BF16, (0, 1))
     )
 
     back, gain_four, gain_five = norm_back(back, norm_three, norm_rows[4])
@@ -1107,13 +1107,12 @@
     pair_grad = jnp.concatenate([key_grad, value_grad], 1)
     expand_half = other_half(expand_keep, expand_came, BF16)
     part = nt(cross_grad, w_cross)
-    back, contract_across, contract_came, expand_across, text_keep, text_wire, text_came = collect(
+    back, contract_across, expand_across, text_keep, text_wire, text_came = collect(
         part,
         13,
         swap(((1, 1),), contract_half, contract_across),
-        ring((1,), contract_wire, contract_came),
         swap(((0, 2),), expand_half),
-        grad(group_captions, pair_grad, text_rows, WIRE),
+        grad(group_captions, pair_grad, text_rows, F32),
         cut=4,
     )
 
@@ -1134,14 +1133,13 @@
     out_two = weight_grad(attn_two, branch_two, HD // extent, BF16)
     out_keep = jnp.stack([out_one[0], out_two[0]], 1)
     out_wire = jnp.stack([out_one[1], out_two[1]], 2)
-    text_half = other_half(text_keep, text_came, WIRE)
+    text_half = other_half(text_keep, text_came, F32)
     part = nt(triple_grad, w_qkv)
     out_wire = plain(out_wire)
-    back, text_across, text_came, out_came, triple_keep, triple_wire, triple_came = collect(
+    back, text_across, out_came, triple_keep, triple_wire, triple_came = collect(
         part,
         15,
-        swap(((0, 4),), text_half),
-        ring((1,), text_wire, text_came),
+        swap(((0, 2),), text_half),
         ring((0,), out_wire),
         grad(a_one, triple_grad, in_rows, WIRE),
         cut=4,
@@ -1154,9 +1152,11 @@
     cross_half = other_half(cross_keep, cross_came, WIRE)
     out_half = other_half(out_keep, out_came, BF16)
     expand_shard = own_half(expand_keep, expand_came, expand_across)
-    looked_grad, triple_came, cross_came, triple_across, expand_shard = spread(
+    looked_grad, text_across, text_came, triple_came, cross_came, triple_across, expand_shard = spread(
         looked_grad,
         16,
+        swap(((2, 2),), text_half, text_across),
+        ring((1,), text_wire, text_came),
         ring((1,), triple_wire, triple_came),
         ring((1,), cross_wire, cross_came),
         swap(((0, 4),), triple_half),

time: 1220 us -> 1240 us (1.016)
  Pallas kernels: 959 us -> 991 us
    pallas_call x19, Pallas kernels: 846 us -> 877 us  [group_call(): pl.pallas_call(partial(group_kernel, kind, cut, plan, extent, len(operand...]
    unnamed x373 -> x353, local copies, waits for them, and re-layouts: 45.4 us -> 38.2 us
  transfers between devices with their start and end apart: 4 -> 4, of which waited for: 1 -> 0; matrix products, arithmetic and copies ran while one was open for 3% -> 2% of each run, Pallas kernels for 4% -> 4%
where the time goes in v4:
time: 1240 us; the launch traced here: 1230 us
  Pallas kernels  991 us (80%)
  other arithmetic  79 us (6%)
  matrix products  78.8 us (6%)
  local copies, waits for them, and re-layouts  60.8 us (5%)
  between operations  12.6 us (1%)
    pallas_call x19, Pallas kernels, group_call(): pl.pallas_call(partial(group_kernel, kind, cut, plan, extent, len(operand...  877 us
    pallas_call x1, Pallas kernels, first_call(): pl.pallas_call(partial(first_kernel, extent), out_shape=tuple(out_shape),...  76.9 us
    dot_general x18, matrix products, dot(): return lax.dot_general(x, y, (dims, ((), ())), preferred_element_type=F32)  73.4 us
    unnamed x353, local copies, waits for them, and re-layouts  38.2 us
    sub x7, other arithmetic, adamw(): return (master - rate * (update + decay * master), first_new, second_new)  28.6 us
  transfers between devices with their start and end apart: 4, of which 0 were waited for; matrix products, arithmetic and copies ran while one was open for 2% of the time, Pallas kernels for 4%

profile of v4, /device:TPU:0, one launch (start us, length us, event | category | flops | bytes accessed | tf_op | source)
XLA Modules:
  0.0 1231.0 jit_solution(14100562020707687575)
XLA Ops:
  5.4 76.9 %shard_map.425 = (s32[8,16,128]{2,1,0:T(8,128)S(1)}, bf16[8,32,4096]{2,1,0:T(8,128)(2,1)}, bf16[4,128,1024]{2,1,0:T(8,128)(2,1)S(1)}, bf16[2,2,4,64,2048]{4,3,2,...) custom-call(s32[16,128]{1,0:T(8,128)S(1)} %pad_bitcast_fusion.refs_0, ...), custom_call_target="tpu_custom_call" | custom-call | tf_op jit(solution)/shard_map/pallas_call | solution.py:609
  82.3 7.1 fusion.9
  89.4 51.5 %shard_map.426 = (bf16[128,2048]{1,0:T(8,128)(2,1)S(1)}, bf16[2,4,2,128,1024]{4,3,2,1,0:T(8,128)(2,1)S(1)}, bf16[4,256,512]{2,1,0:T(8,128)(2,1)S(1)}) custom-call(bf16[8,128,2048]{2,1,0:T(8,128)(2,1)S(1)} %bitcast.298, bf16[4,128,1024]{2,1,0:T(8,128)(2,1)S(1)} %get-tuple-element.102.refs_1_, bf16[4,256,512]{2,1,0:T(8,128)(2,1)S(1)} %get-tuple-element.103.refs_2_), custom_call_target="tpu_custom_call" | custom-call | bytes 80000000 | tf_op jit(solution)/shard_map/pallas_call | solution.py:491
  141.8 43.5 %shard_map.427 = (bf16[8,128,2048]{2,1,0:T(8,128)(2,1)S(1)}, bf16[2,4,2,128,1024]{4,3,2,1,0:T(8,128)(2,1)S(1)}, bf16[2,4,2,256,512]{4,3,2,1,0:T(8,128)(2,1)S(1)}, bf16[4,128,1024]{2,1,0:T(8,128)(2,1)S(1)}) custom-call(bf16[128,2048]{1,0:T(8,128)(2,1)S(1)} %add_convert_fusion.5.refs_0_, ...), custom_call_target="tpu_custom_call", output_to_operand_aliasing={{1}: (2, {})} | custom-call | bytes 80000000 | tf_op jit(solution)/shard_map/pallas_call | solution.py:491
  185.4 3.4 fusion.24.q_ref.k_ref.v_ref
  193.2 62.4 %shard_map.428 = (f32[128,2048]{1,0:T(8,128)S(1)}, bf16[2,4,2,256,512]{4,3,2,1,0:T(8,128)(2,1)S(1)}, bf16[2,2,2,64,2048]{4,3,2,1,0:T(8,128)(2,1)S(1)}) custom-call(f32[8,128,2048]{2,1,0:T(8,128)S(1)} %fusion.117.refs_0_, bf16[4,256,512]{2,1,0:T(8,128)(2,1)S(1)} %get-tuple-element.106.refs_3_.refs_1_, ...), custom_call_target="tpu_custom_call", output_to_operand_aliasing={{1}: (2, {}), {2}: (4, {})} | custom-call | bytes 80000000 | tf_op jit(solution)/shard_map/pallas_call | solution.py:491
  256.3 37.9 %shard_map.429 = (bf16[8,128,2048]{2,1,0:T(8,128)(2,1)S(1)}, bf16[2,4,2,256,512]{4,3,2,1,0:T(8,128)(2,1)S(1)}, bf16[2,2,2,64,2048]{4,3,2,1,0:T(8,128)(2,1)S(1)}, bf16[2,4,2,128,1024]{4,3,2,1,0:T(8,128)(2,1)S(1)}) custom-call(bf16[128,2048]{1,0:T(8,128)(2,1)S(1)} %add_convert_fusion.4.refs_0_, ...), custom_call_target="tpu_custom_call", output_to_operand_aliasing={{1}: (2, {}), {2}: (4, {})} | custom-call | bytes 80000000 | tf_op jit(solution)/shard_map/pallas_call | solution.py:491
  301.5 63.7 %shard_map.430 = (f32[128,2048]{1,0:T(8,128)S(1)}, bf16[2,4,2,128,1024]{4,3,2,1,0:T(8,128)(2,1)S(1)}, bf16[2,2,4,64,2048]{4,3,2,1,0:T(8,128)(2,1)S(1)}) custom-call(f32[8,128,2048]{2,1,0:T(8,128)S(1)} %fusion.116.refs_0_, bf16[4,128,1024]{2,1,0:T(8,128)(2,1)S(1)} %get-tuple-element.116.refs_5_.refs_1_, ...), custom_call_target="tpu_custom_call", output_to_operand_aliasing={{1}: (2, {})} | custom-call | bytes 80000000 | tf_op jit(solution)/shard_map/pallas_call | solution.py:491
  366.0 47.5 %shard_map.431 = (bf16[8,128,2048]{2,1,0:T(8,128)(2,1)S(1)}, bf16[2,4,2,128,1024]{4,3,2,1,0:T(8,128)(2,1)S(1)}, bf16[2,2,4,64,2048]{4,3,2,1,0:T(8,128)(2,1)S(1)}) custom-call(bf16[128,2048]{1,0:T(8,128)(2,1)S(1)} %add_convert_fusion.3.refs_0_, ...), custom_call_target="tpu_custom_call", output_to_operand_aliasing={{1}: (2, {}), {2}: (4, {})} | custom-call | bytes 80000000 | tf_op jit(solution)/shard_map/pallas_call | solution.py:491
  413.5 6.8 multiply_convert_fusion.1
  420.3 4.5 fusion.147.refs_0_
  424.8 38.4 %shard_map.432 = f32[128,2048]{1,0:T(8,128)S(1)} custom-call(f32[8,128,2048]{2,1,0:T(8,128)S(1)} %fusion.147.refs_0_), custom_call_target="tpu_custom_call" | custom-call | bytes 80000000 | tf_op jit(solution)/shard_map/pallas_call | solution.py:491
  463.9 21.9 %shard_map.433 = bf16[8,128,2048]{2,1,0:T(8,128)(2,1)S(1)} custom-call(bf16[128,2048]{1,0:T(8,128)(2,1)S(1)} %add_convert_fusion.2.refs_0_), custom_call_target="tpu_custom_call" | custom-call | bytes 80000000 | tf_op jit(solution)/shard_map/pallas_call | solution.py:491
  485.9 4.8 fusion.146
  492.7 6.9 shard_map.434
  503.5 2.5 collective-permute-start
  508.5 2.4 fusion.8.left_ref
  513.1 2.9 collective-permute-start.1
  527.9 3.2 multiply_convert_fusion.refs_7_
  531.4 4.5 fusion.148.refs_0_
  537.2 40.4 %shard_map.435 = f32[128,2048]{1,0:T(8,128)S(1)} custom-call(f32[8,128,2048]{2,1,0:T(8,128)S(1)} %fusion.148.refs_0_), custom_call_target="tpu_custom_call" | custom-call | bytes 80000000 | tf_op jit(solution)/shard_map/pallas_call | solution.py:491
  579.2 21.2 %shard_map.436 = bf16[8,128,2048]{2,1,0:T(8,128)(2,1)S(1)} custom-call(bf16[128,2048]{1,0:T(8,128)(2,1)S(1)} %get-tuple-element.234.refs_0_), custom_call_target="tpu_custom_call" | custom-call | bytes 80000000 | tf_op jit(solution)/shard_map/pallas_call | solution.py:491
  600.4 7.0 fusion.6.refs_3_
  607.4 6.9 fusion.149.refs_0_
  614.2 58.7 %shard_map.437 = (f32[128,2048]{1,0:T(8,128)S(1)}, f32[2,256,2048]{2,1,0:T(8,128)S(1)}, bf16[1,2,256,2048]{3,2,1,0:T(8,128)(2,1)}, bf16[1,2,256,2048]{3,2,1,0:T(8,128)(2,1)S(1)}) custom-call(f32[8,128,2048]{2,1,0:T(8,128)} %fusion.149.refs_0_, bf16[1024,1024]{1,0:T(8,128)(2,1)S(1)} %get-tuple-element.277.refs_1_, bf16[1024,2048]{1,0:T(8,128)(2,1)S(1)} %bitcast.280), custom_call_target="tpu_custom_call" | custom-call | bytes 80000000 | tf_op jit(solution)/shard_map/pallas_call | solution.py:491
  677.6 33.4 %shard_map.438 = (bf16[8,128,2048]{2,1,0:T(8,128)(2,1)S(1)}, bf16[2,128,2048]{2,1,0:T(8,128)(2,1)S(1)}, f32[8,128,1024]{2,1,0:T(8,128)S(1)}, bf16[1,8,128,1024]{...) custom-call(bf16[128,2048]{1,0:T(8,128)(2,1)S(1)} %get-tuple-element.232.refs_0_, bf16[2,128,2048]{2,1,0:T(8,128)(2,1)S(1)} %bitcast.282, ...), custom_call_target="tpu_custom_call" | custom-call | bytes 80000000 | tf_op jit(solution)/shard_map/pallas_call | solution.py:491
  720.8 5.9 fusion.45.refs_0_
  728.7 3.6 fusion.151
  737.1 66.3 %shard_map.439 = (f32[128,2048]{1,0:T(8,128)S(1)}, bf16[2,128,2048]{2,1,0:T(8,128)(2,1)S(1)}, bf16[4,128,1024]{2,1,0:T(8,128)(2,1)S(1)}, f32[8,256,512]{2,1,0:T(...) custom-call(f32[8,128,2048]{2,1,0:T(8,128)} %fusion.45.refs_0_, ...), custom_call_target="tpu_custom_call", output_to_operand_aliasing={{1}: (2, {})} | custom-call | bytes 80000000 | tf_op jit(solution)/shard_map/pallas_call | solution.py:491
  810.2 37.5 %shard_map.440 = (bf16[8,128,2048]{2,1,0:T(8,128)(2,1)S(1)}, bf16[4,128,1024]{2,1,0:T(8,128)(2,1)S(1)}, bf16[1,8,128,1024]{3,2,1,0:T(8,128)(2,1)S(1)}, f32[8,128...) custom-call(bf16[128,2048]{1,0:T(8,128)(2,1)S(1)} %get-tuple-element, ...), custom_call_target="tpu_custom_call", output_to_operand_aliasing={{1}: (2, {}), {2}: (4, {})} | custom-call | bytes 80000000 | tf_op jit(solution)/shard_map/pallas_call | solution.py:491
  853.3 10.2 shard_map.441.refs_4_
  863.6 9.3 fusion.10
  875.7 66.2 %shard_map.442 = (f32[128,2048]{1,0:T(8,128)S(1)}, f32[4,256,512]{2,1,0:T(8,128)S(1)}, bf16[1,2,2,64,2048]{4,3,2,1,0:T(8,128)(2,1)S(1)}, f32[8,128,768]{2,1,0:T(...) custom-call(f32[8,128,2048]{2,1,0:T(8,128)} %bitcast.324, ...), custom_call_target="tpu_custom_call" | custom-call | bytes 80000000 | tf_op jit(solution)/shard_map/pallas_call | solution.py:491
  950.4 81.9 %shard_map.443 = (bf16[8,128,2048]{2,1,0:T(8,128)(2,1)S(1)}, f32[4,256,512]{2,1,0:T(8,128)S(1)}, f32[1,8,256,512]{3,2,1,0:T(8,128)S(1)}, bf16[1,8,128,768]{3,2,1...) custom-call(bf16[128,2048]{1,0:T(8,128)(2,1)S(1)} %select_convert_fu, ...), custom_call_target="tpu_custom_call", output_to_operand_aliasing={{1}: (2, {}), {2}: (4, {}), {3}: (6, {}), {4}: (8, {})} | custom-call | bytes 80000000 | tf_op jit(solution)/shard_map/pallas_call | solution.py:491
  1032.4 2.1 bitcast_add_fusion.3.refs_6_
  1037.4 10.7 shard_map.444
  1048.2 49.1 %shard_map.445 = (f32[24,2048]{1,0:T(8,128)}, bf16[1,2,256,2048]{3,2,1,0:T(8,128)(2,1)S(1)}, bf16[1,2,2,64,2048]{4,3,2,1,0:T(8,128)(2,1)S(1)}, bf16[4,128,256]{2...) custom-call(f32[8,24,2048]{2,1,0:T(8,128)S(1)} %bitcast.293, ...), custom_call_target="tpu_custom_call", output_to_operand_aliasing={{2}: (3, {})} | custom-call | bytes 80000000 | tf_op jit(solution)/shard_map/pallas_call | solution.py:491
  1107.0 48.8 %shard_map.446 = (f32[8,16,128]{2,1,0:T(8,128)}, bf16[1,2,256,2048]{3,2,1,0:T(8,128)(2,1)S(1)}, bf16[1,256,2048]{2,1,0:T(8,128)(2,1)S(1)}, f32[4,128,1024]{2,1,0:T(8,128)S(1)}) custom-call(f32[16,128]{1,0:T(8,128)S(1)} %broadcast_in_dim.194.refs_0_, bf16[1,2,256,2048]{3,2,1,0:T(8,128)(2,1)S(1)} %get-tuple-element.156.refs_1_, ...), custom_call_target="tpu_custom_call", output_to_operand_aliasing={{1}: (2, {})} | custom-call | bytes 80000000 | tf_op jit(solution)/shard_map/pallas_call | solution.py:491
  1155.8 2.6 multiply_reduce_fusion.4
  1165.9 4.5 multiply_reduce_fusion
  1174.3 16.5 %shard_map.447 = (f32[8,128]{1,0:T(8,128)}, f32[8,24,2048]{2,1,0:T(8,128)}) custom-call(f32[8,128]{1,0:T(8,128)} %broadcast_in_dim.217.tile_ref, f32[24,2048]{1,0:T(8,128)} %get-tuple-element.221.x_ref), custom_call_target="tpu_custom_call" | custom-call | tf_op jit(solution)/shard_map/pallas_call | solution.py:668
  1194.2 7.7 multiply_subtract_fusion.3
  1201.9 4.1 multiply_subtract_fusion.2
  1206.7 3.8 multiply_subtract_fusion.1
  1211.2 2.5 multiply_subtract_fusion.5
  1214.6 2.2 multiply_subtract_fusion.6
  1218.7 4.3 multiply_subtract_fusion.4
  1224.5 4.0 multiply_subtract_fusion
  (498 shorter events, 114.5 us)
Async XLA Ops:
  2.2 138.8 %copy-start.153 = (pred[128]{0:T(512)(128)(4,1)}, pred[128]{0:T(512)(128)(4,1)S(1)}, u32[]{:S(2)}) copy-start(pred[128]{0:T(512)(128)(4,1)S(1)} %compare_bitcast_fusion) | copy-start | bytes 388
  4.0 137.5 %copy-start.126 = (f32[1,2048]{1,0:T(1,128)}, f32[1,2048]{1,0:T(1,128)S(1)}, u32[]{:S(2)}) copy-start(f32[1,2048]{1,0:T(1,128)S(1)} %get-tuple-element.258) | copy-start | bytes 24580
  4.1 252.0 %copy-start.128 = (f32[1,2048]{1,0:T(1,128)}, f32[1,2048]{1,0:T(1,128)S(1)}, u32[]{:S(2)}) copy-start(f32[1,2048]{1,0:T(1,128)S(1)} %get-tuple-element.256) | copy-start | bytes 24580
  4.1 361.7 %copy-start.130 = (f32[1,2048]{1,0:T(1,128)}, f32[1,2048]{1,0:T(1,128)S(1)}, u32[]{:S(2)}) copy-start(f32[1,2048]{1,0:T(1,128)S(1)} %get-tuple-element.254) | copy-start | bytes 24580
  4.1 459.6 %copy-start.132 = (f32[1,2048]{1,0:T(1,128)}, f32[1,2048]{1,0:T(1,128)S(1)}, u32[]{:S(2)}) copy-start(f32[1,2048]{1,0:T(1,128)S(1)} %get-tuple-element.252) | copy-start | bytes 24580
  82.3 408.4 %copy-start.139 = (s32[1024]{0:T(1024)}, s32[1024]{0:T(1024)S(1)}, u32[]{:S(2)}) copy-start(s32[1024]{0:T(1024)S(1)} %fusion.101) | copy-start | bytes 12292
  89.4 51.6 %copy-start.86 = (f32[137,2048]{1,0:T(8,128)S(1)}, f32[137,2048]{1,0:T(8,128)}, u32[]{:S(2)}) copy-start(f32[137,2048]{1,0:T(8,128)} %param.34) | copy-start | bytes 3366916
  141.3 114.3 %copy-start.68 = (f32[128,2048]{1,0:T(8,128)}, f32[128,2048]{1,0:T(8,128)S(1)}, u32[]{:S(2)}) copy-start(f32[128,2048]{1,0:T(8,128)S(1)} %get-tuple-element.244) | copy-start | bytes 3145732
  141.3 44.0 %copy-start.145 = (f32[128]{0:T(128)}, f32[128]{0:T(128)S(1)}, u32[]{:S(2)}) copy-start(f32[128]{0:T(128)S(1)} %broadcast_multiply_fusion.11) | copy-start | bytes 1540
  141.6 43.8 %copy-start.155 = (f32[128]{0:T(128)}, f32[128]{0:T(128)S(1)}, u32[]{:S(2)}) copy-start(f32[128]{0:T(128)S(1)} %add_rsqrt_fusion.3) | copy-start | bytes 1540
  185.3 110.3 %copy-start.14 = (bf16[2,4,2,128,1024]{4,3,2,1,0:T(8,128)(2,1)}, bf16[2,4,2,128,1024]{4,3,2,1,0:T(8,128)(2,1)S(1)}, u32[]{:S(2)}) copy-start(bf16[2,4,2,128,1024]{4,3,2,1,0:T(8,128)(2,1)S(1)} %get-tuple-element.109) | copy-start | bytes 12582916
  255.8 109.4 %copy-start.70 = (f32[128,2048]{1,0:T(8,128)}, f32[128,2048]{1,0:T(8,128)S(1)}, u32[]{:S(2)}) copy-start(f32[128,2048]{1,0:T(8,128)S(1)} %get-tuple-element.242) | copy-start | bytes 3145732
  255.8 38.5 %copy-start.147 = (f32[128]{0:T(128)}, f32[128]{0:T(128)S(1)}, u32[]{:S(2)}) copy-start(f32[128]{0:T(128)S(1)} %broadcast_multiply_fusion.10) | copy-start | bytes 1540
  256.1 38.2 %copy-start.157 = (f32[128]{0:T(128)}, f32[128]{0:T(128)S(1)}, u32[]{:S(2)}) copy-start(f32[128]{0:T(128)S(1)} %add_rsqrt_fusion.2) | copy-start | bytes 1540
  256.3 38.0 %copy-start.58 = (bf16[8,32,4096]{2,1,0:T(8,128)(2,1)S(1)}, bf16[8,32,4096]{2,1,0:T(8,128)(2,1)}, u32[]{:S(2)}) copy-start(bf16[8,32,4096]{2,1,0:T(8,128)(2,1)} %get-tuple-element.118) | copy-start | bytes 6291460
  365.5 48.0 %copy-start.149 = (f32[128]{0:T(128)}, f32[128]{0:T(128)S(1)}, u32[]{:S(2)}) copy-start(f32[128]{0:T(128)S(1)} %broadcast_multiply_fusion.9) | copy-start | bytes 1540
  365.7 47.8 %copy-start.159 = (f32[128]{0:T(128)}, f32[128]{0:T(128)S(1)}, u32[]{:S(2)}) copy-start(f32[128]{0:T(128)S(1)} %add_rsqrt_fusion.1) | copy-start | bytes 1540
  463.4 22.5 %copy-start.72 = (f32[128,2048]{1,0:T(8,128)}, f32[128,2048]{1,0:T(8,128)S(1)}, u32[]{:S(2)}) copy-start(f32[128,2048]{1,0:T(8,128)S(1)} %get-tuple-element.238) | copy-start | bytes 3145732
  463.4 22.5 %copy-start.151 = (f32[128]{0:T(128)}, f32[128]{0:T(128)S(1)}, u32[]{:S(2)}) copy-start(f32[128]{0:T(128)S(1)} %broadcast_multiply_fusion.8) | copy-start | bytes 1540
  463.6 22.2 %copy-start.161 = (f32[128]{0:T(128)}, f32[128]{0:T(128)S(1)}, u32[]{:S(2)}) copy-start(f32[128]{0:T(128)S(1)} %add_rsqrt_fusion) | copy-start | bytes 1540
  503.5 9.6 collective-permute-start
  513.1 12.9 %collective-permute-start.1 = (f32[8,128]{1,0:T(8,128)S(1)}, f32[8,128]{1,0:T(8,128)S(1)}, u32[]{:S(2)}, u32[]{:S(2)}) collective-permute-start(f32[8,128]{1,0:T(8,128)S(1)} %add.497), channel_id=1, source_target_pairs={{0,2},{2,0},{1,3},{3,1},{4,6},{6,4},{5,7},{7,5},{8,10},{10,8},{9,1... | collective-permute-start | bytes 12296 | tf_op jit(solution)/shard_map/ppermute | solution.py:711
  537.2 40.5 %copy-start.73 = (f32[128,2048]{1,0:T(8,128)S(1)}, f32[128,2048]{1,0:T(8,128)}, u32[]{:S(2)}) copy-start(f32[128,2048]{1,0:T(8,128)} %copy-done.72) | copy-start | bytes 3145732
  537.2 40.5 %copy-start.133 = (f32[1,2048]{1,0:T(1,128)S(1)}, f32[1,2048]{1,0:T(1,128)}, u32[]{:S(2)}) copy-start(f32[1,2048]{1,0:T(1,128)} %copy-done.132) | copy-start | bytes 24580
  537.2 40.5 %copy-start.152 = (f32[128]{0:T(128)S(1)}, f32[128]{0:T(128)}, u32[]{:S(2)}) copy-start(f32[128]{0:T(128)} %copy-done.151) | copy-start | bytes 1540
  537.2 40.5 %copy-start.162 = (f32[128]{0:T(128)S(1)}, f32[128]{0:T(128)}, u32[]{:S(2)}) copy-start(f32[128]{0:T(128)} %copy-done.161) | copy-start | bytes 1540
  614.2 58.7 %copy-start.131 = (f32[1,2048]{1,0:T(1,128)S(1)}, f32[1,2048]{1,0:T(1,128)}, u32[]{:S(2)}) copy-start(f32[1,2048]{1,0:T(1,128)} %copy-done.130) | copy-start | bytes 24580
  614.2 58.7 %copy-start.150 = (f32[128]{0:T(128)S(1)}, f32[128]{0:T(128)}, u32[]{:S(2)}) copy-start(f32[128]{0:T(128)} %copy-done.149) | copy-start | bytes 1540
  614.2 58.7 %copy-start.160 = (f32[128]{0:T(128)S(1)}, f32[128]{0:T(128)}, u32[]{:S(2)}) copy-start(f32[128]{0:T(128)} %copy-done.159) | copy-start | bytes 1540
  672.9 38.1 %copy-start.30 = (f32[2,256,2048]{2,1,0:T(8,128)}, f32[2,256,2048]{2,1,0:T(8,128)S(1)}, u32[]{:S(2)}) copy-start(f32[2,256,2048]{2,1,0:T(8,128)S(1)} %get-tuple-element.131) | copy-start | bytes 12582916
  677.6 35.8 %copy-start.90 = (bf16[1,2,2,64,2048]{4,3,2,1,0:T(8,128)(2,1)S(1)}, bf16[1,2,2,64,2048]{4,3,2,1,0:T(8,128)(2,1)}, u32[]{:S(2)}) copy-start(bf16[1,2,2,64,2048]{4,3,2,1,0:T(8,128)(2,1)} %copy-done.89) | copy-start | bytes 3145732
  737.0 68.4 %copy-start.71 = (f32[128,2048]{1,0:T(8,128)S(1)}, f32[128,2048]{1,0:T(8,128)}, u32[]{:S(2)}) copy-start(f32[128,2048]{1,0:T(8,128)} %copy-done.70) | copy-start | bytes 3145732
  737.0 68.4 %copy-start.129 = (f32[1,2048]{1,0:T(1,128)S(1)}, f32[1,2048]{1,0:T(1,128)}, u32[]{:S(2)}) copy-start(f32[1,2048]{1,0:T(1,128)} %copy-done.128) | copy-start | bytes 24580
  737.0 68.4 %copy-start.148 = (f32[128]{0:T(128)S(1)}, f32[128]{0:T(128)}, u32[]{:S(2)}) copy-start(f32[128]{0:T(128)} %copy-done.147) | copy-start | bytes 1540
  737.0 68.4 %copy-start.158 = (f32[128]{0:T(128)S(1)}, f32[128]{0:T(128)}, u32[]{:S(2)}) copy-start(f32[128]{0:T(128)} %copy-done.157) | copy-start | bytes 1540
  737.0 68.8 %copy-start.92 = (f32[128,2048]{1,0:T(8,128)S(1)}, f32[128,2048]{1,0:T(8,128)}, u32[]{:S(2)}) copy-start(f32[128,2048]{1,0:T(8,128)} %get-tuple-element.233) | copy-start | bytes 3145732
  737.1 71.0 %copy-start.20 = (bf16[8,128,2048]{2,1,0:T(8,128)(2,1)S(1)}, bf16[8,128,2048]{2,1,0:T(8,128)(2,1)}, u32[]{:S(2)}) copy-start(bf16[8,128,2048]{2,1,0:T(8,128)(2,1)} %copy-done.19) | copy-start | bytes 12582916
  737.1 71.0 %copy-start.50 = (bf16[1,8,128,1024]{3,2,1,0:T(8,128)(2,1)S(1)}, bf16[1,8,128,1024]{3,2,1,0:T(8,128)(2,1)}, u32[]{:S(2)}) copy-start(bf16[1,8,128,1024]{3,2,1,0:T(8,128)(2,1)} %copy-done.49) | copy-start | bytes 6291460
  810.2 37.5 %copy-start.111 = (bf16[256,1024]{1,0:T(8,128)(2,1)S(1)}, bf16[256,1024]{1,0:T(8,128)(2,1)}, u32[]{:S(2)}) copy-start(bf16[256,1024]{1,0:T(8,128)(2,1)} %copy.87) | copy-start | bytes 1572868
  875.7 66.3 %copy-start.69 = (f32[128,2048]{1,0:T(8,128)S(1)}, f32[128,2048]{1,0:T(8,128)}, u32[]{:S(2)}) copy-start(f32[128,2048]{1,0:T(8,128)} %copy-done.68) | copy-start | bytes 3145732
  875.7 66.3 %copy-start.127 = (f32[1,2048]{1,0:T(1,128)S(1)}, f32[1,2048]{1,0:T(1,128)}, u32[]{:S(2)}) copy-start(f32[1,2048]{1,0:T(1,128)} %copy-done.126) | copy-start | bytes 24580
  875.7 66.3 %copy-start.146 = (f32[128]{0:T(128)S(1)}, f32[128]{0:T(128)}, u32[]{:S(2)}) copy-start(f32[128]{0:T(128)} %copy-done.145) | copy-start | bytes 1540
  875.7 66.3 %copy-start.156 = (f32[128]{0:T(128)S(1)}, f32[128]{0:T(128)}, u32[]{:S(2)}) copy-start(f32[128]{0:T(128)} %copy-done.155) | copy-start | bytes 1540
  942.0 93.8 %copy-start.28 = (bf16[1,2,2,64,2048]{4,3,2,1,0:T(8,128)(2,1)}, bf16[1,2,2,64,2048]{4,3,2,1,0:T(8,128)(2,1)S(1)}, u32[]{:S(2)}) copy-start(bf16[1,2,2,64,2048]{4,3,2,1,0:T(8,128)(2,1)S(1)} %get-tuple-element.157.refs_3_) | copy-start | bytes 3145732
  950.4 81.9 %copy-start.33 = (f32[8,256,512]{2,1,0:T(8,128)S(1)}, f32[8,256,512]{2,1,0:T(8,128)}, u32[]{:S(2)}) copy-start(f32[8,256,512]{2,1,0:T(8,128)} %copy-done.31) | copy-start | bytes 12582916
  1048.1 52.2 %copy-start.48 = (f32[8,128,768]{2,1,0:T(8,128)S(1)}, f32[8,128,768]{2,1,0:T(8,128)}, u32[]{:S(2)}) copy-start(f32[8,128,768]{2,1,0:T(8,128)} %copy-done.47) | copy-start | bytes 9437188
  1098.4 65.5 %collective-permute-start.2 = (f32[24,2048]{1,0:T(8,128)}, f32[24,2048]{1,0:T(8,128)S(1)}, u32[]{:S(2)}, u32[]{:S(2)}) collective-permute-start(f32[24,2048]{1,0:T(8,128)} %get-tuple-element.174), channel_id=1, source_target_pairs={{0,16},{16,0},{1,17},{17,1},{2,18},{18,2},{3,19},{19,3},{4,20},{20... | collective-permute-start | bytes 589832 | tf_op jit(solution)/shard_map/ppermute | solution.py:711
  1164.9 6.2 collective-permute-start.3
  (132 other events, 529.3 us)

commit v5 on v4

--- a/solution.py
+++ b/solution.py
@@ -1159,7 +1159,7 @@
         ring((1,), text_wire, text_came),
         ring((1,), triple_wire, triple_came),
         ring((1,), cross_wire, cross_came),
-        swap(((0, 4),), triple_half),
+        swap(((0, 2),), triple_half),
         exchange(plain(expand_shard), hidden_width),
         cut=4,
     )
@@ -1177,12 +1177,13 @@
     vector_grad = jnp.concatenate([position_grad, tail], 0)
 
     text_shard = own_half(text_keep, text_came, text_across)
-    vector_part, table_came, out_came, cross_across, out_across, text_shard = group_call(
+    vector_part, table_came, out_came, triple_across, cross_across, out_across, text_shard = group_call(
         SCATTER,
         vector_grad.reshape(8, padded // 8, width),
         17,
         ring((0,), table_wire),
         ring((1,), out_wire, out_came),
+        swap(((2, 2),), triple_half, triple_across),
         swap(((0, 4),), cross_half),
         swap(((0, out_half.shape[0]),), out_half),
         exchange(plain(text_shard), HD),

time: 1240 us -> 1240 us (level)
    unnamed x353 -> x359, local copies, waits for them, and re-layouts: 38.2 us -> 42.9 us
  transfers between devices with their start and end apart: 4 -> 4, of which waited for: 0 -> 1; matrix products, arithmetic and copies ran while one was open for 2% -> 2% of each run, Pallas kernels for 4% -> 4%
where the time goes in v5:
time: 1240 us
  Pallas kernels  992 us (80%)
  matrix products  78.7 us (6%)
  other arithmetic  77.8 us (6%)
  local copies, waits for them, and re-layouts  65.5 us (5%)
  between operations  12.6 us (1%)
    pallas_call x19, Pallas kernels, group_call(): pl.pallas_call(partial(group_kernel, kind, cut, plan, extent, len(operand...  880 us
    pallas_call x1, Pallas kernels, first_call(): pl.pallas_call(partial(first_kernel, extent), out_shape=tuple(out_shape),...  76.9 us
    dot_general x18, matrix products, dot(): return lax.dot_general(x, y, (dims, ((), ())), preferred_element_type=F32)  73.3 us
    unnamed x359, local copies, waits for them, and re-layouts  42.9 us
    sub x7, other arithmetic, adamw(): return (master - rate * (update + decay * master), first_new, second_new)  28.6 us
  transfers between devices with their start and end apart: 4, of which 1 were waited for; matrix products, arithmetic and copies ran while one was open for 2% of the time, Pallas kernels for 4%

profile of v5, /device:TPU:0, one launch (start us, length us, event | category | flops | bytes accessed | tf_op | source)
XLA Modules:
  0.0 1235.7 jit_solution(13750752032130785310)
XLA Ops:
  5.4 76.9 %shard_map.425 = (s32[8,16,128]{2,1,0:T(8,128)S(1)}, bf16[8,32,4096]{2,1,0:T(8,128)(2,1)}, bf16[4,128,1024]{2,1,0:T(8,128)(2,1)S(1)}, bf16[2,2,4,64,2048]{4,3,2,...) custom-call(s32[16,128]{1,0:T(8,128)S(1)} %pad_bitcast_fusion.refs_0, ...), custom_call_target="tpu_custom_call" | custom-call | tf_op jit(solution)/shard_map/pallas_call | solution.py:609
  82.3 7.1 fusion.9
  89.4 51.5 %shard_map.426 = (bf16[128,2048]{1,0:T(8,128)(2,1)S(1)}, bf16[2,4,2,128,1024]{4,3,2,1,0:T(8,128)(2,1)S(1)}, bf16[4,256,512]{2,1,0:T(8,128)(2,1)S(1)}) custom-call(bf16[8,128,2048]{2,1,0:T(8,128)(2,1)S(1)} %bitcast.298, bf16[4,128,1024]{2,1,0:T(8,128)(2,1)S(1)} %get-tuple-element.103.refs_1_, bf16[4,256,512]{2,1,0:T(8,128)(2,1)S(1)} %get-tuple-element.104.refs_2_), custom_call_target="tpu_custom_call" | custom-call | bytes 80000000 | tf_op jit(solution)/shard_map/pallas_call | solution.py:491
  141.8 43.5 %shard_map.427 = (bf16[8,128,2048]{2,1,0:T(8,128)(2,1)S(1)}, bf16[2,4,2,128,1024]{4,3,2,1,0:T(8,128)(2,1)S(1)}, bf16[2,4,2,256,512]{4,3,2,1,0:T(8,128)(2,1)S(1)}, bf16[4,128,1024]{2,1,0:T(8,128)(2,1)S(1)}) custom-call(bf16[128,2048]{1,0:T(8,128)(2,1)S(1)} %add_convert_fusion.5.refs_0_, ...), custom_call_target="tpu_custom_call", output_to_operand_aliasing={{1}: (2, {})} | custom-call | bytes 80000000 | tf_op jit(solution)/shard_map/pallas_call | solution.py:491
  185.4 3.4 fusion.24.q_ref.k_ref.v_ref
  193.2 62.4 %shard_map.428 = (f32[128,2048]{1,0:T(8,128)S(1)}, bf16[2,4,2,256,512]{4,3,2,1,0:T(8,128)(2,1)S(1)}, bf16[2,2,2,64,2048]{4,3,2,1,0:T(8,128)(2,1)S(1)}) custom-call(f32[8,128,2048]{2,1,0:T(8,128)S(1)} %fusion.117.refs_0_, bf16[4,256,512]{2,1,0:T(8,128)(2,1)S(1)} %get-tuple-element.107.refs_3_.refs_1_, ...), custom_call_target="tpu_custom_call", output_to_operand_aliasing={{1}: (2, {}), {2}: (4, {})} | custom-call | bytes 80000000 | tf_op jit(solution)/shard_map/pallas_call | solution.py:491
  256.3 37.9 %shard_map.429 = (bf16[8,128,2048]{2,1,0:T(8,128)(2,1)S(1)}, bf16[2,4,2,256,512]{4,3,2,1,0:T(8,128)(2,1)S(1)}, bf16[2,2,2,64,2048]{4,3,2,1,0:T(8,128)(2,1)S(1)}, bf16[2,4,2,128,1024]{4,3,2,1,0:T(8,128)(2,1)S(1)}) custom-call(bf16[128,2048]{1,0:T(8,128)(2,1)S(1)} %add_convert_fusion.4.refs_0_, ...), custom_call_target="tpu_custom_call", output_to_operand_aliasing={{1}: (2, {}), {2}: (4, {})} | custom-call | bytes 80000000 | tf_op jit(solution)/shard_map/pallas_call | solution.py:491
  301.5 63.6 %shard_map.430 = (f32[128,2048]{1,0:T(8,128)S(1)}, bf16[2,4,2,128,1024]{4,3,2,1,0:T(8,128)(2,1)S(1)}, bf16[2,2,4,64,2048]{4,3,2,1,0:T(8,128)(2,1)S(1)}) custom-call(f32[8,128,2048]{2,1,0:T(8,128)S(1)} %fusion.116.refs_0_, bf16[4,128,1024]{2,1,0:T(8,128)(2,1)S(1)} %get-tuple-element.117.refs_5_.refs_1_, ...), custom_call_target="tpu_custom_call", output_to_operand_aliasing={{1}: (2, {})} | custom-call | bytes 80000000 | tf_op jit(solution)/shard_map/pallas_call | solution.py:491
  366.0 47.5 %shard_map.431 = (bf16[8,128,2048]{2,1,0:T(8,128)(2,1)S(1)}, bf16[2,4,2,128,1024]{4,3,2,1,0:T(8,128)(2,1)S(1)}, bf16[2,2,4,64,2048]{4,3,2,1,0:T(8,128)(2,1)S(1)}) custom-call(bf16[128,2048]{1,0:T(8,128)(2,1)S(1)} %add_convert_fusion.3.refs_0_, ...), custom_call_target="tpu_custom_call", output_to_operand_aliasing={{1}: (2, {}), {2}: (4, {})} | custom-call | bytes 80000000 | tf_op jit(solution)/shard_map/pallas_call | solution.py:491
  413.5 6.8 multiply_convert_fusion.1
  420.3 4.5 fusion.147.refs_0_
  424.8 38.4 %shard_map.432 = f32[128,2048]{1,0:T(8,128)S(1)} custom-call(f32[8,128,2048]{2,1,0:T(8,128)S(1)} %fusion.147.refs_0_), custom_call_target="tpu_custom_call" | custom-call | bytes 80000000 | tf_op jit(solution)/shard_map/pallas_call | solution.py:491
  464.0 21.9 %shard_map.433 = bf16[8,128,2048]{2,1,0:T(8,128)(2,1)S(1)} custom-call(bf16[128,2048]{1,0:T(8,128)(2,1)S(1)} %add_convert_fusion.2.refs_0_), custom_call_target="tpu_custom_call" | custom-call | bytes 80000000 | tf_op jit(solution)/shard_map/pallas_call | solution.py:491
  485.9 4.8 fusion.146
  492.7 6.9 shard_map.434
  503.6 2.5 collective-permute-start
  508.5 2.4 fusion.8.left_ref
  513.2 2.9 collective-permute-start.1
  528.0 3.2 multiply_convert_fusion.refs_7_
  531.5 4.5 fusion.148.refs_0_
  537.3 40.4 %shard_map.435 = f32[128,2048]{1,0:T(8,128)S(1)} custom-call(f32[8,128,2048]{2,1,0:T(8,128)S(1)} %fusion.148.refs_0_), custom_call_target="tpu_custom_call" | custom-call | bytes 80000000 | tf_op jit(solution)/shard_map/pallas_call | solution.py:491
  579.3 21.2 %shard_map.436 = bf16[8,128,2048]{2,1,0:T(8,128)(2,1)S(1)} custom-call(bf16[128,2048]{1,0:T(8,128)(2,1)S(1)} %get-tuple-element.236.refs_0_), custom_call_target="tpu_custom_call" | custom-call | bytes 80000000 | tf_op jit(solution)/shard_map/pallas_call | solution.py:491
  600.5 7.0 fusion.6.refs_3_
  607.5 6.7 fusion.149.refs_0_
  614.2 58.7 %shard_map.437 = (f32[128,2048]{1,0:T(8,128)S(1)}, f32[2,256,2048]{2,1,0:T(8,128)S(1)}, bf16[1,2,256,2048]{3,2,1,0:T(8,128)(2,1)}, bf16[1,2,256,2048]{3,2,1,0:T(8,128)(2,1)S(1)}) custom-call(f32[8,128,2048]{2,1,0:T(8,128)} %fusion.149.refs_0_, bf16[1024,1024]{1,0:T(8,128)(2,1)S(1)} %get-tuple-element.279.refs_1_, bf16[1024,2048]{1,0:T(8,128)(2,1)S(1)} %bitcast.280), custom_call_target="tpu_custom_call" | custom-call | bytes 80000000 | tf_op jit(solution)/shard_map/pallas_call | solution.py:491
  677.6 33.5 %shard_map.438 = (bf16[8,128,2048]{2,1,0:T(8,128)(2,1)S(1)}, bf16[2,128,2048]{2,1,0:T(8,128)(2,1)S(1)}, f32[8,128,1024]{2,1,0:T(8,128)S(1)}, bf16[1,8,128,1024]{...) custom-call(bf16[128,2048]{1,0:T(8,128)(2,1)S(1)} %get-tuple-element.234.refs_0_, bf16[2,128,2048]{2,1,0:T(8,128)(2,1)S(1)} %bitcast.282, ...), custom_call_target="tpu_custom_call" | custom-call | bytes 80000000 | tf_op jit(solution)/shard_map/pallas_call | solution.py:491
  720.8 5.9 fusion.45.refs_0_
  728.7 3.6 fusion.151
  737.1 66.3 %shard_map.439 = (f32[128,2048]{1,0:T(8,128)S(1)}, bf16[2,128,2048]{2,1,0:T(8,128)(2,1)S(1)}, bf16[4,128,1024]{2,1,0:T(8,128)(2,1)S(1)}, f32[8,256,512]{2,1,0:T(...) custom-call(f32[8,128,2048]{2,1,0:T(8,128)} %fusion.45.refs_0_, ...), custom_call_target="tpu_custom_call", output_to_operand_aliasing={{1}: (2, {})} | custom-call | bytes 80000000 | tf_op jit(solution)/shard_map/pallas_call | solution.py:491
  810.1 37.5 %shard_map.440 = (bf16[8,128,2048]{2,1,0:T(8,128)(2,1)S(1)}, bf16[4,128,1024]{2,1,0:T(8,128)(2,1)S(1)}, bf16[1,8,128,1024]{3,2,1,0:T(8,128)(2,1)S(1)}, f32[8,128...) custom-call(bf16[128,2048]{1,0:T(8,128)(2,1)S(1)} %get-tuple-element, ...), custom_call_target="tpu_custom_call", output_to_operand_aliasing={{1}: (2, {}), {2}: (4, {})} | custom-call | bytes 80000000 | tf_op jit(solution)/shard_map/pallas_call | solution.py:491
  851.2 2.1 convolution_convert_fusion.g_ref
  853.3 10.2 shard_map.441.refs_4_
  863.6 9.3 fusion.10
  875.7 66.2 %shard_map.442 = (f32[128,2048]{1,0:T(8,128)S(1)}, f32[4,256,512]{2,1,0:T(8,128)S(1)}, bf16[1,2,2,64,2048]{4,3,2,1,0:T(8,128)(2,1)S(1)}, f32[8,128,768]{2,1,0:T(...) custom-call(f32[8,128,2048]{2,1,0:T(8,128)} %bitcast.324, ...), custom_call_target="tpu_custom_call" | custom-call | bytes 80000000 | tf_op jit(solution)/shard_map/pallas_call | solution.py:491
  949.8 71.4 %shard_map.443 = (bf16[8,128,2048]{2,1,0:T(8,128)(2,1)S(1)}, f32[4,256,512]{2,1,0:T(8,128)S(1)}, f32[1,8,256,512]{3,2,1,0:T(8,128)S(1)}, bf16[1,8,128,768]{3,2,1...) custom-call(bf16[128,2048]{1,0:T(8,128)(2,1)S(1)} %select_convert_fu, ...), custom_call_target="tpu_custom_call", output_to_operand_aliasing={{1}: (2, {}), {2}: (4, {}), {3}: (6, {}), {4}: (8, {})} | custom-call | bytes 80000000 | tf_op jit(solution)/shard_map/pallas_call | solution.py:491
  1027.0 10.6 shard_map.444
  1040.2 60.0 %shard_map.445 = (f32[24,2048]{1,0:T(8,128)}, bf16[1,2,256,2048]{3,2,1,0:T(8,128)(2,1)S(1)}, bf16[1,2,2,64,2048]{4,3,2,1,0:T(8,128)(2,1)S(1)}, bf16[4,128,768]{2...) custom-call(f32[8,24,2048]{2,1,0:T(8,128)S(1)} %bitcast.293, ...), custom_call_target="tpu_custom_call", output_to_operand_aliasing={{2}: (3, {}), {3}: (5, {})} | custom-call | bytes 80000000 | tf_op jit(solution)/shard_map/pallas_call | solution.py:491
  1110.4 51.0 %shard_map.446 = (f32[8,16,128]{2,1,0:T(8,128)}, bf16[1,2,256,2048]{3,2,1,0:T(8,128)(2,1)S(1)}, bf16[1,256,2048]{2,1,0:T(8,128)(2,1)S(1)}, f32[4,128,1024]{2,1,0:T(8,128)S(1)}) custom-call(f32[16,128]{1,0:T(8,128)S(1)} %broadcast_in_dim.194.refs_0_, bf16[1,2,256,2048]{3,2,1,0:T(8,128)(2,1)S(1)} %get-tuple-element.157.refs_1_, ...), custom_call_target="tpu_custom_call", output_to_operand_aliasing={{1}: (2, {})} | custom-call | bytes 80000000 | tf_op jit(solution)/shard_map/pallas_call | solution.py:491
  1161.4 2.6 multiply_reduce_fusion.4
  1171.7 4.5 multiply_reduce_fusion
  1180.9 14.6 %shard_map.447 = (f32[8,128]{1,0:T(8,128)}, f32[8,24,2048]{2,1,0:T(8,128)}) custom-call(f32[8,128]{1,0:T(8,128)} %broadcast_in_dim.217.tile_ref, f32[24,2048]{1,0:T(8,128)} %get-tuple-element.223.x_ref), custom_call_target="tpu_custom_call" | custom-call | tf_op jit(solution)/shard_map/pallas_call | solution.py:668
  1198.9 7.7 multiply_subtract_fusion.3
  1206.7 4.1 multiply_subtract_fusion.2
  1211.5 3.8 multiply_subtract_fusion.1
  1215.9 2.5 multiply_subtract_fusion.5
  1219.3 2.2 multiply_subtract_fusion.6
  1223.5 4.3 multiply_subtract_fusion.4
  1229.2 4.0 multiply_subtract_fusion
  (504 shorter events, 118.7 us)
Async XLA Ops:
  2.2 138.8 %copy-start.156 = (pred[128]{0:T(512)(128)(4,1)}, pred[128]{0:T(512)(128)(4,1)S(1)}, u32[]{:S(2)}) copy-start(pred[128]{0:T(512)(128)(4,1)S(1)} %compare_bitcast_fusion) | copy-start | bytes 388
  4.0 137.5 %copy-start.129 = (f32[1,2048]{1,0:T(1,128)}, f32[1,2048]{1,0:T(1,128)S(1)}, u32[]{:S(2)}) copy-start(f32[1,2048]{1,0:T(1,128)S(1)} %get-tuple-element.260) | copy-start | bytes 24580
  4.1 252.0 %copy-start.131 = (f32[1,2048]{1,0:T(1,128)}, f32[1,2048]{1,0:T(1,128)S(1)}, u32[]{:S(2)}) copy-start(f32[1,2048]{1,0:T(1,128)S(1)} %get-tuple-element.258) | copy-start | bytes 24580
  4.1 361.7 %copy-start.133 = (f32[1,2048]{1,0:T(1,128)}, f32[1,2048]{1,0:T(1,128)S(1)}, u32[]{:S(2)}) copy-start(f32[1,2048]{1,0:T(1,128)S(1)} %get-tuple-element.256) | copy-start | bytes 24580
  4.1 459.6 %copy-start.135 = (f32[1,2048]{1,0:T(1,128)}, f32[1,2048]{1,0:T(1,128)S(1)}, u32[]{:S(2)}) copy-start(f32[1,2048]{1,0:T(1,128)S(1)} %get-tuple-element.254) | copy-start | bytes 24580
  82.3 408.4 %copy-start.142 = (s32[1024]{0:T(1024)}, s32[1024]{0:T(1024)S(1)}, u32[]{:S(2)}) copy-start(s32[1024]{0:T(1024)S(1)} %fusion.101) | copy-start | bytes 12292
  89.4 51.6 %copy-start.89 = (f32[137,2048]{1,0:T(8,128)S(1)}, f32[137,2048]{1,0:T(8,128)}, u32[]{:S(2)}) copy-start(f32[137,2048]{1,0:T(8,128)} %param.34) | copy-start | bytes 3366916
  141.3 114.3 %copy-start.71 = (f32[128,2048]{1,0:T(8,128)}, f32[128,2048]{1,0:T(8,128)S(1)}, u32[]{:S(2)}) copy-start(f32[128,2048]{1,0:T(8,128)S(1)} %get-tuple-element.246) | copy-start | bytes 3145732
  141.3 44.0 %copy-start.148 = (f32[128]{0:T(128)}, f32[128]{0:T(128)S(1)}, u32[]{:S(2)}) copy-start(f32[128]{0:T(128)S(1)} %broadcast_multiply_fusion.11) | copy-start | bytes 1540
  141.6 43.8 %copy-start.158 = (f32[128]{0:T(128)}, f32[128]{0:T(128)S(1)}, u32[]{:S(2)}) copy-start(f32[128]{0:T(128)S(1)} %add_rsqrt_fusion.3) | copy-start | bytes 1540
  185.3 110.3 %copy-start.15 = (bf16[2,4,2,128,1024]{4,3,2,1,0:T(8,128)(2,1)}, bf16[2,4,2,128,1024]{4,3,2,1,0:T(8,128)(2,1)S(1)}, u32[]{:S(2)}) copy-start(bf16[2,4,2,128,1024]{4,3,2,1,0:T(8,128)(2,1)S(1)} %get-tuple-element.110) | copy-start | bytes 12582916
  255.8 109.4 %copy-start.73 = (f32[128,2048]{1,0:T(8,128)}, f32[128,2048]{1,0:T(8,128)S(1)}, u32[]{:S(2)}) copy-start(f32[128,2048]{1,0:T(8,128)S(1)} %get-tuple-element.244) | copy-start | bytes 3145732
  255.8 38.5 %copy-start.150 = (f32[128]{0:T(128)}, f32[128]{0:T(128)S(1)}, u32[]{:S(2)}) copy-start(f32[128]{0:T(128)S(1)} %broadcast_multiply_fusion.10) | copy-start | bytes 1540
  256.1 38.2 %copy-start.160 = (f32[128]{0:T(128)}, f32[128]{0:T(128)S(1)}, u32[]{:S(2)}) copy-start(f32[128]{0:T(128)S(1)} %add_rsqrt_fusion.2) | copy-start | bytes 1540
  256.3 38.0 %copy-start.63 = (bf16[8,32,4096]{2,1,0:T(8,128)(2,1)S(1)}, bf16[8,32,4096]{2,1,0:T(8,128)(2,1)}, u32[]{:S(2)}) copy-start(bf16[8,32,4096]{2,1,0:T(8,128)(2,1)} %get-tuple-element.119) | copy-start | bytes 6291460
  365.4 48.0 %copy-start.152 = (f32[128]{0:T(128)}, f32[128]{0:T(128)S(1)}, u32[]{:S(2)}) copy-start(f32[128]{0:T(128)S(1)} %broadcast_multiply_fusion.9) | copy-start | bytes 1540
  365.7 47.8 %copy-start.162 = (f32[128]{0:T(128)}, f32[128]{0:T(128)S(1)}, u32[]{:S(2)}) copy-start(f32[128]{0:T(128)S(1)} %add_rsqrt_fusion.1) | copy-start | bytes 1540
  463.4 22.5 %copy-start.75 = (f32[128,2048]{1,0:T(8,128)}, f32[128,2048]{1,0:T(8,128)S(1)}, u32[]{:S(2)}) copy-start(f32[128,2048]{1,0:T(8,128)S(1)} %get-tuple-element.240) | copy-start | bytes 3145732
  463.4 22.5 %copy-start.154 = (f32[128]{0:T(128)}, f32[128]{0:T(128)S(1)}, u32[]{:S(2)}) copy-start(f32[128]{0:T(128)S(1)} %broadcast_multiply_fusion.8) | copy-start | bytes 1540
  463.7 22.2 %copy-start.164 = (f32[128]{0:T(128)}, f32[128]{0:T(128)S(1)}, u32[]{:S(2)}) copy-start(f32[128]{0:T(128)S(1)} %add_rsqrt_fusion) | copy-start | bytes 1540
  503.6 9.6 collective-permute-start
  513.2 13.0 %collective-permute-start.1 = (f32[8,128]{1,0:T(8,128)S(1)}, f32[8,128]{1,0:T(8,128)S(1)}, u32[]{:S(2)}, u32[]{:S(2)}) collective-permute-start(f32[8,128]{1,0:T(8,128)S(1)} %add.497), channel_id=1, source_target_pairs={{0,2},{2,0},{1,3},{3,1},{4,6},{6,4},{5,7},{7,5},{8,10},{10,8},{9,1... | collective-permute-start | bytes 12296 | tf_op jit(solution)/shard_map/ppermute | solution.py:711
  537.3 40.5 %copy-start.76 = (f32[128,2048]{1,0:T(8,128)S(1)}, f32[128,2048]{1,0:T(8,128)}, u32[]{:S(2)}) copy-start(f32[128,2048]{1,0:T(8,128)} %copy-done.75) | copy-start | bytes 3145732
  537.3 40.5 %copy-start.136 = (f32[1,2048]{1,0:T(1,128)S(1)}, f32[1,2048]{1,0:T(1,128)}, u32[]{:S(2)}) copy-start(f32[1,2048]{1,0:T(1,128)} %copy-done.135) | copy-start | bytes 24580
  537.3 40.5 %copy-start.155 = (f32[128]{0:T(128)S(1)}, f32[128]{0:T(128)}, u32[]{:S(2)}) copy-start(f32[128]{0:T(128)} %copy-done.154) | copy-start | bytes 1540
  537.3 40.5 %copy-start.165 = (f32[128]{0:T(128)S(1)}, f32[128]{0:T(128)}, u32[]{:S(2)}) copy-start(f32[128]{0:T(128)} %copy-done.164) | copy-start | bytes 1540
  614.2 58.7 %copy-start.134 = (f32[1,2048]{1,0:T(1,128)S(1)}, f32[1,2048]{1,0:T(1,128)}, u32[]{:S(2)}) copy-start(f32[1,2048]{1,0:T(1,128)} %copy-done.133) | copy-start | bytes 24580
  614.2 58.7 %copy-start.153 = (f32[128]{0:T(128)S(1)}, f32[128]{0:T(128)}, u32[]{:S(2)}) copy-start(f32[128]{0:T(128)} %copy-done.152) | copy-start | bytes 1540
  614.2 58.7 %copy-start.163 = (f32[128]{0:T(128)S(1)}, f32[128]{0:T(128)}, u32[]{:S(2)}) copy-start(f32[128]{0:T(128)} %copy-done.162) | copy-start | bytes 1540
  672.9 38.1 %copy-start.31 = (f32[2,256,2048]{2,1,0:T(8,128)}, f32[2,256,2048]{2,1,0:T(8,128)S(1)}, u32[]{:S(2)}) copy-start(f32[2,256,2048]{2,1,0:T(8,128)S(1)} %get-tuple-element.132) | copy-start | bytes 12582916
  677.6 35.8 %copy-start.93 = (bf16[1,2,2,64,2048]{4,3,2,1,0:T(8,128)(2,1)S(1)}, bf16[1,2,2,64,2048]{4,3,2,1,0:T(8,128)(2,1)}, u32[]{:S(2)}) copy-start(bf16[1,2,2,64,2048]{4,3,2,1,0:T(8,128)(2,1)} %copy-done.92) | copy-start | bytes 3145732
  737.0 68.4 %copy-start.74 = (f32[128,2048]{1,0:T(8,128)S(1)}, f32[128,2048]{1,0:T(8,128)}, u32[]{:S(2)}) copy-start(f32[128,2048]{1,0:T(8,128)} %copy-done.73) | copy-start | bytes 3145732
  737.0 68.4 %copy-start.132 = (f32[1,2048]{1,0:T(1,128)S(1)}, f32[1,2048]{1,0:T(1,128)}, u32[]{:S(2)}) copy-start(f32[1,2048]{1,0:T(1,128)} %copy-done.131) | copy-start | bytes 24580
  737.0 68.4 %copy-start.151 = (f32[128]{0:T(128)S(1)}, f32[128]{0:T(128)}, u32[]{:S(2)}) copy-start(f32[128]{0:T(128)} %copy-done.150) | copy-start | bytes 1540
  737.0 68.4 %copy-start.161 = (f32[128]{0:T(128)S(1)}, f32[128]{0:T(128)}, u32[]{:S(2)}) copy-start(f32[128]{0:T(128)} %copy-done.160) | copy-start | bytes 1540
  737.0 68.8 %copy-start.95 = (f32[128,2048]{1,0:T(8,128)S(1)}, f32[128,2048]{1,0:T(8,128)}, u32[]{:S(2)}) copy-start(f32[128,2048]{1,0:T(8,128)} %get-tuple-element.235) | copy-start | bytes 3145732
  737.0 71.0 %copy-start.21 = (bf16[8,128,2048]{2,1,0:T(8,128)(2,1)S(1)}, bf16[8,128,2048]{2,1,0:T(8,128)(2,1)}, u32[]{:S(2)}) copy-start(bf16[8,128,2048]{2,1,0:T(8,128)(2,1)} %copy-done.20) | copy-start | bytes 12582916
  737.0 71.0 %copy-start.55 = (bf16[1,8,128,1024]{3,2,1,0:T(8,128)(2,1)S(1)}, bf16[1,8,128,1024]{3,2,1,0:T(8,128)(2,1)}, u32[]{:S(2)}) copy-start(bf16[1,8,128,1024]{3,2,1,0:T(8,128)(2,1)} %copy-done.54) | copy-start | bytes 6291460
  810.1 37.6 %copy-start.114 = (bf16[256,1024]{1,0:T(8,128)(2,1)S(1)}, bf16[256,1024]{1,0:T(8,128)(2,1)}, u32[]{:S(2)}) copy-start(bf16[256,1024]{1,0:T(8,128)(2,1)} %copy.88) | copy-start | bytes 1572868
  875.7 66.3 %copy-start.72 = (f32[128,2048]{1,0:T(8,128)S(1)}, f32[128,2048]{1,0:T(8,128)}, u32[]{:S(2)}) copy-start(f32[128,2048]{1,0:T(8,128)} %copy-done.71) | copy-start | bytes 3145732
  875.7 66.3 %copy-start.130 = (f32[1,2048]{1,0:T(1,128)S(1)}, f32[1,2048]{1,0:T(1,128)}, u32[]{:S(2)}) copy-start(f32[1,2048]{1,0:T(1,128)} %copy-done.129) | copy-start | bytes 24580
  875.7 66.3 %copy-start.149 = (f32[128]{0:T(128)S(1)}, f32[128]{0:T(128)}, u32[]{:S(2)}) copy-start(f32[128]{0:T(128)} %copy-done.148) | copy-start | bytes 1540
  875.7 66.3 %copy-start.159 = (f32[128]{0:T(128)S(1)}, f32[128]{0:T(128)}, u32[]{:S(2)}) copy-start(f32[128]{0:T(128)} %copy-done.158) | copy-start | bytes 1540
  949.8 72.3 %copy-start.34 = (f32[8,256,512]{2,1,0:T(8,128)S(1)}, f32[8,256,512]{2,1,0:T(8,128)}, u32[]{:S(2)}) copy-start(f32[8,256,512]{2,1,0:T(8,128)} %copy-done.32) | copy-start | bytes 12582916
  1040.2 63.5 %copy-start.80 = (f32[2,1,64,2048]{3,2,1,0:T(8,128)S(1)}, f32[2,1,64,2048]{3,2,1,0:T(8,128)}, u32[]{:S(2)}) copy-start(f32[2,1,64,2048]{3,2,1,0:T(8,128)} %constant_dynamic-slice_fusion.1) | copy-start | bytes 3145732
  1040.2 63.5 %copy-start.82 = (f32[2,1,64,2048]{3,2,1,0:T(8,128)S(1)}, f32[2,1,64,2048]{3,2,1,0:T(8,128)}, u32[]{:S(2)}) copy-start(f32[2,1,64,2048]{3,2,1,0:T(8,128)} %constant_dynamic-slice_fusion.2) | copy-start | bytes 3145732
  1102.2 67.3 %collective-permute-start.2 = (f32[24,2048]{1,0:T(8,128)}, f32[24,2048]{1,0:T(8,128)S(1)}, u32[]{:S(2)}, u32[]{:S(2)}) collective-permute-start(f32[24,2048]{1,0:T(8,128)} %get-tuple-element.176), channel_id=1, source_target_pairs={{0,16},{16,0},{1,17},{17,1},{2,18},{18,2},{3,19},{19,3},{4,20},{20... | collective-permute-start | bytes 589832 | tf_op jit(solution)/shard_map/ppermute | solution.py:711
  1170.5 7.2 collective-permute-start.3
  (135 other events, 515.4 us)
